TPU v7x, 32 devices: a whole 2x2x4 slice. The times are simulated.
32 devices in a mesh: dp: 16 (over z, y, core), tensor: 2 (over x).
Axes of the slice: x: 2, y: 2, z: 4, core: 2. Of those that a mesh axis runs over, the one named last changes fastest.
Arguments:
- tokens: bfloat16 [8192, 1024], P(('dp', 'tensor')), may hold values from -6 to 6
- cotangent: bfloat16 [8192, 1024], P(('dp', 'tensor')), may hold values from -6 to 6
- lengths: int32 [16], replicated, may hold values from 128 to 512, as said below
- bucket_table: int32 [1023], replicated, may hold values from 0 to 31, as said below
- routes: int32 [8192, 2], P('dp'), may hold values from 0 to 15, all different within a row
- gate_values: bfloat16 [8192, 2], P('dp'), may hold values from 0.19921875 to 1
- qkv_weight: bfloat16 [3, 1024, 1024], P(None, 'dp', 'tensor'), may hold values from -0.1875 to 0.1875
- out_weight: bfloat16 [1024, 1024], P('dp', 'tensor'), may hold values from -2 to 2
- norm_gains: bfloat16 [2, 1024], P(None, 'dp'), may hold values from 0.5 to 1.5
- rel_bias: bfloat16 [16, 32], P('tensor'), may hold values from -3 to 3
- gate_weight: bfloat16 [16, 1024, 2816], P(None, 'dp', 'tensor'), may hold values from -0.1875 to 0.1875
- up_weight: bfloat16 [16, 1024, 2816], P(None, 'dp', 'tensor'), may hold values from -0.1875 to 0.1875
- down_weight: bfloat16 [16, 1024, 2816], P(None, 'dp', 'tensor'), may hold values from -0.109375 to 0.109375
Outputs:
- mixed: bfloat16 [8192, 1024], P(('dp', 'tensor'))
- input_grad: float32 [8192, 1024], P(('dp', 'tensor'))
- qkv_grad: float32 [3, 1024, 1024], P(None, 'dp', 'tensor')
- out_grad: float32 [1024, 1024], P('dp', 'tensor')
- gains_grad: float32 [2, 1024], P(None, 'dp')
- bias_grad: float32 [16, 32], P('tensor')
- gate_grad: float32 [16, 1024, 2816], P(None, 'dp', 'tensor')
- up_grad: float32 [16, 1024, 2816], P(None, 'dp', 'tensor')
- down_grad: float32 [16, 1024, 2816], P(None, 'dp', 'tensor')
Inputs may be any that keep to these rules, and one draw needn't show every extreme that they name: `lengths`: one sequence is 512 long and another a quarter of 512. `bucket_table`: entry r + 511 is the bucket of a key r positions after its query (before it for negative r); it depends only on the sign of r and on |r|, and never falls as |r| grows on either side. `routes`: each token names two different experts.
All inputs are finite; a program needn't handle non-finite values.
Results may differ from a plain program's by a relative error of at most 0.018.
Values may be sent and summed in bfloat16 or wider, within the bound.
No kernel may reach another device: no remote copies, remote signals or barrier semaphores. Data moves between devices by JAX's collectives and lax.ppermute only.
A program may use at most 192 MiB of HBM per device.

v0:
```python
import jax
import jax.numpy as jnp
from jax import lax
from jax.sharding import PartitionSpec as P

HEAD_DIM = 64


EPSILON = 1e-06
MASKED_SCORE = -1e30
HIGHEST = lax.Precision.HIGHEST
SCORE_SCALE = 0.125


def rms_norm(activations, gain_row):
    row_scale = lax.rsqrt(jnp.mean(activations * activations, axis=-1, keepdims=True) + EPSILON)
    return activations * row_scale * gain_row


def geglu(gate_pre, up_pre):
    return jax.nn.gelu(gate_pre, approximate=True) * up_pre


def contract_rows(left_side, right_side):
    return lax.dot_general(
        left_side, right_side, (((0,), (0,)), ((), ())), preferred_element_type=jnp.float32
    )


def contract_cols(left_side, right_side):
    return lax.dot_general(
        left_side, right_side, (((1,), (1,)), ((), ())), preferred_element_type=jnp.float32
    )


def toeplitz(segment, row_count, col_count):
    period = row_count + col_count
    wrapped = jnp.concatenate(
        [segment[row_count - 1 :], jnp.zeros((1,), segment.dtype), segment[: row_count - 1]]
    )
    repeated = jnp.broadcast_to(wrapped[None, :], (row_count, period)).reshape(-1)
    return repeated[: row_count * (period - 1)].reshape(row_count, period - 1)[:, :col_count]


def diagonal_sums(block_values, row_count, col_count):
    period = row_count + col_count
    padded = jnp.concatenate(
        [block_values, jnp.zeros((row_count, row_count - 1), block_values.dtype)], axis=1
    )
    flattened = jnp.concatenate([padded.reshape(-1), jnp.zeros((row_count,), block_values.dtype)])
    wrapped = jnp.sum(flattened.reshape(row_count, period), axis=0)
    return jnp.concatenate([wrapped[period - row_count + 1 :], wrapped[:col_count]])


def bucket_hot(bucket_table, bucket_count):
    return (bucket_table[:, None] == jnp.arange(bucket_count, dtype=jnp.int32)[None, :]).astype(
        jnp.float32
    )


def block_scores(query_block, key_head, bias_head, hot_rows, key_valid):
    bias_values = jnp.dot(hot_rows, bias_head, precision=HIGHEST)
    scores = contract_cols(query_block, key_head) * SCORE_SCALE + toeplitz(
        bias_values, query_block.shape[0], key_head.shape[0]
    )
    return jnp.where(key_valid[None, :], scores, MASKED_SCORE)


def join_heads(per_head):
    return jnp.transpose(per_head, (1, 0, 2)).reshape(
        per_head.shape[1], per_head.shape[0] * per_head.shape[2]
    )


def attend_forward(queries, keys_seq, values_seq, bias_rows, bucket_table, key_valid, block_rows):
    head_count = bias_rows.shape[0]
    bucket_count = bias_rows.shape[1]
    row_count = queries.shape[0]

    def one_head(head_index):
        query_head = lax.dynamic_slice_in_dim(queries, head_index * HEAD_DIM, HEAD_DIM, 1)
        key_head = lax.dynamic_slice_in_dim(keys_seq, head_index * HEAD_DIM, HEAD_DIM, 1)
        value_head = lax.dynamic_slice_in_dim(values_seq, head_index * HEAD_DIM, HEAD_DIM, 1)
        bias_head = bias_rows[head_index]

        def one_block(block_index):
            hot_rows = bucket_hot(bucket_table, bucket_count)
            scores = block_scores(query_head, key_head, bias_head, hot_rows, key_valid)
            row_max = jnp.max(scores, axis=1, keepdims=True)
            exponent = jnp.exp(scores - row_max)
            row_total = jnp.sum(exponent, axis=1, keepdims=True)
            softmax_rows = (exponent / row_total).astype(jnp.bfloat16)
            attended = jnp.dot(softmax_rows, value_head, preferred_element_type=jnp.float32).astype(
                jnp.bfloat16
            )
            return (attended, (row_max + jnp.log(row_total))[:, 0])

        attended, log_total = lax.map(one_block, jnp.arange(row_count // block_rows))
        return (attended.reshape(row_count, HEAD_DIM), log_total.reshape(row_count))

    attended, log_total = lax.map(one_head, jnp.arange(head_count))
    return (join_heads(attended), log_total)


def attend_backward(
    queries,
    keys_seq,
    values_seq,
    attended_grad,
    log_total,
    bias_rows,
    bucket_table,
    key_valid,
    block_rows,
):
    head_count = bias_rows.shape[0]
    bucket_count = bias_rows.shape[1]
    row_count = queries.shape[0]
    seq_len = keys_seq.shape[0]

    def one_head(head_index):
        query_head = lax.dynamic_slice_in_dim(queries, head_index * HEAD_DIM, HEAD_DIM, 1)
        key_head = lax.dynamic_slice_in_dim(keys_seq, head_index * HEAD_DIM, HEAD_DIM, 1)
        value_head = lax.dynamic_slice_in_dim(values_seq, head_index * HEAD_DIM, HEAD_DIM, 1)
        grad_head = lax.dynamic_slice_in_dim(attended_grad, head_index * HEAD_DIM, HEAD_DIM, 1)
        bias_head = bias_rows[head_index]
        total_head = log_total[head_index]

        def one_block(running, block_index):
            key_acc, value_acc, bias_acc = running
            hot_rows = bucket_hot(bucket_table, bucket_count)
            scores = block_scores(query_head, key_head, bias_head, hot_rows, key_valid)
            softmax_rows = jnp.exp(scores - total_head[:, None])
            probs_grad = contract_cols(grad_head, value_head)
            score_grad = (
                softmax_rows
                * (probs_grad - jnp.sum(softmax_rows * probs_grad, axis=1, keepdims=True))
            ).astype(jnp.bfloat16)
            query_grad = (
                jnp.dot(score_grad, key_head, preferred_element_type=jnp.float32) * SCORE_SCALE
            )
            key_acc = key_acc + contract_rows(score_grad, query_head) * SCORE_SCALE
            value_acc = value_acc + contract_rows(softmax_rows.astype(jnp.bfloat16), grad_head)
            bias_acc = bias_acc + jnp.dot(
                diagonal_sums(score_grad.astype(jnp.float32), block_rows, seq_len),
                hot_rows,
                precision=HIGHEST,
            )
            return ((key_acc, value_acc, bias_acc), query_grad)

        start_values = (
            jnp.zeros((seq_len, HEAD_DIM), jnp.float32),
            jnp.zeros((seq_len, HEAD_DIM), jnp.float32),
            jnp.zeros((bucket_count,), jnp.float32),
        )
        (key_grad, value_grad, bias_grad), query_grad = lax.scan(
            one_block, start_values, jnp.arange(row_count // block_rows)
        )
        return (query_grad.reshape(row_count, HEAD_DIM), key_grad, value_grad, bias_grad)

    query_grad, key_grad, value_grad, bias_grad = lax.map(one_head, jnp.arange(head_count))
    return (join_heads(query_grad), join_heads(key_grad), join_heads(value_grad), bias_grad)


def on_device(
    tokens,
    cotangent,
    lengths,
    bucket_table,
    routes,
    gate_values,
    qkv_weight,
    out_weight,
    norm_gains,
    rel_bias,
    gate_weight,
    up_weight,
    down_weight,
):
    tok_rows = tokens.shape[0]
    model_width = tokens.shape[1]
    tensor_count = lax.axis_size("tensor")
    dp_count = lax.axis_size("dp")
    group_rows = tok_rows * tensor_count
    expert_count = gate_weight.shape[0]
    shard_rows = gate_weight.shape[1]
    capacity = 9 * group_rows // 64
    group_size = dp_count // expert_count
    slot_count = (capacity + group_size - 1) // group_size
    total_slots = dp_count * slot_count
    block_rows = min(512, group_rows)
    head_count = rel_bias.shape[0]
    dp_index = lax.axis_index("dp")
    tensor_index = lax.axis_index("tensor")
    length = lengths[dp_index]
    group_valid = jnp.arange(group_rows, dtype=jnp.int32) < length
    own_valid = lax.dynamic_slice_in_dim(group_valid, tensor_index * tok_rows, tok_rows, 0).astype(
        jnp.float32
    )[:, None]
    bias_rows = rel_bias.astype(jnp.float32)

    def gather_rows(row_block):
        return lax.all_gather(row_block, "tensor", axis=0, tiled=True)

    def sum_rows(row_block):
        return lax.psum_scatter(
            row_block.astype(jnp.bfloat16), "tensor", scatter_dimension=0, tiled=True
        ).astype(jnp.float32)

    def route_out(slot_rows):
        arrived = lax.all_to_all(
            slot_rows.reshape(dp_count, slot_count, model_width),
            "dp",
            split_axis=0,
            concat_axis=0,
            tiled=True,
        )
        return arrived.reshape(total_slots, model_width)

    def route_back(slot_rows):
        arrived = lax.all_to_all(
            slot_rows.reshape(dp_count, slot_count, model_width).astype(jnp.bfloat16),
            "dp",
            split_axis=0,
            concat_axis=0,
            tiled=True,
        ).astype(jnp.float32)
        return arrived.reshape(total_slots, model_width)

    def fetch_layer():
        return (
            lax.all_gather(qkv_weight, "dp", axis=1, tiled=True),
            lax.all_gather(out_weight[None], "dp", axis=1, tiled=True),
            lax.all_gather(norm_gains, "dp", axis=1, tiled=True),
        )

    def home_order(weight):
        return jnp.repeat(weight, group_size, axis=0)

    def fetch_experts():
        arrived = (
            lax.all_to_all(home_order(gate_weight), "dp", split_axis=0, concat_axis=1, tiled=True),
            lax.all_to_all(home_order(up_weight), "dp", split_axis=0, concat_axis=1, tiled=True),
            lax.all_to_all(home_order(down_weight), "dp", split_axis=0, concat_axis=1, tiled=True),
        )
        return (arrived[0][0], arrived[1][0], arrived[2][0])

    def regroup(arrived):
        shaped = arrived.reshape(dp_count, shard_rows, arrived.shape[1])
        return jnp.sum(
            shaped.reshape(expert_count, group_size, shard_rows, arrived.shape[1]), axis=1
        )

    pair_expert = routes.reshape(-1)
    pair_valid = jnp.repeat(group_valid, 2)
    chosen = (
        (pair_expert[:, None] == jnp.arange(expert_count, dtype=jnp.int32)[None, :])
        & pair_valid[:, None]
    ).astype(jnp.int32)
    earlier = jnp.cumsum(chosen, axis=0) - chosen
    position = jnp.sum(earlier * chosen, axis=1)
    kept_pair = pair_valid & (position < capacity)
    member = position // slot_count
    device = pair_expert * group_size + member
    pair_slot = jnp.where(kept_pair, device * slot_count + position % slot_count, total_slots)
    slot_token = (
        jnp.full((total_slots,), group_rows, jnp.int32)
        .at[pair_slot]
        .set(jnp.arange(2 * group_rows, dtype=jnp.int32) // 2, mode="drop")
    )
    slot_gate = (
        jnp.zeros((total_slots,), jnp.float32)
        .at[pair_slot]
        .set(gate_values.reshape(-1).astype(jnp.float32), mode="drop")
    )
    gate_float = gate_values.astype(jnp.float32)
    qkv_all, out_stack, gains_all = fetch_layer()
    out_all = out_stack[0]
    gate_all, up_all, down_all = fetch_experts()
    inputs = tokens.astype(jnp.float32)
    gain_one = gains_all[0].astype(jnp.float32)
    gain_two = gains_all[1].astype(jnp.float32)
    norm_one_all = gather_rows(rms_norm(inputs, gain_one).astype(jnp.bfloat16))
    queries = jnp.dot(norm_one_all, qkv_all[0], preferred_element_type=jnp.float32).astype(
        jnp.bfloat16
    )
    keys_seq = jnp.dot(norm_one_all, qkv_all[1], preferred_element_type=jnp.float32).astype(
        jnp.bfloat16
    )
    values_seq = jnp.dot(norm_one_all, qkv_all[2], preferred_element_type=jnp.float32).astype(
        jnp.bfloat16
    )
    attended, log_total = attend_forward(
        queries, keys_seq, values_seq, bias_rows, bucket_table, group_valid, block_rows
    )
    branch = sum_rows(contract_cols(attended, out_all))
    residual_mid = inputs + own_valid * branch
    norm_two_all = gather_rows(rms_norm(residual_mid, gain_two).astype(jnp.bfloat16))
    expert_in = route_out(jnp.take(norm_two_all, slot_token, axis=0, mode="fill", fill_value=0))
    gate_pre = jnp.dot(expert_in, gate_all, preferred_element_type=jnp.float32)
    up_pre = jnp.dot(expert_in, up_all, preferred_element_type=jnp.float32)
    hidden, geglu_pull = jax.vjp(geglu, gate_pre, up_pre)
    hidden = hidden.astype(jnp.bfloat16)
    returned = route_back(contract_cols(hidden, down_all))
    pair_out = jnp.take(returned, pair_slot, axis=0, mode="fill", fill_value=0.0).reshape(
        group_rows, 2, model_width
    )
    expert_mix = sum_rows(jnp.sum(pair_out * gate_float[:, :, None], axis=1))
    mixed = (residual_mid + own_valid * expert_mix).astype(jnp.bfloat16)
    qkv_all, out_stack, gains_all = fetch_layer()
    out_all = out_stack[0]
    gate_all, up_all, down_all = fetch_experts()
    upstream = own_valid * cotangent.astype(jnp.float32)
    mix_grad_all = gather_rows(upstream.astype(jnp.bfloat16))
    slot_grad = (
        jnp.take(mix_grad_all, slot_token, axis=0, mode="fill", fill_value=0).astype(jnp.float32)
        * slot_gate[:, None]
    ).astype(jnp.bfloat16)
    out_slot_grad = route_out(slot_grad)
    hidden_grad = jnp.dot(out_slot_grad, down_all, preferred_element_type=jnp.float32)
    down_part = contract_rows(out_slot_grad, hidden)
    gate_pre_grad, up_pre_grad = geglu_pull(hidden_grad)
    gate_pre_grad = gate_pre_grad.astype(jnp.bfloat16)
    up_pre_grad = up_pre_grad.astype(jnp.bfloat16)
    gate_part = contract_rows(expert_in, gate_pre_grad)
    up_part = contract_rows(expert_in, up_pre_grad)
    slot_back = route_back(
        contract_cols(gate_pre_grad, gate_all) + contract_cols(up_pre_grad, up_all)
    )
    pair_back = jnp.take(slot_back, pair_slot, axis=0, mode="fill", fill_value=0.0).reshape(
        group_rows, 2, model_width
    )
    norm_two_grad = sum_rows(jnp.sum(pair_back, axis=1))
    norm_two_out, norm_two_pull = jax.vjp(rms_norm, residual_mid, gain_two)
    mid_norm_grad, gain_two_grad = norm_two_pull(norm_two_grad)
    mid_grad = upstream + mid_norm_grad
    branch_grad_all = gather_rows((own_valid * mid_grad).astype(jnp.bfloat16))
    attended_grad = jnp.dot(branch_grad_all, out_all, preferred_element_type=jnp.float32).astype(
        jnp.bfloat16
    )
    out_part = contract_rows(branch_grad_all, attended)
    query_grad, key_grad, value_grad, bias_grad = attend_backward(
        queries,
        keys_seq,
        values_seq,
        attended_grad,
        log_total,
        bias_rows,
        bucket_table,
        group_valid,
        block_rows,
    )
    key_own_grad = key_grad.astype(jnp.bfloat16)
    value_own_grad = value_grad.astype(jnp.bfloat16)
    query_grad = query_grad.astype(jnp.bfloat16)
    norm_one_grad = sum_rows(
        contract_cols(query_grad, qkv_all[0])
        + contract_cols(key_own_grad, qkv_all[1])
        + contract_cols(value_own_grad, qkv_all[2])
    )
    qkv_part = jnp.stack(
        [
            contract_rows(norm_one_all, query_grad),
            contract_rows(norm_one_all, key_own_grad),
            contract_rows(norm_one_all, value_own_grad),
        ]
    )
    norm_one_out, norm_one_pull = jax.vjp(rms_norm, inputs, gain_one)
    inputs_norm_grad, gain_one_grad = norm_one_pull(norm_one_grad)
    input_grad = mid_grad + inputs_norm_grad
    qkv_grad, out_grad = (
        lax.psum_scatter(qkv_part, "dp", scatter_dimension=1, tiled=True),
        lax.psum_scatter(out_part[None], "dp", scatter_dimension=1, tiled=True),
    )
    gate_back, up_back, down_back = (
        lax.all_to_all(
            gate_part.astype(jnp.bfloat16), "dp", split_axis=0, concat_axis=0, tiled=True
        ).astype(gate_part.dtype),
        lax.all_to_all(
            up_part.astype(jnp.bfloat16), "dp", split_axis=0, concat_axis=0, tiled=True
        ).astype(up_part.dtype),
        lax.all_to_all(
            down_part.astype(jnp.bfloat16), "dp", split_axis=0, concat_axis=0, tiled=True
        ).astype(down_part.dtype),
    )
    bias_full = lax.dynamic_update_slice_in_dim(
        jnp.zeros((head_count * tensor_count, bias_grad.shape[1]), jnp.float32),
        bias_grad,
        tensor_index * head_count,
        0,
    )
    gain_sums, bias_sums = lax.psum(
        (jnp.stack([gain_one_grad, gain_two_grad]), bias_full), ("dp", "tensor")
    )
    gains_grad = lax.dynamic_slice_in_dim(gain_sums, dp_index * shard_rows, shard_rows, 1)
    bias_out = lax.dynamic_slice_in_dim(bias_sums, tensor_index * head_count, head_count, 0)
    return (
        mixed,
        input_grad,
        qkv_grad,
        out_grad[0],
        gains_grad,
        bias_out,
        regroup(gate_back),
        regroup(up_back),
        regroup(down_back),
    )


def solution(mesh):
    placed = (
        P(("dp", "tensor"), None),
        P(("dp", "tensor"), None),
        P(),
        P(),
        P("dp", None),
        P("dp", None),
        P(None, "dp", "tensor"),
        P("dp", "tensor"),
        P(None, "dp"),
        P("tensor", None),
        P(None, "dp", "tensor"),
        P(None, "dp", "tensor"),
        P(None, "dp", "tensor"),
    )
    return jax.shard_map(
        on_device,
        mesh=mesh,
        in_specs=placed,
        out_specs=(
            P(("dp", "tensor"), None),
            P(("dp", "tensor"), None),
            P(None, "dp", "tensor"),
            P("dp", "tensor"),
            P(None, "dp"),
            P("tensor", None),
            P(None, "dp", "tensor"),
            P(None, "dp", "tensor"),
            P(None, "dp", "tensor"),
        ),
        check_vma=False,
    )
```

profile of v0, /device:TPU:16, one launch (start us, length us, event | category | flops | bytes accessed | tf_op | source)
XLA Modules:
  0.0 1174.3 jit_solution(2398553649881257064)
XLA Ops:
  13.6 74.3 %all-gather.1 = bf16[16,64,2]{1,2,0:T(2,128)(2,1)S(1)} all-gather(bf16[1,64,2]{1,2,0:T(2,128)(2,1)S(1)} %bitcast.248), channel_id=1, replica_groups=mesh['dp'=16,'tensor'=2] {'dp'}, dimensions={0}, use_global_device_ids=true | all-gather | bytes 4352 | tf_op jit(solution)/shard_map/all_gather | solution.py:234
  96.3 14.0 %all-gather.9.cloned.1.call-done = bf16[512,1024]{1,0:T(8,128)(2,1)} async-done(((bf16[256,1024]{1,0:T(8,128)(2,1)}), bf16[512,1024]{1,0:T(8,128)(2,1)}) %all-gather.9.cloned.1.call-update) | async-done | bytes 1048592 | tf_op jit(solution)/shard_map/all_gather | solution.py:203
  110.3 65.4 %all-gather.11.cloned.1.call-done = bf16[3,1024,512]{2,1,0:T(8,128)(2,1)} async-done(((bf16[3,64,512]{2,1,0:T(8,128)(2,1)}), bf16[3,1024,512]{2,1,0:T(8,128)(2,1)}) %all-gather.11.cloned.1.call-update) | async-done | bytes 3145744 | tf_op jit(solution)/shard_map/all_gather | solution.py:232
  184.3 8.6 all-to-all-start.3
  192.9 99.5 %while.30 = (s32[]{:T(128)}, bf16[8,512,64]{1,2,0:T(8,128)(2,1)S(1)}, f32[8,512]{1,0:T(8,128)S(1)}, s32[8]{0:T(128)S(1)}, bf16[512,512]{1,0:T(8,128)(2,1)}, /*in...) while((s32[]{:T(128)}, ...), condition=%wide.region_4.5_spmd.clone, body=%wide.region_1.0_spmd.clone.sunk | while | flops 69928552 | bytes 19381492 | solution.py:101
  302.9 14.2 %reduce-scatter.7.cloned.1.call-done = bf16[256,1024]{1,0:T(8,128)(2,1)} async-done(((bf16[512,1024]{1,0:T(8,128)(2,1)}), bf16[256,1024]{1,0:T(8,128)(2,1)}) %reduce-scatter.7.cloned.1.call-update) | async-done | bytes 524304 | tf_op jit(solution)/shard_map/reduce_scatter | solution.py:206
  321.3 16.4 %scatter_custom_fusion = s32[1152]{0:T(1024)S(1)} fusion(s32[1024]{0:T(1024)S(1)} %bitcast.246, s32[1024]{0:T(1024)S(1)} %add_select_fusion.2, s32[]{:T(128)} %constant.180.clone.1), kind=kCustom, calls=%fused_computation.180 | custom fusion | bytes 4612 | tf_op jit(solution)/shard_map/scatter | solution.py:269
  365.0 18.8 %all-gather.15.cloned.1.call-done = bf16[512,1024]{1,0:T(8,128)(2,1)} async-done(((bf16[256,1024]{1,0:T(8,128)(2,1)}), bf16[512,1024]{1,0:T(8,128)(2,1)}) %all-gather.15.cloned.1.call-update) | async-done | bytes 1048592 | tf_op jit(solution)/shard_map/all_gather | solution.py:203
  394.9 18.2 %all-to-all-done = bf16[16,72,1024]{2,1,0:T(8,128)(2,1)} async-done(((bf16[16,72,1024]{2,1,0:T(8,128)(2,1)}), bf16[16,72,1024]{2,1,0:T(8,128)(2,1)}, u32[]{:S(2)}, u32[]{:S(2)}) %all-to-all-start) | async-done | bytes 2359328 | tf_op jit(solution)/shard_map/all_to_all | solution.py:211
  417.8 9.1 fusion.90
  426.9 9.1 fusion.91
  436.0 35.2 %all-to-all-done.5 = bf16[16,72,1024]{2,1,0:T(8,128)(2,1)} async-done(((bf16[16,72,1024]{2,1,0:T(8,128)(2,1)}), bf16[16,72,1024]{2,1,0:T(8,128)(2,1)}, u32[]{:S(2)}, u32[]{:S(2)}) %all-to-all-start.5) | async-done | bytes 2359328 | tf_op jit(solution)/shard_map/all_to_all | solution.py:211
  471.2 14.3 %multiply_convert_fusion.1 = (bf16[1152,1408]{1,0:T(8,128)(2,1)S(1)}, bf16[1152,1408]{1,0:T(8,128)(2,1)S(1)}, bf16[1152,1408]{1,0:T(8,128)(2,1)}) fusion(f32[1152,1408]{1,0:T(8,128)} %fusion.90, f32[1152,1408]{1,0:T(8,128)} %fusion.91, bf16[1152,1024]{1,0:T(8,128)(2,1)} %bitcast.25, bf16[1024,1408]{1,0:T(8,128)(2,1)} %bitcast.21), kind=kOutput, calls=%fused_computation.82 | convolution fusion | flops 3364061184 | bytes 27951104 | tf_op jit(solution)/shard_map/dot_general | solution.py:320
  513.5 45.3 %all-to-all-done.6 = bf16[16,72,1024]{2,1,0:T(8,128)(2,1)} async-done(((bf16[16,72,1024]{2,1,0:T(8,128)(2,1)}), bf16[16,72,1024]{2,1,0:T(8,128)(2,1)}, u32[]{:S(2)}, u32[]{:S(2)}) %all-to-all-start.6) | async-done | bytes 2359328 | tf_op jit(solution)/shard_map/all_to_all | solution.py:221
  567.9 8.7 gather_fusion.3
  576.5 40.3 %all-to-all-done.4 = bf16[16,72,1024]{2,1,0:T(8,128)(2,1)} async-done(((bf16[16,72,1024]{2,1,0:T(8,128)(2,1)}), bf16[16,72,1024]{2,1,0:T(8,128)(2,1)}, u32[]{:S(2)}, u32[]{:S(2)}) %all-to-all-start.4) | async-done | bytes 2359328 | tf_op jit(solution)/shard_map/all_to_all | solution.py:221
  621.2 8.7 gather_fusion.1
  651.7 18.9 %reduce-scatter.11.cloned.1.call-done = bf16[256,1024]{1,0:T(8,128)(2,1)} async-done(((bf16[512,1024]{1,0:T(8,128)(2,1)}), bf16[256,1024]{1,0:T(8,128)(2,1)}) %reduce-scatter.11.cloned.1.call-update) | async-done | bytes 524304 | tf_op jit(solution)/shard_map/reduce_scatter | solution.py:206
  698.8 213.1 %while.31 = (s32[]{:T(128)}, bf16[8,512,64]{1,2,0:T(8,128)(2,1)}, bf16[8,512,64]{1,2,0:T(8,128)(2,1)}, bf16[8,512,64]{1,2,0:T(8,128)(2,1)}, f32[8,32]{1,0:T(8,12...) while((s32[]{:T(128)}, bf16[8,512,64]{1,2,0:T(8,128)(2,1)}, ...), condition=%wide.region_20.23_spmd.clone, body=%wide.region_17.22_spmd.clone.sunk | while | flops 172360896 | bytes 41221816 | solution.py:161
  923.3 8.7 multiply_reduce_fusion.1
  956.1 8.5 convolution_convert_fusion.2
  964.6 58.5 %all-to-all-done.7 = bf16[16,64,1408]{2,1,0:T(8,128)(2,1)S(1)} async-done(((bf16[16,64,1408]{2,1,0:T(8,128)(2,1)}), bf16[16,64,1408]{2,1,0:T(8,128)(2,1)S(1)}, u32[]{:S(2)}, u32[]{:S(2)}) %all-to-all-start.7) | async-done | bytes 2883616 | tf_op jit(solution)/shard_map/all_to_all | solution.py:376
  1035.9 81.8 %all-to-all-done.8 = bf16[16,64,1408]{2,1,0:T(8,128)(2,1)} async-done(((bf16[16,64,1408]{2,1,0:T(8,128)(2,1)}), bf16[16,64,1408]{2,1,0:T(8,128)(2,1)}, u32[]{:S(2)}, u32[]{:S(2)}) %all-to-all-start.8) | async-done | bytes 2883616 | tf_op jit(solution)/shard_map/all_to_all | solution.py:379
  1124.2 38.6 %all-reduce.2 = (f32[2,1024]{1,0:T(2,128)S(1)}, f32[16,32]{1,0:T(8,128)S(1)}) all-reduce(f32[2,1024]{1,0:T(2,128)S(1)} %pad_maximum_fusion.4, f32[16,32]{1,0:T(8,128)S(1)} %constant_dynamic-update-slice_fusion), channel_id=1, replica_groups=mesh['dp'=16,'tensor'=2] {'dp','tensor'}, use_global_device_ids=true, to_apply=%region_27.30 | all-reduce | flops 2560 | bytes 20480 | tf_op jit(solution)/shard_map/psum | solution.py:392
  (580 shorter events, 501.0 us)
Async XLA Ops:
  7.2 83.3 %all-to-all-start.1 = ((bf16[16,64,1408]{2,1,0:T(8,128)(2,1)}), bf16[16,64,1408]{2,1,0:T(8,128)(2,1)}, u32[]{:S(2)}, u32[]{:S(2)}) async-start(bf16[16,64,1408]{2,1,0:T(8,128)(2,1)} %param.31), calls=%async_computation.2 | async-start | bytes 5767168 | tf_op jit(solution)/shard_map/all_to_all | solution.py:242
  13.5 96.8 %all-gather.9.cloned.1.call-start = ((), (), s32[]{:S(2)}) async-start(), calls=%async_computation.16 | async-start | bytes 1572864 | tf_op jit(solution)/shard_map/all_gather | solution.py:203
  89.7 86.0 %all-gather.11.cloned.1.call-start = ((), (), s32[]{:S(2)}) async-start(), calls=%async_computation.17 | async-start | bytes 3342336 | tf_op jit(solution)/shard_map/all_gather | solution.py:232
  90.5 93.8 %all-to-all-start.2 = ((bf16[16,64,1408]{2,1,0:T(8,128)(2,1)}), bf16[16,64,1408]{2,1,0:T(8,128)(2,1)}, u32[]{:S(2)}, u32[]{:S(2)}) async-start(bf16[16,64,1408]{2,1,0:T(8,128)(2,1)} %param.32), calls=%async_computation.3 | async-start | bytes 5767168 | tf_op jit(solution)/shard_map/all_to_all | solution.py:243
  94.9 197.6 %all-gather.19.cloned.1.call-start = ((), (), s32[]{:S(2)}) async-start(), calls=%async_computation.27 | async-start | bytes 1114112 | tf_op jit(solution)/shard_map/all_gather | solution.py:233
  184.3 169.3 %all-to-all-start.3 = ((bf16[16,64,1408]{2,1,0:T(8,128)(2,1)}), bf16[16,64,1408]{2,1,0:T(8,128)(2,1)}, u32[]{:S(2)}, u32[]{:S(2)}) async-start(bf16[16,64,1408]{2,1,0:T(8,128)(2,1)} %param.33), calls=%async_computation.4 | async-start | bytes 5767168 | tf_op jit(solution)/shard_map/all_to_all | solution.py:244
  192.9 124.2 %reduce-scatter.7.cloned.1.call-start = ((), (), s32[]{:S(2)}) async-start(), calls=%async_computation.18 | async-start | bytes 1572864 | tf_op jit(solution)/shard_map/reduce_scatter | solution.py:206
  295.6 46.6 %all-gather.13.cloned.1.call-start = ((), (), s32[]{:S(2)}) async-start(), calls=%async_computation.19 | async-start | bytes 1572864 | tf_op jit(solution)/shard_map/all_gather | solution.py:203
  353.6 59.6 %all-to-all-start = ((bf16[16,72,1024]{2,1,0:T(8,128)(2,1)}), bf16[16,72,1024]{2,1,0:T(8,128)(2,1)}, u32[]{:S(2)}, u32[]{:S(2)}) async-start(bf16[16,72,1024]{2,1,0:T(8,128)(2,1)} %bitcast.212), calls=%async_computation.1 | async-start | bytes 4718592 | tf_op jit(solution)/shard_map/all_to_all | solution.py:211
  359.7 24.0 %all-gather.15.cloned.1.call-start = ((), (), s32[]{:S(2)}) async-start(), calls=%async_computation.21 | async-start | bytes 1572864 | tf_op jit(solution)/shard_map/all_gather | solution.py:203
  413.1 58.1 %all-to-all-start.5 = ((bf16[16,72,1024]{2,1,0:T(8,128)(2,1)}), bf16[16,72,1024]{2,1,0:T(8,128)(2,1)}, u32[]{:S(2)}, u32[]{:S(2)}) async-start(bf16[16,72,1024]{2,1,0:T(8,128)(2,1)} %bitcast.213), calls=%async_computation.7 | async-start | bytes 4718592 | tf_op jit(solution)/shard_map/all_to_all | solution.py:211
  500.3 58.4 %all-to-all-start.6 = ((bf16[16,72,1024]{2,1,0:T(8,128)(2,1)}), bf16[16,72,1024]{2,1,0:T(8,128)(2,1)}, u32[]{:S(2)}, u32[]{:S(2)}) async-start(bf16[16,72,1024]{2,1,0:T(8,128)(2,1)} %bitcast.216), calls=%async_computation.8 | async-start | bytes 4718592 | tf_op jit(solution)/shard_map/all_to_all | solution.py:221
  558.7 58.1 %all-to-all-start.4 = ((bf16[16,72,1024]{2,1,0:T(8,128)(2,1)}), bf16[16,72,1024]{2,1,0:T(8,128)(2,1)}, u32[]{:S(2)}, u32[]{:S(2)}) async-start(bf16[16,72,1024]{2,1,0:T(8,128)(2,1)} %convolution_convert_fusion.4), calls=%async_computation.5 | async-start | bytes 4718592 | tf_op jit(solution)/shard_map/all_to_all | solution.py:221
  563.4 107.1 %reduce-scatter.11.cloned.1.call-start = ((), (), s32[]{:S(2)}) async-start(), calls=%async_computation.22 | async-start | bytes 1572864 | tf_op jit(solution)/shard_map/reduce_scatter | solution.py:206
  651.4 44.6 %all-gather.17.cloned.1.call-start = ((), (), s32[]{:S(2)}) async-start(), calls=%async_computation.23 | async-start | bytes 1572864 | tf_op jit(solution)/shard_map/all_gather | solution.py:203
  683.1 259.6 %all-to-all-start.9 = ((bf16[16,64,1408]{2,1,0:T(8,128)(2,1)}), bf16[16,64,1408]{2,1,0:T(8,128)(2,1)}, u32[]{:S(2)}, u32[]{:S(2)}) async-start(bf16[16,64,1408]{2,1,0:T(8,128)(2,1)} %bitcast.47), calls=%async_computation.15 | async-start | bytes 5767168 | tf_op jit(solution)/shard_map/all_to_all | solution.py:382
  689.3 433.4 %reduce-scatter.13.cloned.1.call-start = ((), (), s32[]{:S(2)}) async-start(), calls=%async_computation.24 | async-start | bytes 1572864 | tf_op jit(solution)/shard_map/reduce_scatter | solution.py:206
  916.9 247.1 %reduce-scatter.9.cloned.1.call-start = ((), (), s32[]{:S(2)}) async-start(), calls=%async_computation.20 | async-start | bytes 1572864 | tf_op jit(solution)/shard_map/reduce_scatter | solution.py:206
  932.0 235.3 %reduce-scatter.17.cloned.1.call-start = ((), (), s32[]{:S(2)}) async-start(), calls=%async_computation.26 | async-start | bytes 2228224 | tf_op jit(solution)/shard_map/reduce_scatter | solution.py:373
  942.7 80.4 %all-to-all-start.7 = ((bf16[16,64,1408]{2,1,0:T(8,128)(2,1)}), bf16[16,64,1408]{2,1,0:T(8,128)(2,1)S(1)}, u32[]{:S(2)}, u32[]{:S(2)}) async-start(bf16[16,64,1408]{2,1,0:T(8,128)(2,1)} %bitcast.215), calls=%async_computation.13 | async-start | bytes 5767168 | tf_op jit(solution)/shard_map/all_to_all | solution.py:376
  948.7 218.6 %reduce-scatter.15.cloned.1.call-start = ((), (), s32[]{:S(2)}) async-start(), calls=%async_computation.25 | async-start | bytes 6684672 | tf_op jit(solution)/shard_map/reduce_scatter | solution.py:372
  1023.1 94.6 %all-to-all-start.8 = ((bf16[16,64,1408]{2,1,0:T(8,128)(2,1)}), bf16[16,64,1408]{2,1,0:T(8,128)(2,1)}, u32[]{:S(2)}, u32[]{:S(2)}) async-start(bf16[16,64,1408]{2,1,0:T(8,128)(2,1)} %bitcast.214), calls=%async_computation.14 | async-start | bytes 5767168 | tf_op jit(solution)/shard_map/all_to_all | solution.py:379
  1035.8 128.2 %copy-start.4 = (bf16[256,1024]{1,0:T(8,128)(2,1)S(1)}, bf16[256,1024]{1,0:T(8,128)(2,1)}, u32[]{:S(2)}) copy-start(bf16[256,1024]{1,0:T(8,128)(2,1)} %reduce-scatter.7.cloned.1.call-done) | copy-start | bytes 1572868
  1035.9 128.2 %copy-start.7 = (bf16[256,1024]{1,0:T(8,128)(2,1)S(1)}, bf16[256,1024]{1,0:T(8,128)(2,1)}, u32[]{:S(2)}) copy-start(bf16[256,1024]{1,0:T(8,128)(2,1)} %reduce-scatter.11.cloned.1.call-done) | copy-start | bytes 1572868
  (39 other events, 915.8 us)
Sparse Core Ops, SparseCore 0:
  89.8 20.4 all-gather.8
  112.5 63.1 all-gather.10
  177.9 61.6 all-gather.18
  295.8 21.2 reduce-scatter.6
  320.9 21.2 all-gather.12
  362.4 21.2 all-gather.14
  651.6 18.9 reduce-scatter.10
  674.7 21.3 all-gather.16
  917.1 20.3 reduce-scatter.12
  939.6 20.3 reduce-scatter.8
  964.3 66.3 reduce-scatter.16
  1035.5 100.5 reduce-scatter.14
where the time goes:
time: 1190 us; the launch traced here: 1170 us
  waiting for transfers between devices  424 us (36%)
  local copies, waits for them, and re-layouts  211 us (18%)
  matrix products  208 us (17%)
  blocking collectives  113 us (9%)
  other arithmetic  103 us (9%)
  starting transfers between devices  58 us (5%)
  loops' own time  43 us (4%)
  between operations  15.1 us (1%)
    all_to_all x2, waiting for transfers between devices, route_back(): lax.all_to_all(slot_rows.reshape(dp_count, slot_count, model_width).astyp...  85.5 us
    all_to_all x1, waiting for transfers between devices, on_device(): lax.all_to_all(up_part.astype(jnp.bfloat16), 'dp', split_axis=0, concat_a...  81.8 us
    all_gather x1, blocking collectives, fetch_layer(): lax.all_gather(norm_gains, 'dp', axis=1, tiled=True)  74.3 us
    all_gather x1, waiting for transfers between devices, fetch_layer(): lax.all_gather(qkv_weight, 'dp', axis=1, tiled=True)  65.4 us
    dot_general x31, matrix products, contract_cols(): lax.dot_general(left_side, right_side, (((1,), (1,)), ((), ())), preferre...  64.8 us
    dot_general x23, matrix products, contract_rows(): lax.dot_general(left_side, right_side, (((0,), (0,)), ((), ())), preferre...  62.9 us
    all_to_all x1, waiting for transfers between devices, on_device(): lax.all_to_all(gate_part.astype(jnp.bfloat16), 'dp', split_axis=0, concat...  58.5 us
    all_to_all x2, waiting for transfers between devices, route_out(): lax.all_to_all(slot_rows.reshape(dp_count, slot_count, model_width), 'dp'...  53.3 us
  transfers between devices with their start and end apart: 22, of which 13 were waited for; matrix products, arithmetic and copies ran while one was open for 39% of the time, Pallas kernels for 0%

commit v1 on v0

v1 whole, which is shorter than its diff:
```python
import jax
import jax.numpy as jnp
from jax import lax
from jax.experimental import pallas as pl
from jax.experimental.pallas import tpu as pltpu
from jax.sharding import PartitionSpec as P

HEAD_DIM = 64
EPSILON = 1e-06
MASKED_SCORE = -1e30
HIGHEST = lax.Precision.HIGHEST
SCORE_SCALE = 0.125
QUERY_COLS = 256
LANES = 128
GELU_SCALE = 0.7978845608028654
GELU_CUBIC = 0.044715


def dot_nt(left, right):
    return lax.dot_general(
        left, right, (((1,), (1,)), ((), ())), preferred_element_type=jnp.float32
    )


def dot_nn(left, right):
    return lax.dot_general(
        left, right, (((1,), (0,)), ((), ())), preferred_element_type=jnp.float32
    )


def dot_tn(left, right):
    return lax.dot_general(
        left, right, (((0,), (0,)), ((), ())), preferred_element_type=jnp.float32
    )


def bias_base(bias_row, seq):
    return pltpu.roll(
        jnp.broadcast_to(bias_row, (LANES, 2 * seq)),
        2 * seq - (LANES - 1),
        1,
        stride=1,
        stride_axis=0,
    )


def masked_scores(keys, query_block, base_ref, start, seq, cols, length):
    scores = dot_nt(keys, query_block) * SCORE_SCALE
    blocks = []
    for first in range(0, seq, LANES):
        offset = seq - LANES - first + start
        block = scores[first : first + LANES] + base_ref[:, offset : offset + cols]
        key_index = lax.broadcasted_iota(jnp.int32, block.shape, 0) + first
        blocks.append(jnp.where(key_index < length, block, MASKED_SCORE))
    return jnp.concatenate(blocks, axis=0)


def head_part(ref, start, cols, head):
    lane = lax.broadcasted_iota(jnp.int32, (cols, LANES), 1)
    return jnp.where(
        lane // HEAD_DIM == head, ref[start : start + cols, :], jnp.zeros((), jnp.bfloat16)
    )


def forward_kernel(
    length_ref, query_ref, key_ref, value_ref, bias_ref, out_ref, total_ref, base_ref
):
    seq = query_ref.shape[0]
    cols = min(QUERY_COLS, seq)
    length = length_ref[0]
    values_t = value_ref[...].T
    keys = key_ref[...]
    starts = range(0, seq, cols)
    outs = {}
    for head in range(LANES // HEAD_DIM):
        base_ref[...] = bias_base(bias_ref[0, head : head + 1, :], seq)
        for start in starts:
            query_block = head_part(query_ref, start, cols, head)
            scores = masked_scores(keys, query_block, base_ref, start, seq, cols, length)
            top = jnp.max(scores, axis=0, keepdims=True)
            exponent = jnp.exp(scores - top)
            total = jnp.sum(exponent, axis=0, keepdims=True)
            probs = (exponent * (1.0 / total)).astype(jnp.bfloat16)
            total_ref[0, head : head + 1, start : start + cols] = top + jnp.log(total)
            outs[start, head] = dot_nn(
                values_t[head * HEAD_DIM : (head + 1) * HEAD_DIM], probs
            )
    for start in starts:
        joined = jnp.concatenate(
            [outs[start, head] for head in range(LANES // HEAD_DIM)], axis=0
        )
        out_ref[start : start + cols, :] = joined.T.astype(jnp.bfloat16)


def attend_forward(length, queries, keys, values, bias_rows):
    seq, width = queries.shape
    pairs = width // LANES
    heads = LANES // HEAD_DIM
    column = pl.BlockSpec((seq, LANES), lambda i: (0, i))
    return pl.pallas_call(
        forward_kernel,
        grid=(pairs,),
        in_specs=[
            pl.BlockSpec(memory_space=pltpu.SMEM),
            column,
            column,
            column,
            pl.BlockSpec((1, heads, 2 * seq), lambda i: (i, 0, 0)),
        ],
        out_specs=[column, pl.BlockSpec((1, heads, seq), lambda i: (i, 0, 0))],
        out_shape=[
            jax.ShapeDtypeStruct((seq, width), jnp.bfloat16),
            jax.ShapeDtypeStruct((pairs, heads, seq), jnp.float32),
        ],
        scratch_shapes=[pltpu.VMEM((LANES, 2 * seq), jnp.float32)],
        cost_estimate=pl.CostEstimate(
            flops=16 * seq * seq * width,
            transcendentals=seq * seq * width // HEAD_DIM,
            bytes_accessed=8 * seq * width,
        ),
        name="attend_forward",
    )(length, queries, keys, values, bias_rows)


def diagonal_sums(acc_ref, seq):
    period = 2 * seq
    folded = acc_ref[0:8, :]
    for first in range(8, LANES, 8):
        folded = folded + pltpu.roll(acc_ref[first : first + 8, :], period - first, 1)
    row = lax.broadcasted_iota(jnp.int32, folded.shape, 0)
    for bit in (1, 2, 4):
        folded = jnp.where((row & bit) != 0, pltpu.roll(folded, period - bit, 1), folded)
    return pltpu.roll(jnp.sum(folded, axis=0, keepdims=True), LANES - 1, 1)


def backward_kernel(
    length_ref,
    query_ref,
    key_ref,
    value_ref,
    grad_ref,
    total_ref,
    bias_ref,
    query_grad_ref,
    key_grad_ref,
    value_grad_ref,
    bias_grad_ref,
    base_ref,
    acc_ref,
):
    seq = query_ref.shape[0]
    cols = min(QUERY_COLS, seq)
    length = length_ref[0]
    keys = key_ref[...]
    values = value_ref[...]
    keys_t = keys.T
    starts = range(0, seq, cols)
    key_acc = jnp.zeros((seq, LANES), jnp.float32)
    value_acc = jnp.zeros((seq, LANES), jnp.float32)
    query_parts = {}
    for head in range(LANES // HEAD_DIM):
        base_ref[...] = bias_base(bias_ref[0, head : head + 1, :], seq)
        acc_ref[...] = jnp.zeros_like(acc_ref)
        for start in starts:
            query_block = head_part(query_ref, start, cols, head)
            grad_block = head_part(grad_ref, start, cols, head)
            scores = masked_scores(keys, query_block, base_ref, start, seq, cols, length)
            probs = jnp.exp(scores - total_ref[0, head : head + 1, start : start + cols])
            probs_grad = dot_nt(values, grad_block)
            mean_grad = jnp.sum(probs * probs_grad, axis=0, keepdims=True)
            score_grad = (probs * (probs_grad - mean_grad)).astype(jnp.bfloat16)
            value_acc = value_acc + dot_nn(probs.astype(jnp.bfloat16), grad_block)
            key_acc = key_acc + dot_nn(score_grad, query_block)
            query_parts[start, head] = dot_nn(
                keys_t[head * HEAD_DIM : (head + 1) * HEAD_DIM], score_grad
            )
            for first in range(0, seq, LANES):
                offset = seq - LANES - first + start
                acc_ref[:, offset : offset + cols] += score_grad[
                    first : first + LANES
                ].astype(jnp.float32)
        bias_grad_ref[0, head : head + 1, :] = diagonal_sums(acc_ref, seq)
    key_grad_ref[...] = (key_acc * SCORE_SCALE).astype(jnp.bfloat16)
    value_grad_ref[...] = value_acc.astype(jnp.bfloat16)
    for start in starts:
        joined = jnp.concatenate(
            [query_parts[start, head] for head in range(LANES // HEAD_DIM)], axis=0
        )
        query_grad_ref[start : start + cols, :] = (joined * SCORE_SCALE).T.astype(
            jnp.bfloat16
        )


def attend_backward(length, queries, keys, values, attended_grad, totals, bias_rows):
    seq, width = queries.shape
    pairs = width // LANES
    heads = LANES // HEAD_DIM
    column = pl.BlockSpec((seq, LANES), lambda i: (0, i))
    vector = pl.BlockSpec((1, heads, 2 * seq), lambda i: (i, 0, 0))
    grad_shape = jax.ShapeDtypeStruct((seq, width), jnp.bfloat16)
    return pl.pallas_call(
        backward_kernel,
        grid=(pairs,),
        in_specs=[
            pl.BlockSpec(memory_space=pltpu.SMEM),
            column,
            column,
            column,
            column,
            pl.BlockSpec((1, heads, seq), lambda i: (i, 0, 0)),
            vector,
        ],
        out_specs=[column, column, column, vector],
        out_shape=[
            grad_shape,
            grad_shape,
            grad_shape,
            jax.ShapeDtypeStruct((pairs, heads, 2 * seq), jnp.float32),
        ],
        scratch_shapes=[
            pltpu.VMEM((LANES, 2 * seq), jnp.float32),
            pltpu.VMEM((LANES, 2 * seq), jnp.float32),
        ],
        cost_estimate=pl.CostEstimate(
            flops=40 * seq * seq * width,
            transcendentals=seq * seq * width // HEAD_DIM,
            bytes_accessed=14 * seq * width,
        ),
        name="attend_backward",
    )(length, queries, keys, values, attended_grad, totals, bias_rows)


def gelu_parts(gate_pre):
    inner = jnp.tanh(GELU_SCALE * (gate_pre + GELU_CUBIC * gate_pre * gate_pre * gate_pre))
    gelu = 0.5 * gate_pre * (1.0 + inner)
    slope = 0.5 * (1.0 + inner) + 0.5 * gate_pre * (1.0 - inner * inner) * GELU_SCALE * (
        1.0 + 3.0 * GELU_CUBIC * gate_pre * gate_pre
    )
    return gelu, slope


def on_device(
    tokens,
    cotangent,
    lengths,
    bucket_table,
    routes,
    gate_values,
    qkv_weight,
    out_weight,
    norm_gains,
    rel_bias,
    gate_weight,
    up_weight,
    down_weight,
):
    tok_rows, width = tokens.shape
    half = width // 2
    dp_count = lax.axis_size("dp")
    tensor_count = lax.axis_size("tensor")
    seq = tok_rows * tensor_count
    expert_count, shard_rows, hidden_cols = gate_weight.shape
    head_cols = qkv_weight.shape[2]
    head_count, bucket_count = rel_bias.shape
    capacity = 9 * seq // 64
    group_size = dp_count // expert_count
    slot_count = (capacity + group_size - 1) // group_size
    total_slots = dp_count * slot_count
    dp_index = lax.axis_index("dp")
    tensor_index = lax.axis_index("tensor")
    first_tensor = tensor_index == 0
    length = lengths[dp_index]
    length_row = length[None]
    group_valid = jnp.arange(seq, dtype=jnp.int32) < length
    own_valid = lax.dynamic_slice_in_dim(group_valid, tensor_index * tok_rows, tok_rows, 0)
    own_valid = own_valid.astype(jnp.float32)[:, None]

    def swap(block):
        return lax.ppermute(block, "tensor", [(0, 1), (1, 0)])

    def after(block, *earlier):
        return lax.optimization_barrier((block, *earlier))[0]

    def ordered(own, other, axis):
        return jnp.where(
            first_tensor,
            jnp.concatenate([own, other], axis=axis),
            jnp.concatenate([other, own], axis=axis),
        )

    def own_part(block, axis):
        size = block.shape[axis] // 2
        return lax.dynamic_slice_in_dim(block, tensor_index * size, size, axis)

    def other_part(block, axis):
        size = block.shape[axis] // 2
        return lax.dynamic_slice_in_dim(block, (1 - tensor_index) * size, size, axis)

    def exchange(block):
        return lax.all_to_all(block, "dp", split_axis=0, concat_axis=0, tiled=True)

    def home_order(weight):
        return jnp.repeat(weight, group_size, axis=0)

    def fetch(weight, *earlier):
        arrived = exchange(after(home_order(weight), *earlier))
        return arrived.reshape(dp_count * shard_rows, weight.shape[2])

    def send_grad(grad, *earlier):
        return exchange(after(grad.reshape(dp_count, shard_rows, grad.shape[1]), *earlier))

    def route(rows, *earlier):
        arrived = exchange(after(rows.reshape(dp_count, slot_count, rows.shape[1]), *earlier))
        return arrived.reshape(total_slots, rows.shape[1])

    def regroup(arrived):
        return jnp.sum(
            arrived.astype(jnp.float32).reshape(
                expert_count, group_size, shard_rows, arrived.shape[2]
            ),
            axis=1,
        )

    gain_pad = jnp.pad(norm_gains, ((0, 14), (0, head_cols - shard_rows)))
    layer_shard = jnp.concatenate(
        [qkv_weight.reshape(3 * shard_rows, head_cols), gain_pad], axis=0
    )
    layer_all = lax.all_gather(layer_shard, "dp", axis=0, tiled=False)
    tokens_other = swap(tokens)
    mix_grad = (own_valid * cotangent.astype(jnp.float32)).astype(jnp.bfloat16)
    mix_other = swap(other_part(mix_grad, 1))
    out_all = lax.all_gather(out_weight, "dp", axis=0, tiled=True)
    gate_up_all = fetch(jnp.concatenate([gate_weight, up_weight], axis=2))

    pair_expert = routes.reshape(-1)
    pair_valid = jnp.repeat(group_valid, 2)
    chosen = (
        pair_expert[:, None] == jnp.arange(expert_count, dtype=jnp.int32)[None, :]
    ) & pair_valid[:, None]
    pair_index = jnp.arange(2 * seq, dtype=jnp.int32)
    before = (pair_index[:, None] > pair_index[None, :]).astype(jnp.bfloat16)
    earlier_pairs = dot_nn(before, chosen.astype(jnp.bfloat16))
    position = jnp.sum(jnp.where(chosen, earlier_pairs, 0.0), axis=1).astype(jnp.int32)
    kept_pair = pair_valid & (position < capacity)
    device = pair_expert * group_size + position // slot_count
    pair_slot = jnp.where(
        kept_pair, device * slot_count + position % slot_count, total_slots
    ).reshape(seq, 2)
    slot_index = jnp.arange(total_slots, dtype=jnp.int32)
    first_hit = pair_slot[:, 0][None, :] == slot_index[:, None]
    second_hit = pair_slot[:, 1][None, :] == slot_index[:, None]
    no_gate = jnp.zeros((), jnp.bfloat16)
    pick = (first_hit | second_hit).astype(jnp.bfloat16)
    pick_gate = jnp.where(
        first_hit,
        gate_values[:, 0][None, :],
        jnp.where(second_hit, gate_values[:, 1][None, :], no_gate),
    )

    out_grad_cols = dot_nn(
        pick_gate, ordered(own_part(mix_grad, 1), mix_other, 0)
    ).astype(jnp.bfloat16)
    slot_grad_half = route(out_grad_cols, gate_up_all)
    slot_grad = ordered(slot_grad_half, swap(slot_grad_half), 1)

    distance = jnp.arange(2 * seq, dtype=jnp.int32)
    table_reversed = jnp.concatenate(
        [bucket_table[::-1], jnp.full((1,), bucket_count, jnp.int32)]
    )
    hot = (
        jnp.arange(bucket_count, dtype=jnp.int32)[:, None] == table_reversed[None, :]
    ).astype(jnp.float32)
    bias_rows = jnp.dot(rel_bias.astype(jnp.float32), hot, precision=HIGHEST).reshape(
        head_count // 2, 2, 2 * seq
    )
    gains_all = jnp.transpose(
        layer_all[:, 3 * shard_rows : 3 * shard_rows + 2, :shard_rows], (1, 0, 2)
    ).reshape(2, width)
    gain_one = gains_all[0].astype(jnp.float32)
    gain_two = gains_all[1].astype(jnp.float32)
    projections = [
        layer_all[:, i * shard_rows : (i + 1) * shard_rows].reshape(width, head_cols)
        for i in range(3)
    ]
    inputs_all = ordered(tokens, tokens_other, 0).astype(jnp.float32)
    scale_all = lax.rsqrt(jnp.mean(inputs_all * inputs_all, axis=-1, keepdims=True) + EPSILON)
    norm_one_all = (inputs_all * scale_all * gain_one).astype(jnp.bfloat16)
    queries, keys, values = [
        dot_nn(norm_one_all, weight).astype(jnp.bfloat16) for weight in projections
    ]
    attended, totals = attend_forward(length_row, queries, keys, values, bias_rows)
    branch = dot_nt(attended, out_all)
    branch_other = swap(other_part(branch, 0).astype(jnp.bfloat16))
    inputs = tokens.astype(jnp.float32)
    mid = inputs + own_valid * (own_part(branch, 0) + branch_other.astype(jnp.float32))
    mid_scale = lax.rsqrt(jnp.mean(mid * mid, axis=-1, keepdims=True) + EPSILON)
    norm_two = (mid * mid_scale * gain_two).astype(jnp.bfloat16)
    norm_two_cols = ordered(own_part(norm_two, 1), swap(other_part(norm_two, 1)), 0)
    expert_half = route(
        dot_nn(pick, norm_two_cols).astype(jnp.bfloat16), slot_grad_half
    )
    down_all = fetch(down_weight, expert_half)
    expert_in = ordered(expert_half, swap(expert_half), 1)

    pre = dot_nn(expert_in, gate_up_all)
    gate_pre = pre[:, :hidden_cols]
    up_pre = pre[:, hidden_cols:]
    gelu, slope = gelu_parts(gate_pre)
    hidden = (gelu * up_pre).astype(jnp.bfloat16)
    down_back = send_grad(dot_tn(slot_grad, hidden).astype(jnp.bfloat16), down_all)
    hidden_grad = dot_nn(slot_grad, down_all)
    pre_grad = jnp.concatenate(
        [
            (hidden_grad * up_pre * slope).astype(jnp.bfloat16),
            (hidden_grad * gelu).astype(jnp.bfloat16),
        ],
        axis=1,
    )
    slot_back_part = dot_nt(pre_grad, gate_up_all)
    slot_back_half = (
        own_part(slot_back_part, 1)
        + swap(other_part(slot_back_part, 1).astype(jnp.bfloat16)).astype(jnp.float32)
    ).astype(jnp.bfloat16)
    slot_back = route(slot_back_half, down_back)
    expert_out_part = dot_nt(hidden, down_all)
    expert_out_half = (
        own_part(expert_out_part, 1)
        + swap(other_part(expert_out_part, 1).astype(jnp.bfloat16)).astype(jnp.float32)
    ).astype(jnp.bfloat16)
    returned = route(expert_out_half, slot_back)
    gate_up_back = send_grad(dot_tn(expert_in, pre_grad).astype(jnp.bfloat16), returned)

    mix_cols = dot_tn(pick_gate, returned)
    mix_own = ordered(
        own_part(mix_cols, 0), swap(other_part(mix_cols, 0).astype(jnp.bfloat16)).astype(jnp.float32), 1
    )
    mixed = (mid + own_valid * mix_own).astype(jnp.bfloat16)
    back_cols = dot_tn(pick, slot_back)
    norm_two_grad = ordered(
        own_part(back_cols, 0), swap(other_part(back_cols, 0).astype(jnp.bfloat16)).astype(jnp.float32), 1
    )
    mid_unit = mid * mid_scale
    mid_inner = norm_two_grad * gain_two
    mid_grad = own_valid * cotangent.astype(jnp.float32) + mid_scale * (
        mid_inner - mid_unit * jnp.mean(mid_inner * mid_unit, axis=-1, keepdims=True)
    )
    gain_two_grad = jnp.sum(norm_two_grad * mid_unit, axis=0)
    branch_grad = (own_valid * mid_grad).astype(jnp.bfloat16)
    branch_grad_all = ordered(branch_grad, swap(branch_grad), 0)

    attended_grad = dot_nn(branch_grad_all, out_all).astype(jnp.bfloat16)
    out_part = dot_tn(branch_grad_all, attended).astype(jnp.bfloat16)
    out_grad = lax.psum_scatter(out_part, "dp", scatter_dimension=0, tiled=True)
    query_grad, key_grad, value_grad, bias_sums = attend_backward(
        length_row, queries, keys, values, attended_grad, totals, bias_rows
    )
    bias_grad = jnp.dot(
        bias_sums.reshape(head_count, 2 * seq), hot.T, precision=HIGHEST
    )
    norm_one_part = (
        dot_nt(query_grad, projections[0])
        + dot_nt(key_grad, projections[1])
        + dot_nt(value_grad, projections[2])
    )
    qkv_part = jnp.stack(
        [
            dot_tn(norm_one_all, grad).astype(jnp.bfloat16)
            for grad in (query_grad, key_grad, value_grad)
        ]
    )
    qkv_grad = lax.psum_scatter(qkv_part, "dp", scatter_dimension=1, tiled=True)
    gain_one_grad = jnp.sum(norm_one_part * (inputs_all * scale_all), axis=0)
    norm_one_grad = own_part(norm_one_part, 0) + swap(
        other_part(norm_one_part, 0).astype(jnp.bfloat16)
    ).astype(jnp.float32)
    scale = lax.rsqrt(jnp.mean(inputs * inputs, axis=-1, keepdims=True) + EPSILON)
    unit = inputs * scale
    inner = norm_one_grad * gain_one
    input_grad = mid_grad + scale * (
        inner - unit * jnp.mean(inner * unit, axis=-1, keepdims=True)
    )

    bias_full = lax.dynamic_update_slice_in_dim(
        jnp.zeros((head_count * tensor_count, bucket_count), jnp.float32),
        bias_grad,
        tensor_index * head_count,
        0,
    )
    gain_sums, bias_sums = lax.psum(
        (jnp.stack([gain_one_grad, gain_two_grad]), bias_full), ("dp", "tensor")
    )
    gains_grad = lax.dynamic_slice_in_dim(gain_sums, dp_index * shard_rows, shard_rows, 1)
    bias_out = lax.dynamic_slice_in_dim(bias_sums, tensor_index * head_count, head_count, 0)
    return (
        mixed,
        input_grad,
        qkv_grad.astype(jnp.float32),
        out_grad.astype(jnp.float32),
        gains_grad,
        bias_out,
        regroup(gate_up_back[:, :, :hidden_cols]),
        regroup(gate_up_back[:, :, hidden_cols:]),
        regroup(down_back),
    )


def solution(mesh):
    rows = P(("dp", "tensor"), None)
    shard = P("dp", "tensor")
    stacked = P(None, "dp", "tensor")
    return jax.shard_map(
        on_device,
        mesh=mesh,
        in_specs=(
            rows,
            rows,
            P(),
            P(),
            P("dp", None),
            P("dp", None),
            stacked,
            shard,
            P(None, "dp"),
            P("tensor", None),
            stacked,
            stacked,
            stacked,
        ),
        out_specs=(
            rows,
            rows,
            stacked,
            shard,
            P(None, "dp"),
            P("tensor", None),
            stacked,
            stacked,
            stacked,
        ),
        check_vma=False,
    )
```

time: 1190 us -> 734 us (0.62)
  local copies, waits for them, and re-layouts: 211 us -> 12.2 us
  matrix products: 208 us -> 94.1 us
  waiting for transfers between devices: 424 us -> 358 us
  other arithmetic: 103 us -> 37.8 us
  loops' own time: 43 us -> 0 us
  Pallas kernels: 0 us -> 24.2 us
    all_to_all x10 -> x7, waiting for transfers between devices: 279 us -> 66.7 us  [exchange(): return lax.all_to_all(block, 'dp', split_axis=0, concat_axis=0, tiled=True)]
    ppermute x0 -> x12, waiting for transfers between devices: none -> 147 us  [swap(): return lax.ppermute(block, 'tensor', [(0, 1), (1, 0)])]
    dot_general x101 -> x25, matrix products: 208 us -> 94.1 us  [the longest x9 37.9 us: dot_nn(): lax.dot_general(left, right, (((1,), (0,)), ((), ())), preferred_element_...]
    reshape x36 -> x2, local copies, waits for them, and re-layouts: 92.2 us -> 0.66 us  [the longest x1 0.64 us: on_device(): jnp.dot(rel_bias.astype(jnp.float32), hot, precision=HIGHEST)]
    all_gather x1 -> x0, blocking collectives: 74.3 us -> none  [fetch_layer(): lax.all_gather(norm_gains, 'dp', axis=1, tiled=True)]
    psum x1, blocking collectives: 38.6 us -> 82.1 us  [on_device(): lax.psum((jnp.stack([gain_one_grad, gain_two_grad]), bias_full), ('dp', '...]
    another operation x2 -> x0, loops' own time: 43 us -> none  [the longest x1 21.6 us: attend_backward(): lax.map(one_head, jnp.arange(head_count))]
    gather x4 -> x0, local copies, waits for them, and re-layouts: 33.3 us -> none  [the longest x1 8.67 us: on_device(): jnp.take(slot_back, pair_slot, axis=0, mode='fill', fill_value=0.0)]
  transfers between devices with their start and end apart: 22 -> 23, of which waited for: 13 -> 18; matrix products, arithmetic and copies ran while one was open for 39% -> 15% of each run, Pallas kernels for 0% -> 3%
where the time goes in v1:
time: 734 us; the launch traced here: 722 us
  waiting for transfers between devices  358 us (49%)
  blocking collectives  115 us (16%)
  matrix products  94.1 us (13%)
  starting transfers between devices  66.4 us (9%)
  other arithmetic  37.8 us (5%)
  Pallas kernels  24.2 us (3%)
  between operations  14.8 us (2%)
  local copies, waits for them, and re-layouts  12.2 us (2%)
    ppermute x12, waiting for transfers between devices, swap(): return lax.ppermute(block, 'tensor', [(0, 1), (1, 0)])  147 us
    all_gather x1, waiting for transfers between devices, on_device(): layer_all = lax.all_gather(layer_shard, 'dp', axis=0, tiled=False)  85.6 us
    psum x1, blocking collectives, on_device(): lax.psum((jnp.stack([gain_one_grad, gain_two_grad]), bias_full), ('dp', '...  82.1 us
    all_to_all x7, waiting for transfers between devices, exchange(): return lax.all_to_all(block, 'dp', split_axis=0, concat_axis=0, tiled=True)  66.7 us
    all_to_all x7, starting transfers between devices, exchange(): return lax.all_to_all(block, 'dp', split_axis=0, concat_axis=0, tiled=True)  47.5 us
    dot_general x9, matrix products, dot_nn(): lax.dot_general(left, right, (((1,), (0,)), ((), ())), preferred_element_...  37.9 us
    reduce_scatter x1, waiting for transfers between devices, on_device(): qkv_grad = lax.psum_scatter(qkv_part, 'dp', scatter_dimension=1, tiled=True)  35 us
    all_to_all x1, blocking collectives, exchange(): return lax.all_to_all(block, 'dp', split_axis=0, concat_axis=0, tiled=True)  32.7 us
  transfers between devices with their start and end apart: 23, of which 18 were waited for; matrix products, arithmetic and copies ran while one was open for 15% of the time, Pallas kernels for 3%

profile of v1, /device:TPU:16, one launch (start us, length us, event | category | flops | bytes accessed | tf_op | source)
XLA Modules:
  0.0 722.4 jit_solution(7815646543017094268)
XLA Ops:
  26.2 8.9 %collective-permute-done = bf16[256,1024]{1,0:T(8,128)(2,1)S(1)} collective-permute-done((bf16[256,1024]{1,0:T(8,128)(2,1)S(1)}, bf16[256,1024]{1,0:T(8,128)(2,1)S(1)}, u32[]{:S(2)}, u32[]{:S(2)}) %collective-permute-start) | collective-permute-done | bytes 524320 | tf_op jit(solution)/shard_map/ppermute | solution.py:279
  35.5 85.6 %all-gather.6.cloned.1.call-done = bf16[3328,512]{1,0:T(8,128)(2,1)} async-done(((bf16[208,512]{1,0:T(8,128)(2,1)}), bf16[3328,512]{1,0:T(8,128)(2,1)}) %all-gather.6.cloned.1.call-update) | async-done | bytes 3407888 | tf_op jit(solution)/shard_map/all_gather | solution.py:328
  129.7 11.1 %attend_forward.1 = (bf16[512,512]{1,0:T(8,128)(2,1)}, f32[4,2,512]{2,1,0:T(2,128)}) custom-call(s32[1]{0:T(128)} %dynamic_slice.60.length_ref, bf16[512,512]{1,0:T(8,128)(2,1)} %convolution_convert_fusion.11.query_ref, bf16[512,512]{1,0:T(8,128)(2,1)} %convolution_convert_fusion.10.key_ref, bf16[512,512]{1,0:T(8,128)(2,1)} %convolution_convert_fusion.9.value_ref, ...), custom_call_target="tpu_custom_call" | custom-call | flops 2147483648 | bytes 2097152 | tf_op jit(solution)/shard_map/attend_forward/pallas_call | solution.py:100
  140.8 23.4 %all-gather.4.cloned.1.call-done = bf16[1024,512]{1,0:T(8,128)(2,1)} async-done(((bf16[64,512]{1,0:T(8,128)(2,1)}), bf16[1024,512]{1,0:T(8,128)(2,1)}) %all-gather.4.cloned.1.call-update) | async-done | bytes 1048592 | tf_op jit(solution)/shard_map/all_gather | solution.py:332
  170.4 11.7 %collective-permute-done.1 = bf16[256,1024]{1,0:T(8,128)(2,1)} collective-permute-done((bf16[256,1024]{1,0:T(8,128)(2,1)S(1)}, bf16[256,1024]{1,0:T(8,128)(2,1)}, u32[]{:S(2)}, u32[]{:S(2)}) %collective-permute-start.1) | collective-permute-done | bytes 524320 | tf_op jit(solution)/shard_map/ppermute | solution.py:279
  194.2 14.9 %all-to-all-start.1 = ((bf16[16,72,512]{2,1,0:T(8,128)(2,1)}), bf16[16,72,512]{2,1,0:T(8,128)(2,1)}, u32[]{:S(2)}, u32[]{:S(2)}) async-start(bf16[16,72,512]{2,1,0:T(8,128)(2,1)} %bitcast.76), calls=%async_computation.1 | async-start | bytes 2359296 | tf_op jit(solution)/shard_map/all_to_all | solution.py:300
  219.7 17.5 %all-to-all-done.1 = bf16[16,72,512]{2,1,0:T(8,128)(2,1)} async-done(((bf16[16,72,512]{2,1,0:T(8,128)(2,1)}), bf16[16,72,512]{2,1,0:T(8,128)(2,1)}, u32[]{:S(2)}, u32[]{:S(2)}) %all-to-all-start.1) | async-done | bytes 1179680 | tf_op jit(solution)/shard_map/all_to_all | solution.py:300
  237.2 32.7 %all_to_all.40 = bf16[16,72,512]{2,1,0:T(8,128)(2,1)} all-to-all(bf16[16,72,512]{2,1,0:T(8,128)(2,1)} %bitcast.77), channel_id=1, replica_groups=mesh['dp'=16,'tensor'=2] {'dp'}, dimensions={0} | all-to-all | bytes 2359296 | tf_op jit(solution)/shard_map/all_to_all | solution.py:300
  278.2 27.0 %collective-permute-done.4 = bf16[1152,512]{1,0:T(8,128)(2,1)S(1)} collective-permute-done((bf16[1152,512]{1,0:T(8,128)(2,1)}, bf16[1152,512]{1,0:T(8,128)(2,1)S(1)}, u32[]{:S(2)}, u32[]{:S(2)}) %collective-permute-start.4) | collective-permute-done | bytes 1179680 | tf_op jit(solution)/shard_map/ppermute | solution.py:279
  305.2 13.3 %fusion.67 = f32[1152,2816]{1,0:T(8,128)} fusion(bf16[1024,2816]{1,0:T(8,128)(2,1)} %bitcast.10, bf16[1152,512]{1,0:T(8,128)(2,1)S(1)} %collective-permute-done.4, bf16[1152,512]{1,0:T(8,128)(2,1)} %bitcast.74, pred[]{:T(512)S(6)} %eq.63), kind=kOutput, calls=%fused_computation.121 | convolution fusion | flops 6654394368 | bytes 21102592 | tf_op jit(solution)/shard_map/dot_general | solution.py:26
  318.5 11.3 %collective-permute-done.6 = bf16[1152,512]{1,0:T(8,128)(2,1)} collective-permute-done((bf16[1152,512]{1,0:T(8,128)(2,1)}, bf16[1152,512]{1,0:T(8,128)(2,1)}, u32[]{:S(2)}, u32[]{:S(2)}) %collective-permute-start.6) | collective-permute-done | bytes 1179680 | tf_op jit(solution)/shard_map/ppermute | solution.py:279
  329.8 10.8 %all-to-all-done.3 = bf16[16,64,1408]{2,1,0:T(8,128)(2,1)} async-done(((bf16[16,64,1408]{2,1,0:T(8,128)(2,1)}), bf16[16,64,1408]{2,1,0:T(8,128)(2,1)}, u32[]{:S(2)}, u32[]{:S(2)}) %all-to-all-start.3) | async-done | bytes 2883616 | tf_op jit(solution)/shard_map/all_to_all | solution.py:300
  340.5 14.1 %fusion.6 = (bf16[1152,1408]{1,0:T(8,128)(2,1)}, bf16[1152,1408]{1,0:T(8,128)(2,1)}, bf16[1152,1408]{1,0:T(8,128)(2,1)S(1)}) fusion(f32[1152,2816]{1,0:T(8,128)} %fusion.67, bf16[1024,1408]{1,0:T(8,128)(2,1)} %bitcast.13, bf16[1152,512]{1,0:T(8,128)(2,1)} %collective-permute-done.6, bf16[1152,512]{1,0:T(8,128)(2,1)} %bitcast.11, pred[]{:T(512)S(6)} %eq.63), kind=kOutput, calls=%fused_computation.8 | convolution fusion | flops 3373056000 | bytes 27951104 | tf_op jit(solution)/shard_map/dot_general | solution.py:26
  354.6 9.4 %convolution_convert_fusion.1 = bf16[1024,1408]{1,0:T(8,128)(2,1)} fusion(bf16[1152,1408]{1,0:T(8,128)(2,1)S(1)} %get-tuple-element.51, bf16[1152,512]{1,0:T(8,128)(2,1)} %collective-permute-done.6, bf16[1152,512]{1,0:T(8,128)(2,1)} %bitcast.11, pred[]{:T(512)S(6)} %eq.63), kind=kOutput, calls=%fused_computation.18 | convolution fusion | flops 3333947392 | bytes 8486913 | tf_op jit(solution)/shard_map/dot_general | solution.py:32
  368.7 10.7 %fusion.8 = f32[1152,1024]{1,0:T(8,128)S(1)} fusion(bf16[1024,2816]{1,0:T(8,128)(2,1)} %bitcast.10, bf16[1152,1408]{1,0:T(8,128)(2,1)} %get-tuple-element.50, bf16[1152,1408]{1,0:T(8,128)(2,1)} %get-tuple-element.49), kind=kOutput, calls=%fused_computation.17 | convolution fusion | flops 6656753664 | bytes 16973824 | tf_op jit(solution)/shard_map/dot_general | solution.py:20
  381.4 26.4 %collective-permute-done.7 = bf16[1152,512]{1,0:T(8,128)(2,1)S(1)} collective-permute-done((bf16[1152,512]{1,0:T(8,128)(2,1)S(1)}, bf16[1152,512]{1,0:T(8,128)(2,1)S(1)}, u32[]{:S(2)}, u32[]{:S(2)}) %collective-permute-start.7) | collective-permute-done | bytes 1179680 | tf_op jit(solution)/shard_map/ppermute | solution.py:279
  409.2 24.1 %all-to-all-done.4 = bf16[16,64,1408]{2,1,0:T(8,128)(2,1)} async-done(((bf16[16,64,1408]{2,1,0:T(8,128)(2,1)}), bf16[16,64,1408]{2,1,0:T(8,128)(2,1)}, u32[]{:S(2)}, u32[]{:S(2)}) %all-to-all-start.4) | async-done | bytes 2883616 | tf_op jit(solution)/shard_map/all_to_all | solution.py:300
  446.6 26.4 %collective-permute-done.5 = bf16[1152,512]{1,0:T(8,128)(2,1)S(1)} collective-permute-done((bf16[1152,512]{1,0:T(8,128)(2,1)S(1)}, bf16[1152,512]{1,0:T(8,128)(2,1)S(1)}, u32[]{:S(2)}, u32[]{:S(2)}) %collective-permute-start.5) | collective-permute-done | bytes 1179680 | tf_op jit(solution)/shard_map/ppermute | solution.py:279
  480.4 13.8 %convolution_convert_fusion = bf16[1024,2816]{1,0:T(8,128)(2,1)} fusion(bf16[1152,1408]{1,0:T(8,128)(2,1)} %get-tuple-element.50, bf16[1152,1408]{1,0:T(8,128)(2,1)} %get-tuple-element.49, bf16[1152,512]{1,0:T(8,128)(2,1)} %copy-done.32, bf16[1152,512]{1,0:T(8,128)(2,1)} %bitcast.75, pred[]{:T(512)S(6)} %eq.63), kind=kOutput, calls=%fused_computation.14 | convolution fusion | flops 6670254080 | bytes 14614529 | tf_op jit(solution)/shard_map/dot_general | solution.py:32
  494.2 14.3 %all-to-all-done.6 = bf16[16,72,512]{2,1,0:T(8,128)(2,1)} async-done(((bf16[16,72,512]{2,1,0:T(8,128)(2,1)}), bf16[16,72,512]{2,1,0:T(8,128)(2,1)}, u32[]{:S(2)}, u32[]{:S(2)}) %all-to-all-start.6) | async-done | bytes 1179680 | tf_op jit(solution)/shard_map/all_to_all | solution.py:300
  537.8 10.8 %collective-permute-done.10 = bf16[256,1024]{1,0:T(8,128)(2,1)S(1)} collective-permute-done((bf16[256,1024]{1,0:T(8,128)(2,1)S(1)}, bf16[256,1024]{1,0:T(8,128)(2,1)S(1)}, u32[]{:S(2)}, u32[]{:S(2)}) %collective-permute-start.10) | collective-permute-done | bytes 524320 | tf_op jit(solution)/shard_map/ppermute | solution.py:279
  552.2 13.1 %attend_backward.1 = (bf16[512,512]{1,0:T(8,128)(2,1)}, bf16[512,512]{1,0:T(8,128)(2,1)}, bf16[512,512]{1,0:T(8,128)(2,1)}, f32[4,2,1024]{2,1,0:T(2,128)}) custom-call(s32[1]{0:T(128)} %dynamic_slice.60.length_ref, bf16[512,512]{1,0:T(8,128)(2,1)} %convolution_convert_fusion.11.query_ref, bf16[512,512]{1,0:T(8,128)(2,1)} %convolution_convert_fusion.10.key_ref, ...), custom_call_target="tpu_custom_call" | custom-call | flops 5368709120 | bytes 3670016 | tf_op jit(solution)/shard_map/attend_backward/pallas_call | solution.py:201
  583.5 82.1 %all-reduce.1 = (f32[2,1024]{1,0:T(2,128)S(1)}, f32[16,32]{1,0:T(8,128)S(1)}) all-reduce(f32[2,1024]{1,0:T(2,128)S(1)} %pad_maximum_fusion.5, f32[16,32]{1,0:T(8,128)S(1)} %convolution_dynamic-update-slice_fusion), channel_id=1, replica_groups=mesh['dp'=16,'tensor'=2] {'dp','tensor'}, use_global_device_ids=true, to_apply=%region_10.11 | all-reduce | flops 2560 | bytes 20480 | tf_op jit(solution)/shard_map/psum | solution.py:489
  670.1 35.0 %reduce-scatter.3.cloned.1.call-done = bf16[3,64,512]{2,1,0:T(8,128)(2,1)} async-done(((bf16[3,1024,512]{2,1,0:T(8,128)(2,1)}), bf16[3,64,512]{2,1,0:T(8,128)(2,1)}) %reduce-scatter.3.cloned.1.call-update) | async-done | bytes 196624 | tf_op jit(solution)/shard_map/reduce_scatter | solution.py:471
  (189 shorter events, 159.3 us)
Async XLA Ops:
  7.2 113.9 %all-gather.6.cloned.1.call-start = ((), (), s32[]{:S(2)}) async-start(), calls=%async_computation.13 | async-start | bytes 3620864 | tf_op jit(solution)/shard_map/all_gather | solution.py:328
  14.7 179.5 %all-to-all-start = ((bf16[16,64,2816]{2,1,0:T(8,128)(2,1)}), bf16[16,64,2816]{2,1,0:T(8,128)(2,1)}, u32[]{:S(2)}, u32[]{:S(2)}) async-start(bf16[16,64,2816]{2,1,0:T(8,128)(2,1)} %pad_maximum_fusion.1), calls=%async_computation | async-start | bytes 11534336 | tf_op jit(solution)/shard_map/all_to_all | solution.py:300
  21.0 143.2 %all-gather.4.cloned.1.call-start = ((), (), s32[]{:S(2)}) async-start(), calls=%async_computation.10 | async-start | bytes 1114112 | tf_op jit(solution)/shard_map/all_gather | solution.py:332
  21.1 14.0 %collective-permute-start = (bf16[256,1024]{1,0:T(8,128)(2,1)S(1)}, bf16[256,1024]{1,0:T(8,128)(2,1)S(1)}, u32[]{:S(2)}, u32[]{:S(2)}) collective-permute-start(bf16[256,1024]{1,0:T(8,128)(2,1)S(1)} %copy-done.2), channel_id=1, source_target_pairs={{0,1},{1,0},{2,3},{3,2},{4,5},{5,4},{6,7},{7,6},{8,9},{9,8},{10,11... | collective-permute-start | bytes 1572872 | tf_op jit(solution)/shard_map/ppermute | solution.py:279
  25.0 145.3 %copy-start.26 = (pred[512]{0:T(512)(128)(4,1)}, pred[512]{0:T(512)(128)(4,1)S(1)}, u32[]{:S(2)}) copy-start(pred[512]{0:T(512)(128)(4,1)S(1)} %iota_compare_fusion.13) | copy-start | bytes 1540
  167.8 14.3 %collective-permute-start.1 = (bf16[256,1024]{1,0:T(8,128)(2,1)S(1)}, bf16[256,1024]{1,0:T(8,128)(2,1)}, u32[]{:S(2)}, u32[]{:S(2)}) collective-permute-start(bf16[256,1024]{1,0:T(8,128)(2,1)S(1)} %dynamic-slice_convert_fusion.3), channel_id=1, source_target_pairs={{0,1},{1,0},{2,3},{3,2},{4,5},{5,4},{6,7},{7,6},{8,9},{9,8},{10,11... | collective-permute-start | bytes 1572872 | tf_op jit(solution)/shard_map/ppermute | solution.py:279
  184.6 7.7 %collective-permute-start.3 = (bf16[256,512]{1,0:T(8,128)(2,1)S(1)}, bf16[256,512]{1,0:T(8,128)(2,1)S(1)}, u32[]{:S(2)}, u32[]{:S(2)}) collective-permute-start(bf16[256,512]{1,0:T(8,128)(2,1)S(1)} %get-tuple-element.60), channel_id=1, source_target_pairs={{0,1},{1,0},{2,3},{3,2},{4,5},{5,4},{6,7},{7,6},{8,9},{9,8},{10,11... | collective-permute-start | bytes 786440 | tf_op jit(solution)/shard_map/ppermute | solution.py:279
  194.2 43.0 %all-to-all-start.1 = ((bf16[16,72,512]{2,1,0:T(8,128)(2,1)}), bf16[16,72,512]{2,1,0:T(8,128)(2,1)}, u32[]{:S(2)}, u32[]{:S(2)}) async-start(bf16[16,72,512]{2,1,0:T(8,128)(2,1)} %bitcast.76), calls=%async_computation.1 | async-start | bytes 2359296 | tf_op jit(solution)/shard_map/all_to_all | solution.py:300
  209.4 8.4 %collective-permute-start.2 = (bf16[256,512]{1,0:T(8,128)(2,1)S(1)}, bf16[256,512]{1,0:T(8,128)(2,1)S(1)}, u32[]{:S(2)}, u32[]{:S(2)}) collective-permute-start(bf16[256,512]{1,0:T(8,128)(2,1)S(1)} %get-tuple-element.62), channel_id=1, source_target_pairs={{0,1},{1,0},{2,3},{3,2},{4,5},{5,4},{6,7},{7,6},{8,9},{9,8},{10,11... | collective-permute-start | bytes 786440 | tf_op jit(solution)/shard_map/ppermute | solution.py:279
  269.9 70.6 %all-to-all-start.3 = ((bf16[16,64,1408]{2,1,0:T(8,128)(2,1)}), bf16[16,64,1408]{2,1,0:T(8,128)(2,1)}, u32[]{:S(2)}, u32[]{:S(2)}) async-start(bf16[16,64,1408]{2,1,0:T(8,128)(2,1)} %param.25), calls=%async_computation.3 | async-start | bytes 5767168 | tf_op jit(solution)/shard_map/all_to_all | solution.py:300
  276.1 29.1 %collective-permute-start.4 = (bf16[1152,512]{1,0:T(8,128)(2,1)}, bf16[1152,512]{1,0:T(8,128)(2,1)S(1)}, u32[]{:S(2)}, u32[]{:S(2)}) collective-permute-start(bf16[1152,512]{1,0:T(8,128)(2,1)} %bitcast.73), channel_id=1, source_target_pairs={{0,1},{1,0},{2,3},{3,2},{4,5},{5,4},{6,7},{7,6},{8,9},{9,8},{10,11... | collective-permute-start | bytes 3538952 | tf_op jit(solution)/shard_map/ppermute | solution.py:279
  277.8 52.0 %collective-permute-start.6 = (bf16[1152,512]{1,0:T(8,128)(2,1)}, bf16[1152,512]{1,0:T(8,128)(2,1)}, u32[]{:S(2)}, u32[]{:S(2)}) collective-permute-start(bf16[1152,512]{1,0:T(8,128)(2,1)} %bitcast.11), channel_id=1, source_target_pairs={{0,1},{1,0},{2,3},{3,2},{4,5},{5,4},{6,7},{7,6},{8,9},{9,8},{10,11... | collective-permute-start | bytes 3538952 | tf_op jit(solution)/shard_map/ppermute | solution.py:279
  364.0 69.3 %all-to-all-start.4 = ((bf16[16,64,1408]{2,1,0:T(8,128)(2,1)}), bf16[16,64,1408]{2,1,0:T(8,128)(2,1)}, u32[]{:S(2)}, u32[]{:S(2)}) async-start(bf16[16,64,1408]{2,1,0:T(8,128)(2,1)} %bitcast.72), calls=%async_computation.4 | async-start | bytes 5767168 | tf_op jit(solution)/shard_map/all_to_all | solution.py:300
  379.7 28.1 %collective-permute-start.7 = (bf16[1152,512]{1,0:T(8,128)(2,1)S(1)}, bf16[1152,512]{1,0:T(8,128)(2,1)S(1)}, u32[]{:S(2)}, u32[]{:S(2)}) collective-permute-start(bf16[1152,512]{1,0:T(8,128)(2,1)S(1)} %dynamic-slice_convert_fusion), channel_id=1, source_target_pairs={{0,1},{1,0},{2,3},{3,2},{4,5},{5,4},{6,7},{7,6},{8,9},{9,8},{10,11... | collective-permute-start | bytes 3538952 | tf_op jit(solution)/shard_map/ppermute | solution.py:279
  433.3 41.1 %all-to-all-start.5 = ((bf16[16,72,512]{2,1,0:T(8,128)(2,1)}), bf16[16,72,512]{2,1,0:T(8,128)(2,1)}, u32[]{:S(2)}, u32[]{:S(2)}) async-start(bf16[16,72,512]{2,1,0:T(8,128)(2,1)} %bitcast.15), calls=%async_computation.5 | async-start | bytes 2359296 | tf_op jit(solution)/shard_map/all_to_all | solution.py:300
  444.9 28.1 %collective-permute-start.5 = (bf16[1152,512]{1,0:T(8,128)(2,1)S(1)}, bf16[1152,512]{1,0:T(8,128)(2,1)S(1)}, u32[]{:S(2)}, u32[]{:S(2)}) collective-permute-start(bf16[1152,512]{1,0:T(8,128)(2,1)S(1)} %dynamic-slice_convert_fusion.1), channel_id=1, source_target_pairs={{0,1},{1,0},{2,3},{3,2},{4,5},{5,4},{6,7},{7,6},{8,9},{9,8},{10,11... | collective-permute-start | bytes 3538952 | tf_op jit(solution)/shard_map/ppermute | solution.py:279
  474.4 34.1 %all-to-all-start.6 = ((bf16[16,72,512]{2,1,0:T(8,128)(2,1)}), bf16[16,72,512]{2,1,0:T(8,128)(2,1)}, u32[]{:S(2)}, u32[]{:S(2)}) async-start(bf16[16,72,512]{2,1,0:T(8,128)(2,1)} %bitcast.14), calls=%async_computation.6 | async-start | bytes 2359296 | tf_op jit(solution)/shard_map/all_to_all | solution.py:300
  508.5 198.3 %all-to-all-start.7 = ((bf16[16,64,2816]{2,1,0:T(8,128)(2,1)}), bf16[16,64,2816]{2,1,0:T(8,128)(2,1)}, u32[]{:S(2)}, u32[]{:S(2)}) async-start(bf16[16,64,2816]{2,1,0:T(8,128)(2,1)} %bitcast.63), calls=%async_computation.9 | async-start | bytes 11534336 | tf_op jit(solution)/shard_map/all_to_all | solution.py:300
  513.2 155.4 %reduce-scatter.5.cloned.1.call-start = ((), (), s32[]{:S(2)}) async-start(), calls=%async_computation.12 | async-start | bytes 1114112 | tf_op jit(solution)/shard_map/reduce_scatter | solution.py:453
  515.4 8.4 %collective-permute-start.9 = (bf16[256,512]{1,0:T(8,128)(2,1)S(1)}, bf16[256,512]{1,0:T(8,128)(2,1)S(1)}, u32[]{:S(2)}, u32[]{:S(2)}) collective-permute-start(bf16[256,512]{1,0:T(8,128)(2,1)S(1)} %dynamic-slice_convert_fusion.4), channel_id=1, source_target_pairs={{0,1},{1,0},{2,3},{3,2},{4,5},{5,4},{6,7},{7,6},{8,9},{9,8},{10,11... | collective-permute-start | bytes 786440 | tf_op jit(solution)/shard_map/ppermute | solution.py:279
  526.6 7.7 %collective-permute-start.8 = (bf16[256,512]{1,0:T(8,128)(2,1)S(1)}, bf16[256,512]{1,0:T(8,128)(2,1)S(1)}, u32[]{:S(2)}, u32[]{:S(2)}) collective-permute-start(bf16[256,512]{1,0:T(8,128)(2,1)S(1)} %dynamic-slice_convert_fusion.5), channel_id=1, source_target_pairs={{0,1},{1,0},{2,3},{3,2},{4,5},{5,4},{6,7},{7,6},{8,9},{9,8},{10,11... | collective-permute-start | bytes 786440 | tf_op jit(solution)/shard_map/ppermute | solution.py:279
  536.1 12.4 %collective-permute-start.10 = (bf16[256,1024]{1,0:T(8,128)(2,1)S(1)}, bf16[256,1024]{1,0:T(8,128)(2,1)S(1)}, u32[]{:S(2)}, u32[]{:S(2)}) collective-permute-start(bf16[256,1024]{1,0:T(8,128)(2,1)S(1)} %get-tuple-element.45), channel_id=1, source_target_pairs={{0,1},{1,0},{2,3},{3,2},{4,5},{5,4},{6,7},{7,6},{8,9},{9,8},{10,11... | collective-permute-start | bytes 1572872 | tf_op jit(solution)/shard_map/ppermute | solution.py:279
  550.3 154.8 %reduce-scatter.3.cloned.1.call-start = ((), (), s32[]{:S(2)}) async-start(), calls=%async_computation.11 | async-start | bytes 3342336 | tf_op jit(solution)/shard_map/reduce_scatter | solution.py:471
  581.7 85.1 %collective-permute-start.11 = (bf16[256,1024]{1,0:T(8,128)(2,1)}, bf16[256,1024]{1,0:T(8,128)(2,1)S(1)}, u32[]{:S(2)}, u32[]{:S(2)}) collective-permute-start(bf16[256,1024]{1,0:T(8,128)(2,1)} %dynamic-slice_convert_fusion.2), channel_id=1, source_target_pairs={{0,1},{1,0},{2,3},{3,2},{4,5},{5,4},{6,7},{7,6},{8,9},{9,8},{10,11... | collective-permute-start | bytes 1572872 | tf_op jit(solution)/shard_map/ppermute | solution.py:279
  (34 other events, 340.8 us)
Sparse Core Ops, SparseCore 0:
  10.9 110.1 all-gather.5
  123.3 40.8 all-gather.3
  550.5 83.4 reduce-scatter.4
  638.7 66.4 reduce-scatter.2

commit v2 on v1

--- a/solution.py
+++ b/solution.py
@@ -14,6 +14,7 @@
 LANES = 128
 GELU_SCALE = 0.7978845608028654
 GELU_CUBIC = 0.044715
+GAIN_ROWS = 16
 
 
 def dot_nt(left, right):
@@ -62,10 +63,11 @@
     )
 
 
-def forward_kernel(
-    length_ref, query_ref, key_ref, value_ref, bias_ref, out_ref, total_ref, base_ref
-):
-    seq = query_ref.shape[0]
+def forward_kernel(length_ref, joined_ref, bias_ref, out_ref, total_ref, base_ref):
+    query_ref, key_ref, value_ref = [
+        joined_ref.at[:, i * LANES : (i + 1) * LANES] for i in range(3)
+    ]
+    seq = joined_ref.shape[0]
     cols = min(QUERY_COLS, seq)
     length = length_ref[0]
     values_t = value_ref[...].T
@@ -92,8 +94,9 @@
         out_ref[start : start + cols, :] = joined.T.astype(jnp.bfloat16)
 
 
-def attend_forward(length, queries, keys, values, bias_rows):
-    seq, width = queries.shape
+def attend_forward(length, joined, bias_rows):
+    seq = joined.shape[0]
+    width = joined.shape[1] // 3
     pairs = width // LANES
     heads = LANES // HEAD_DIM
     column = pl.BlockSpec((seq, LANES), lambda i: (0, i))
@@ -102,9 +105,7 @@
         grid=(pairs,),
         in_specs=[
             pl.BlockSpec(memory_space=pltpu.SMEM),
-            column,
-            column,
-            column,
+            pl.BlockSpec((seq, 3 * LANES), lambda i: (0, i)),
             pl.BlockSpec((1, heads, 2 * seq), lambda i: (i, 0, 0)),
         ],
         out_specs=[column, pl.BlockSpec((1, heads, seq), lambda i: (i, 0, 0))],
@@ -119,7 +120,7 @@
             bytes_accessed=8 * seq * width,
         ),
         name="attend_forward",
-    )(length, queries, keys, values, bias_rows)
+    )(length, joined, bias_rows)
 
 
 def diagonal_sums(acc_ref, seq):
@@ -135,20 +136,19 @@
 
 def backward_kernel(
     length_ref,
-    query_ref,
-    key_ref,
-    value_ref,
+    joined_ref,
     grad_ref,
     total_ref,
     bias_ref,
-    query_grad_ref,
-    key_grad_ref,
-    value_grad_ref,
+    joined_grad_ref,
     bias_grad_ref,
     base_ref,
     acc_ref,
 ):
-    seq = query_ref.shape[0]
+    query_ref, key_ref, value_ref = [
+        joined_ref.at[:, i * LANES : (i + 1) * LANES] for i in range(3)
+    ]
+    seq = joined_ref.shape[0]
     cols = min(QUERY_COLS, seq)
     length = length_ref[0]
     keys = key_ref[...]
@@ -180,41 +180,37 @@
                     first : first + LANES
                 ].astype(jnp.float32)
         bias_grad_ref[0, head : head + 1, :] = diagonal_sums(acc_ref, seq)
-    key_grad_ref[...] = (key_acc * SCORE_SCALE).astype(jnp.bfloat16)
-    value_grad_ref[...] = value_acc.astype(jnp.bfloat16)
+    joined_grad_ref[:, LANES : 2 * LANES] = (key_acc * SCORE_SCALE).astype(jnp.bfloat16)
+    joined_grad_ref[:, 2 * LANES :] = value_acc.astype(jnp.bfloat16)
     for start in starts:
         joined = jnp.concatenate(
             [query_parts[start, head] for head in range(LANES // HEAD_DIM)], axis=0
         )
-        query_grad_ref[start : start + cols, :] = (joined * SCORE_SCALE).T.astype(
+        joined_grad_ref[start : start + cols, :LANES] = (joined * SCORE_SCALE).T.astype(
             jnp.bfloat16
         )
 
 
-def attend_backward(length, queries, keys, values, attended_grad, totals, bias_rows):
-    seq, width = queries.shape
+def attend_backward(length, joined, attended_grad, totals, bias_rows):
+    seq, width = attended_grad.shape
     pairs = width // LANES
     heads = LANES // HEAD_DIM
     column = pl.BlockSpec((seq, LANES), lambda i: (0, i))
+    triple = pl.BlockSpec((seq, 3 * LANES), lambda i: (0, i))
     vector = pl.BlockSpec((1, heads, 2 * seq), lambda i: (i, 0, 0))
-    grad_shape = jax.ShapeDtypeStruct((seq, width), jnp.bfloat16)
     return pl.pallas_call(
         backward_kernel,
         grid=(pairs,),
         in_specs=[
             pl.BlockSpec(memory_space=pltpu.SMEM),
-            column,
-            column,
-            column,
+            triple,
             column,
             pl.BlockSpec((1, heads, seq), lambda i: (i, 0, 0)),
             vector,
         ],
-        out_specs=[column, column, column, vector],
+        out_specs=[triple, vector],
         out_shape=[
-            grad_shape,
-            grad_shape,
-            grad_shape,
+            jax.ShapeDtypeStruct((seq, 3 * width), jnp.bfloat16),
             jax.ShapeDtypeStruct((pairs, heads, 2 * seq), jnp.float32),
         ],
         scratch_shapes=[
@@ -227,7 +223,56 @@
             bytes_accessed=14 * seq * width,
         ),
         name="attend_backward",
-    )(length, queries, keys, values, attended_grad, totals, bias_rows)
+    )(length, joined, attended_grad, totals, bias_rows)
+
+
+def assemble_kernel(place_ref, *refs):
+    parts, (weight_ref, out_ref, gain_ref) = refs[:-3], refs[-3:]
+    rows = weight_ref.shape[0]
+    pairs = weight_ref.shape[1] // (3 * LANES)
+    wanted = pl.program_id(1) ^ place_ref[1]
+    for index, part_ref in enumerate(parts):
+
+        @pl.when(wanted == index)
+        def _(part_ref=part_ref):
+            for kind in range(3):
+                for pair in range(pairs):
+                    first = (3 * pair + kind) * LANES
+                    weight_ref[:, first : first + LANES] = part_ref[
+                        0, kind * rows : (kind + 1) * rows, pair * LANES : (pair + 1) * LANES
+                    ]
+            out_ref[...] = part_ref[0, 3 * rows : 4 * rows, :]
+            gain_ref[0] = part_ref[0, 4 * rows :, :]
+
+
+def assemble(place, parts):
+    outer, block_rows, cols = parts[0].shape
+    inner = len(parts)
+    rows = (block_rows - GAIN_ROWS) // 4
+    block = pl.BlockSpec(
+        (1, block_rows, cols), lambda i, j, place_ref: (i ^ place_ref[0], 0, 0)
+    )
+    return pl.pallas_call(
+        assemble_kernel,
+        grid_spec=pltpu.PrefetchScalarGridSpec(
+            num_scalar_prefetch=1,
+            grid=(outer, inner),
+            in_specs=[block] * inner,
+            out_specs=[
+                pl.BlockSpec((rows, 3 * cols), lambda i, j, place_ref: (i * inner + j, 0)),
+                pl.BlockSpec((rows, cols), lambda i, j, place_ref: (i * inner + j, 0)),
+                pl.BlockSpec(
+                    (1, GAIN_ROWS, cols), lambda i, j, place_ref: (i * inner + j, 0, 0)
+                ),
+            ],
+        ),
+        out_shape=[
+            jax.ShapeDtypeStruct((outer * inner * rows, 3 * cols), jnp.bfloat16),
+            jax.ShapeDtypeStruct((outer * inner * rows, cols), jnp.bfloat16),
+            jax.ShapeDtypeStruct((outer * inner, GAIN_ROWS, cols), jnp.bfloat16),
+        ],
+        name="assemble",
+    )(place, *parts)
 
 
 def gelu_parts(gate_pre):
@@ -278,8 +323,8 @@
     def swap(block):
         return lax.ppermute(block, "tensor", [(0, 1), (1, 0)])
 
-    def after(block, *earlier):
-        return lax.optimization_barrier((block, *earlier))[0]
+    def chain(block, earlier):
+        return lax.optimization_barrier((block, earlier))
 
     def ordered(own, other, axis):
         return jnp.where(
@@ -302,15 +347,14 @@
     def home_order(weight):
         return jnp.repeat(weight, group_size, axis=0)
 
-    def fetch(weight, *earlier):
-        arrived = exchange(after(home_order(weight), *earlier))
-        return arrived.reshape(dp_count * shard_rows, weight.shape[2])
-
-    def send_grad(grad, *earlier):
-        return exchange(after(grad.reshape(dp_count, shard_rows, grad.shape[1]), *earlier))
-
-    def route(rows, *earlier):
-        arrived = exchange(after(rows.reshape(dp_count, slot_count, rows.shape[1]), *earlier))
+    def fetch(weight):
+        return exchange(home_order(weight)).reshape(dp_count * shard_rows, weight.shape[2])
+
+    def send_grad(grad):
+        return exchange(grad.reshape(dp_count, shard_rows, grad.shape[1]))
+
+    def route(rows):
+        arrived = exchange(rows.reshape(dp_count, slot_count, rows.shape[1]))
         return arrived.reshape(total_slots, rows.shape[1])
 
     def regroup(arrived):
@@ -321,17 +365,11 @@
             axis=1,
         )
 
-    gain_pad = jnp.pad(norm_gains, ((0, 14), (0, head_cols - shard_rows)))
+    gain_pad = jnp.pad(norm_gains, ((0, GAIN_ROWS - 2), (0, head_cols - shard_rows)))
     layer_shard = jnp.concatenate(
-        [qkv_weight.reshape(3 * shard_rows, head_cols), gain_pad], axis=0
-    )
-    layer_all = lax.all_gather(layer_shard, "dp", axis=0, tiled=False)
-    tokens_other = swap(tokens)
-    mix_grad = (own_valid * cotangent.astype(jnp.float32)).astype(jnp.bfloat16)
-    mix_other = swap(other_part(mix_grad, 1))
-    out_all = lax.all_gather(out_weight, "dp", axis=0, tiled=True)
-    gate_up_all = fetch(jnp.concatenate([gate_weight, up_weight], axis=2))
-
+        [qkv_weight.reshape(3 * shard_rows, head_cols), out_weight, gain_pad], axis=0
+    )
+    pairs = head_cols // LANES
     pair_expert = routes.reshape(-1)
     pair_valid = jnp.repeat(group_valid, 2)
     chosen = (
@@ -357,11 +395,41 @@
         jnp.where(second_hit, gate_values[:, 1][None, :], no_gate),
     )
 
+    tokens_other = swap(tokens)
+    mix_grad = lax.optimization_barrier(
+        (own_valid * cotangent.astype(jnp.float32)).astype(jnp.bfloat16)
+    )
+    mix_other = swap(other_part(mix_grad, 1))
     out_grad_cols = dot_nn(
         pick_gate, ordered(own_part(mix_grad, 1), mix_other, 0)
     ).astype(jnp.bfloat16)
-    slot_grad_half = route(out_grad_cols, gate_up_all)
-    slot_grad = ordered(slot_grad_half, swap(slot_grad_half), 1)
+    residual, out_grad_cols = chain(tokens, out_grad_cols)
+    gate_up = jnp.concatenate([gate_weight, up_weight], axis=2)
+    if dp_count == 16:
+        across = [
+            lax.ppermute(layer_shard, "dp", [(i, i ^ (4 * k)) for i in range(16)])
+            for k in range(1, 4)
+        ]
+        gate_up, across = chain(gate_up, across)
+        near = jnp.stack([layer_shard, *across])
+        side = lax.ppermute(near, "dp", [(i, i ^ 2) for i in range(16)])
+        core = [(i, i ^ 1) for i in range(16)]
+        parts = [near, lax.ppermute(near, "dp", core), side, lax.ppermute(side, "dp", core)]
+        place = jnp.stack([dp_index // 4, dp_index % 4])
+        projection, out_all, gain_rows = assemble(place, parts)
+    else:
+        layer_all = lax.all_gather(layer_shard, "dp", axis=0, tiled=False)
+        gate_up, layer_all = chain(gate_up, layer_all)
+        projection = (
+            layer_all[:, : 3 * shard_rows]
+            .reshape(dp_count, 3, shard_rows, pairs, LANES)
+            .transpose(0, 2, 3, 1, 4)
+            .reshape(width, 3 * head_cols)
+        )
+        out_all = layer_all[:, 3 * shard_rows : 4 * shard_rows].reshape(width, head_cols)
+        gain_rows = layer_all[:, 4 * shard_rows :]
+    out_grad_cols, gate_up_all = chain(out_grad_cols, fetch(gate_up))
+    slot_grad_half = route(out_grad_cols)
 
     distance = jnp.arange(2 * seq, dtype=jnp.int32)
     table_reversed = jnp.concatenate(
@@ -373,41 +441,40 @@
     bias_rows = jnp.dot(rel_bias.astype(jnp.float32), hot, precision=HIGHEST).reshape(
         head_count // 2, 2, 2 * seq
     )
-    gains_all = jnp.transpose(
-        layer_all[:, 3 * shard_rows : 3 * shard_rows + 2, :shard_rows], (1, 0, 2)
-    ).reshape(2, width)
+    gains_all = jnp.transpose(gain_rows[:, :2, :shard_rows], (1, 0, 2)).reshape(2, width)
     gain_one = gains_all[0].astype(jnp.float32)
     gain_two = gains_all[1].astype(jnp.float32)
-    projections = [
-        layer_all[:, i * shard_rows : (i + 1) * shard_rows].reshape(width, head_cols)
-        for i in range(3)
-    ]
     inputs_all = ordered(tokens, tokens_other, 0).astype(jnp.float32)
     scale_all = lax.rsqrt(jnp.mean(inputs_all * inputs_all, axis=-1, keepdims=True) + EPSILON)
     norm_one_all = (inputs_all * scale_all * gain_one).astype(jnp.bfloat16)
-    queries, keys, values = [
-        dot_nn(norm_one_all, weight).astype(jnp.bfloat16) for weight in projections
-    ]
-    attended, totals = attend_forward(length_row, queries, keys, values, bias_rows)
+    joined = dot_nn(norm_one_all, projection).astype(jnp.bfloat16)
+    attended, totals = attend_forward(length_row, joined, bias_rows)
     branch = dot_nt(attended, out_all)
     branch_other = swap(other_part(branch, 0).astype(jnp.bfloat16))
-    inputs = tokens.astype(jnp.float32)
+    inputs = residual.astype(jnp.float32)
     mid = inputs + own_valid * (own_part(branch, 0) + branch_other.astype(jnp.float32))
     mid_scale = lax.rsqrt(jnp.mean(mid * mid, axis=-1, keepdims=True) + EPSILON)
     norm_two = (mid * mid_scale * gain_two).astype(jnp.bfloat16)
-    norm_two_cols = ordered(own_part(norm_two, 1), swap(other_part(norm_two, 1)), 0)
-    expert_half = route(
+    norm_two_away, gate_up_all = chain(other_part(norm_two, 1), gate_up_all)
+    norm_two_cols = ordered(own_part(norm_two, 1), swap(norm_two_away), 0)
+    expert_rows, slot_grad_half = chain(
         dot_nn(pick, norm_two_cols).astype(jnp.bfloat16), slot_grad_half
     )
-    down_all = fetch(down_weight, expert_half)
+    slot_grad_other = swap(slot_grad_half)
+    down_late, (expert_half, slot_grad_other) = chain(
+        down_weight, (route(expert_rows), slot_grad_other)
+    )
+    down_all = fetch(down_late)
     expert_in = ordered(expert_half, swap(expert_half), 1)
+    slot_grad = ordered(slot_grad_half, slot_grad_other, 1)
 
     pre = dot_nn(expert_in, gate_up_all)
     gate_pre = pre[:, :hidden_cols]
     up_pre = pre[:, hidden_cols:]
     gelu, slope = gelu_parts(gate_pre)
-    hidden = (gelu * up_pre).astype(jnp.bfloat16)
-    down_back = send_grad(dot_tn(slot_grad, hidden).astype(jnp.bfloat16), down_all)
+    hidden = lax.optimization_barrier((gelu * up_pre).astype(jnp.bfloat16))
+    down_grad, down_all = chain(dot_tn(slot_grad, hidden).astype(jnp.bfloat16), down_all)
+    down_back = send_grad(down_grad)
     hidden_grad = dot_nn(slot_grad, down_all)
     pre_grad = jnp.concatenate(
         [
@@ -417,18 +484,25 @@
         axis=1,
     )
     slot_back_part = dot_nt(pre_grad, gate_up_all)
+    slot_back_away = other_part(slot_back_part, 1).astype(jnp.bfloat16)
+    hidden_late, slot_back_away = chain(hidden, slot_back_away)
+    slot_back_other = swap(slot_back_away)
+    expert_out_part = dot_nt(hidden_late, down_all)
+    expert_out_away, slot_back_other = chain(
+        other_part(expert_out_part, 1).astype(jnp.bfloat16), slot_back_other
+    )
     slot_back_half = (
-        own_part(slot_back_part, 1)
-        + swap(other_part(slot_back_part, 1).astype(jnp.bfloat16)).astype(jnp.float32)
+        own_part(slot_back_part, 1) + slot_back_other.astype(jnp.float32)
     ).astype(jnp.bfloat16)
-    slot_back = route(slot_back_half, down_back)
-    expert_out_part = dot_nt(hidden, down_all)
     expert_out_half = (
-        own_part(expert_out_part, 1)
-        + swap(other_part(expert_out_part, 1).astype(jnp.bfloat16)).astype(jnp.float32)
+        own_part(expert_out_part, 1) + swap(expert_out_away).astype(jnp.float32)
     ).astype(jnp.bfloat16)
-    returned = route(expert_out_half, slot_back)
-    gate_up_back = send_grad(dot_tn(expert_in, pre_grad).astype(jnp.bfloat16), returned)
+    slot_back_half, down_back = chain(slot_back_half, down_back)
+    expert_out_half, slot_back = chain(expert_out_half, route(slot_back_half))
+    gate_up_grad, returned = chain(
+        dot_tn(expert_in, pre_grad).astype(jnp.bfloat16), route(expert_out_half)
+    )
+    gate_up_back = send_grad(gate_up_grad)
 
     mix_cols = dot_tn(pick_gate, returned)
     mix_own = ordered(
@@ -449,26 +523,51 @@
     branch_grad_all = ordered(branch_grad, swap(branch_grad), 0)
 
     attended_grad = dot_nn(branch_grad_all, out_all).astype(jnp.bfloat16)
-    out_part = dot_tn(branch_grad_all, attended).astype(jnp.bfloat16)
-    out_grad = lax.psum_scatter(out_part, "dp", scatter_dimension=0, tiled=True)
-    query_grad, key_grad, value_grad, bias_sums = attend_backward(
-        length_row, queries, keys, values, attended_grad, totals, bias_rows
+    joined_grad, bias_sums = attend_backward(
+        length_row, joined, attended_grad, totals, bias_rows
     )
     bias_grad = jnp.dot(
         bias_sums.reshape(head_count, 2 * seq), hot.T, precision=HIGHEST
     )
-    norm_one_part = (
-        dot_nt(query_grad, projections[0])
-        + dot_nt(key_grad, projections[1])
-        + dot_nt(value_grad, projections[2])
-    )
-    qkv_part = jnp.stack(
+    norm_one_part = dot_nt(joined_grad, projection)
+    layer_part = jnp.concatenate(
         [
-            dot_tn(norm_one_all, grad).astype(jnp.bfloat16)
-            for grad in (query_grad, key_grad, value_grad)
-        ]
-    )
-    qkv_grad = lax.psum_scatter(qkv_part, "dp", scatter_dimension=1, tiled=True)
+            dot_tn(norm_one_all, joined_grad).astype(jnp.bfloat16),
+            dot_tn(branch_grad_all, attended).astype(jnp.bfloat16),
+        ],
+        axis=1,
+    )
+    if dp_count == 16:
+        blocks = layer_part.reshape(dp_count, shard_rows, layer_part.shape[1])
+        for step in (1, 2):
+            pieces = blocks.reshape(-1, 2, shard_rows, blocks.shape[2])
+            bit = (dp_index // step) % 2
+            away = lax.dynamic_index_in_dim(pieces, 1 - bit, 1, keepdims=False)
+            stay = lax.dynamic_index_in_dim(pieces, bit, 1, keepdims=False)
+            arrived = lax.ppermute(away, "dp", [(i, i ^ step) for i in range(dp_count)])
+            blocks = (stay.astype(jnp.float32) + arrived.astype(jnp.float32)).astype(
+                jnp.bfloat16
+            )
+        place_out = dp_index // 4
+        layer_grad = lax.dynamic_index_in_dim(blocks, place_out, 0, keepdims=False).astype(
+            jnp.float32
+        )
+        for k in range(1, 4):
+            away = lax.dynamic_index_in_dim(blocks, place_out ^ k, 0, keepdims=False)
+            layer_grad = layer_grad + lax.ppermute(
+                away, "dp", [(i, i ^ (4 * k)) for i in range(dp_count)]
+            ).astype(jnp.float32)
+    else:
+        layer_grad = lax.psum_scatter(
+            layer_part, "dp", scatter_dimension=0, tiled=True
+        ).astype(jnp.float32)
+    qkv_grad = (
+        layer_grad[:, : 3 * head_cols]
+        .reshape(shard_rows, pairs, 3, LANES)
+        .transpose(2, 0, 1, 3)
+        .reshape(3, shard_rows, head_cols)
+    )
+    out_grad = layer_grad[:, 3 * head_cols :]
     gain_one_grad = jnp.sum(norm_one_part * (inputs_all * scale_all), axis=0)
     norm_one_grad = own_part(norm_one_part, 0) + swap(
         other_part(norm_one_part, 0).astype(jnp.bfloat16)
@@ -480,22 +579,27 @@
         inner - unit * jnp.mean(inner * unit, axis=-1, keepdims=True)
     )
 
-    bias_full = lax.dynamic_update_slice_in_dim(
-        jnp.zeros((head_count * tensor_count, bucket_count), jnp.float32),
-        bias_grad,
-        tensor_index * head_count,
-        0,
-    )
-    gain_sums, bias_sums = lax.psum(
-        (jnp.stack([gain_one_grad, gain_two_grad]), bias_full), ("dp", "tensor")
-    )
+    gain_size = 2 * width
+    gain_part = jnp.concatenate([gain_one_grad, gain_two_grad]).reshape(-1, LANES)
+    small = jnp.concatenate(
+        [gain_part + swap(gain_part), bias_grad.reshape(-1, LANES)], axis=0
+    )
+    step = 1
+    while step < dp_count:
+        last = min(4, dp_count // step) if step >= 4 else 2
+        small = small + sum(
+            lax.ppermute(small, "dp", [(i, i ^ (k * step)) for i in range(dp_count)])
+            for k in range(1, last)
+        )
+        step *= last
+    gain_sums = small.reshape(-1)[:gain_size].reshape(2, width)
+    bias_out = small.reshape(-1)[gain_size:].reshape(head_count, bucket_count)
     gains_grad = lax.dynamic_slice_in_dim(gain_sums, dp_index * shard_rows, shard_rows, 1)
-    bias_out = lax.dynamic_slice_in_dim(bias_sums, tensor_index * head_count, head_count, 0)
     return (
         mixed,
         input_grad,
-        qkv_grad.astype(jnp.float32),
-        out_grad.astype(jnp.float32),
+        qkv_grad,
+        out_grad,
         gains_grad,
         bias_out,
         regroup(gate_up_back[:, :, :hidden_cols]),

time: 734 us -> 629 us (0.86)
  blocking collectives: 115 us -> 0 us
  local copies, waits for them, and re-layouts: 12.2 us -> 26.6 us
  starting transfers between devices: 66.4 us -> 80.4 us
  between operations: 14.8 us -> 1.57 us
  waiting for transfers between devices: 358 us -> 347 us
  Pallas kernels: 24.2 us -> 34.4 us
    ppermute x0 -> x16, waiting for transfers between devices: none -> 136 us  [the longest x1 56.2 us: on_device(): side = lax.ppermute(near, 'dp', [(i, i ^ 2) for i in range(16)])]
    all_gather x2 -> x0, waiting for transfers between devices: 109 us -> none  [the longest x1 85.6 us: on_device(): layer_all = lax.all_gather(layer_shard, 'dp', axis=0, tiled=False)]
    psum x1 -> x0, blocking collectives: 82.1 us -> none  [on_device(): lax.psum((jnp.stack([gain_one_grad, gain_two_grad]), bias_full), ('dp', '...]
    reduce_scatter x2 -> x0, waiting for transfers between devices: 35 us -> none  [the longest x1 35 us: on_device(): qkv_grad = lax.psum_scatter(qkv_part, 'dp', scatter_dimension=1, tiled=True)]
    all_to_all x1 -> x0, blocking collectives: 32.7 us -> none  [exchange(): return lax.all_to_all(block, 'dp', split_axis=0, concat_axis=0, tiled=True)]
    ppermute x12 -> x13, waiting for transfers between devices: 147 us -> 129 us  [swap(): return lax.ppermute(block, 'tensor', [(0, 1), (1, 0)])]
    all_to_all x7 -> x8, waiting for transfers between devices: 66.7 us -> 82.4 us  [exchange(): return lax.all_to_all(block, 'dp', split_axis=0, concat_axis=0, tiled=True)]
    ppermute x0 -> x16, starting transfers between devices: none -> 14.4 us  [the longest x5 5.04 us: on_device(): lax.ppermute(small, 'dp', [(i, i ^ k * step) for i in range(dp_count)])]
  transfers between devices with their start and end apart: 23 -> 37, of which waited for: 18 -> 27; matrix products, arithmetic and copies ran while one was open for 15% -> 22% of each run, Pallas kernels for 3% -> 6%
where the time goes in v2:
time: 629 us; the launch traced here: 624 us
  waiting for transfers between devices  347 us (55%)
  matrix products  89.7 us (14%)
  starting transfers between devices  80.4 us (13%)
  other arithmetic  44.5 us (7%)
  Pallas kernels  34.4 us (5%)
  local copies, waits for them, and re-layouts  26.6 us (4%)
    ppermute x13, waiting for transfers between devices, swap(): return lax.ppermute(block, 'tensor', [(0, 1), (1, 0)])  129 us
    all_to_all x8, waiting for transfers between devices, exchange(): return lax.all_to_all(block, 'dp', split_axis=0, concat_axis=0, tiled=True)  82.4 us
    ppermute x1, waiting for transfers between devices, on_device(): side = lax.ppermute(near, 'dp', [(i, i ^ 2) for i in range(16)])  56.2 us
    all_to_all x8, starting transfers between devices, exchange(): return lax.all_to_all(block, 'dp', split_axis=0, concat_axis=0, tiled=True)  53.9 us
    ppermute x5, waiting for transfers between devices, on_device(): lax.ppermute(small, 'dp', [(i, i ^ k * step) for i in range(dp_count)])  40 us
    dot_general x7, matrix products, dot_nn(): lax.dot_general(left, right, (((1,), (0,)), ((), ())), preferred_element_...  35.9 us
    dot_general x6, matrix products, dot_tn(): lax.dot_general(left, right, (((0,), (0,)), ((), ())), preferred_element_...  32.1 us
    dot_general x4, matrix products, dot_nt(): lax.dot_general(left, right, (((1,), (1,)), ((), ())), preferred_element_...  21.5 us
  transfers between devices with their start and end apart: 37, of which 27 were waited for; matrix products, arithmetic and copies ran while one was open for 22% of the time, Pallas kernels for 6%

profile of v2, /device:TPU:16, one launch (start us, length us, event | category | flops | bytes accessed | tf_op | source)
XLA Modules:
  0.0 624.4 jit_solution(12788461955421247)
XLA Ops:
  13.9 8.8 %collective-permute-done.3 = bf16[272,512]{1,0:T(8,128)(2,1)S(1)} collective-permute-done((bf16[272,512]{1,0:T(8,128)(2,1)S(1)}, bf16[272,512]{1,0:T(8,128)(2,1)S(1)}, u32[]{:S(2)}, u32[]{:S(2)}) %collective-permute-start.3) | collective-permute-done | bytes 278560 | tf_op jit(solution)/shard_map/ppermute | solution.py:410
  44.6 56.2 %collective-permute-done.6.refs_2_ = bf16[4,272,512]{2,1,0:T(8,128)(2,1)} collective-permute-done((bf16[4,272,512]{2,1,0:T(8,128)(2,1)S(1)}, bf16[4,272,512]{2,1,0:T(8,128)(2,1)}, u32[]{:S(2)}, u32[]{:S(2)}) %collective-permute-start.6) | collective-permute-done | bytes 1114144 | tf_op jit(solution)/shard_map/ppermute | solution.py:415
  107.2 10.2 %assemble.1 = (bf16[1024,1536]{1,0:T(8,128)(2,1)}, bf16[1024,512]{1,0:T(8,128)(2,1)}, bf16[16,16,512]{2,1,0:T(8,128)(2,1)}) custom-call(s32[2]{0:T(128)} %pad_add_fusion.1.place_ref, bf16[4,272,512]{2,1,0:T(8,128)(2,1)} %copy-done.6, bf16[4,272,512]{2,1,0:T(8,128)(2,1)} %collective-permute-done.5.refs_1_, ...), custom_call_target="tpu_custom_call" | custom-call | tf_op jit(solution)/shard_map/assemble/pallas_call | solution.py:255
  123.7 11.0 %attend_forward.1 = (bf16[512,512]{1,0:T(8,128)(2,1)}, f32[4,2,512]{2,1,0:T(2,128)}) custom-call(s32[1]{0:T(128)} %dynamic_slice.84.length_ref, bf16[512,1536]{1,0:T(8,128)(2,1)} %convolution_convert_fusion.4.joined_ref, f32[4,2,1024]{2,1,0:T(2,128)} %reshape.179.bias_ref), custom_call_target="tpu_custom_call" | custom-call | flops 2147483648 | bytes 2097152 | tf_op jit(solution)/shard_map/attend_forward/pallas_call | solution.py:103
  134.7 26.2 %all-to-all-done = bf16[16,64,2816]{2,1,0:T(8,128)(2,1)} async-done(((bf16[16,64,2816]{2,1,0:T(8,128)(2,1)}), bf16[16,64,2816]{2,1,0:T(8,128)(2,1)}, u32[]{:S(2)}, u32[]{:S(2)}) %all-to-all-start) | async-done | bytes 5767200 | tf_op jit(solution)/shard_map/all_to_all | solution.py:345
  169.4 12.4 %collective-permute-done.8 = bf16[256,1024]{1,0:T(8,128)(2,1)S(1)} collective-permute-done((bf16[256,1024]{1,0:T(8,128)(2,1)S(1)}, bf16[256,1024]{1,0:T(8,128)(2,1)S(1)}, u32[]{:S(2)}, u32[]{:S(2)}) %collective-permute-start.8) | collective-permute-done | bytes 524320 | tf_op jit(solution)/shard_map/ppermute | solution.py:324
  200.8 26.9 %collective-permute-done.10 = bf16[1152,512]{1,0:T(8,128)(2,1)} collective-permute-done((bf16[1152,512]{1,0:T(8,128)(2,1)}, bf16[1152,512]{1,0:T(8,128)(2,1)}, u32[]{:S(2)}, u32[]{:S(2)}) %collective-permute-start.10) | collective-permute-done | bytes 1179680 | tf_op jit(solution)/shard_map/ppermute | solution.py:324
  229.1 17.8 %all-to-all-start.3 = ((bf16[16,64,1408]{2,1,0:T(8,128)(2,1)}), bf16[16,64,1408]{2,1,0:T(8,128)(2,1)}, u32[]{:S(2)}, u32[]{:S(2)}) async-start(bf16[16,64,1408]{2,1,0:T(8,128)(2,1)} %param.25), calls=%async_computation.3 | async-start | bytes 5767168 | tf_op jit(solution)/shard_map/all_to_all | solution.py:345
  247.0 8.2 %collective-permute-done.11 = bf16[1152,512]{1,0:T(8,128)(2,1)} collective-permute-done((bf16[1152,512]{1,0:T(8,128)(2,1)}, bf16[1152,512]{1,0:T(8,128)(2,1)}, u32[]{:S(2)}, u32[]{:S(2)}) %collective-permute-start.11) | collective-permute-done | bytes 1179680 | tf_op jit(solution)/shard_map/ppermute | solution.py:324
  255.2 10.5 %fusion.68 = f32[1152,2816]{1,0:T(8,128)S(1)} fusion(bf16[1024,2816]{1,0:T(8,128)(2,1)} %bitcast.10, bf16[1152,512]{1,0:T(8,128)(2,1)} %collective-permute-done.11, bf16[1152,512]{1,0:T(8,128)(2,1)} %bitcast.14, pred[]{:T(512)S(6)} %eq.79), kind=kOutput, calls=%fused_computation.122 | convolution fusion | flops 6654394368 | bytes 21102592 | tf_op jit(solution)/shard_map/dot_general | solution.py:27
  272.1 8.2 %convolution_convert_fusion.2 = bf16[1024,1408]{1,0:T(8,128)(2,1)} fusion(bf16[1152,1408]{1,0:T(8,128)(2,1)S(1)} %multiply_convert_fusion.1, bf16[1152,512]{1,0:T(8,128)(2,1)} %collective-permute-done.10, bf16[1152,512]{1,0:T(8,128)(2,1)} %bitcast.12, pred[]{:T(512)S(6)} %eq.79), kind=kOutput, calls=%fused_computation.22 | convolution fusion | flops 3333947392 | bytes 8486913 | tf_op jit(solution)/shard_map/dot_general | solution.py:33
  280.3 31.2 %all-to-all-done.3 = bf16[16,64,1408]{2,1,0:T(8,128)(2,1)} async-done(((bf16[16,64,1408]{2,1,0:T(8,128)(2,1)}), bf16[16,64,1408]{2,1,0:T(8,128)(2,1)}, u32[]{:S(2)}, u32[]{:S(2)}) %all-to-all-start.3) | async-done | bytes 2883616 | tf_op jit(solution)/shard_map/all_to_all | solution.py:345
  316.1 12.0 %fusion.6 = (bf16[1152,1408]{1,0:T(8,128)(2,1)S(1)}, bf16[1152,1408]{1,0:T(8,128)(2,1)S(1)}) fusion(f32[1152,2816]{1,0:T(8,128)} %copy-done.3, bf16[1024,1408]{1,0:T(8,128)(2,1)} %bitcast.15, bf16[1152,512]{1,0:T(8,128)(2,1)} %collective-permute-done.10, bf16[1152,512]{1,0:T(8,128)(2,1)} %bitcast.12, pred[]{:T(512)S(6)} %eq.79), kind=kOutput, calls=%fused_computation.8 | convolution fusion | flops 3369811968 | bytes 24707072 | tf_op jit(solution)/shard_map/dot_general | solution.py:27
  329.8 10.6 %fusion.9 = f32[1152,1024]{1,0:T(8,128)S(1)} fusion(bf16[1024,2816]{1,0:T(8,128)(2,1)} %bitcast.10, bf16[1152,1408]{1,0:T(8,128)(2,1)S(1)} %get-tuple-element.90, bf16[1152,1408]{1,0:T(8,128)(2,1)S(1)} %get-tuple-element.89), kind=kOutput, calls=%fused_computation.20 | convolution fusion | flops 6656753664 | bytes 16973824 | tf_op jit(solution)/shard_map/dot_general | solution.py:21
  350.4 18.4 %collective-permute-done.12 = bf16[1152,512]{1,0:T(8,128)(2,1)S(1)} collective-permute-done((bf16[1152,512]{1,0:T(8,128)(2,1)S(1)}, bf16[1152,512]{1,0:T(8,128)(2,1)S(1)}, u32[]{:S(2)}, u32[]{:S(2)}) %collective-permute-start.12) | collective-permute-done | bytes 1179680 | tf_op jit(solution)/shard_map/ppermute | solution.py:324
  370.2 10.5 %all-to-all-done.4 = bf16[16,64,1408]{2,1,0:T(8,128)(2,1)} async-done(((bf16[16,64,1408]{2,1,0:T(8,128)(2,1)}), bf16[16,64,1408]{2,1,0:T(8,128)(2,1)}, u32[]{:S(2)}, u32[]{:S(2)}) %all-to-all-start.4) | async-done | bytes 2883616 | tf_op jit(solution)/shard_map/all_to_all | solution.py:345
  385.9 27.7 %collective-permute-done.13 = bf16[1152,512]{1,0:T(8,128)(2,1)S(1)} collective-permute-done((bf16[1152,512]{1,0:T(8,128)(2,1)}, bf16[1152,512]{1,0:T(8,128)(2,1)S(1)}, u32[]{:S(2)}, u32[]{:S(2)}) %collective-permute-start.13) | collective-permute-done | bytes 1179680 | tf_op jit(solution)/shard_map/ppermute | solution.py:324
  423.4 13.8 %convolution_convert_fusion = bf16[1024,2816]{1,0:T(8,128)(2,1)} fusion(bf16[1152,1408]{1,0:T(8,128)(2,1)} %copy-done.25, bf16[1152,1408]{1,0:T(8,128)(2,1)} %copy-done.24, bf16[1152,512]{1,0:T(8,128)(2,1)} %collective-permute-done.11, bf16[1152,512]{1,0:T(8,128)(2,1)} %bitcast.14, pred[]{:T(512)S(6)} %eq.79), kind=kOutput, calls=%fused_computation.14 | convolution fusion | flops 6670254080 | bytes 14614529 | tf_op jit(solution)/shard_map/dot_general | solution.py:33
  437.1 14.2 %all-to-all-done.6 = bf16[16,72,512]{2,1,0:T(8,128)(2,1)} async-done(((bf16[16,72,512]{2,1,0:T(8,128)(2,1)}), bf16[16,72,512]{2,1,0:T(8,128)(2,1)}, u32[]{:S(2)}, u32[]{:S(2)}) %all-to-all-start.6) | async-done | bytes 1179680 | tf_op jit(solution)/shard_map/all_to_all | solution.py:345
  479.1 12.1 %collective-permute-done.16 = bf16[256,1024]{1,0:T(8,128)(2,1)S(1)} collective-permute-done((bf16[256,1024]{1,0:T(8,128)(2,1)}, bf16[256,1024]{1,0:T(8,128)(2,1)S(1)}, u32[]{:S(2)}, u32[]{:S(2)}) %collective-permute-start.16) | collective-permute-done | bytes 524320 | tf_op jit(solution)/shard_map/ppermute | solution.py:324
  496.0 13.1 %attend_backward.1 = (bf16[512,1536]{1,0:T(8,128)(2,1)}, f32[4,2,1024]{2,1,0:T(2,128)}) custom-call(s32[1]{0:T(128)} %dynamic_slice.84.length_ref, bf16[512,1536]{1,0:T(8,128)(2,1)} %convolution_convert_fusion.4.joined_ref, bf16[512,512]{1,0:T(8,128)(2,1)} %convolution_convert_fusion.7.grad_ref, f32[4,2,512]{2,1,0:T(2,128)} %get-tuple-element.72.total_ref, ...), custom_call_target="tpu_custom_call" | custom-call | flops 5368709120 | bytes 3670016 | tf_op jit(solution)/shard_map/attend_backward/pallas_call | solution.py:201
  552.1 29.3 %collective-permute-done.27 = f32[18,128]{1,0:T(8,128)S(1)} collective-permute-done((f32[18,128]{1,0:T(8,128)S(1)}, f32[18,128]{1,0:T(8,128)S(1)}, u32[]{:S(2)}, u32[]{:S(2)}) %collective-permute-start.27) | collective-permute-done | bytes 9248 | tf_op jit(solution)/shard_map/ppermute | solution.py:591
  598.3 10.1 %collective-permute-done.21 = bf16[64,2048]{1,0:T(8,128)(2,1)S(1)} collective-permute-done((bf16[64,2048]{1,0:T(8,128)(2,1)S(1)}, bf16[64,2048]{1,0:T(8,128)(2,1)S(1)}, u32[]{:S(2)}, u32[]{:S(2)}) %collective-permute-start.21) | collective-permute-done | bytes 262176 | tf_op jit(solution)/shard_map/ppermute | solution.py:557
  615.6 8.6 %slice_convert_fusion = (f32[16,64,1408]{2,1,0:T(8,128)}, f32[16,64,1408]{2,1,0:T(8,128)}) fusion(bf16[16,64,2816]{2,1,0:T(8,128)(2,1)} %all-to-all-done.7), kind=kLoop, calls=%fused_computation.26 | loop fusion | flops 2883584 | bytes 17301504 | tf_op jit(solution)/shard_map/convert_element_type | solution.py:362
  (206 shorter events, 214.9 us)
Async XLA Ops:
  3.3 19.4 %collective-permute-start.3 = (bf16[272,512]{1,0:T(8,128)(2,1)S(1)}, bf16[272,512]{1,0:T(8,128)(2,1)S(1)}, u32[]{:S(2)}, u32[]{:S(2)}) collective-permute-start(bf16[272,512]{1,0:T(8,128)(2,1)S(1)} %get-tuple-element.103), channel_id=1, source_target_pairs={{0,16},{2,18},{4,20},{6,22},{8,24},{10,26},{12,28},{14,30},{16,0},... | collective-permute-start | bytes 835592 | tf_op jit(solution)/shard_map/ppermute | solution.py:410
  3.7 25.6 %collective-permute-start.4 = (bf16[272,512]{1,0:T(8,128)(2,1)S(1)}, bf16[272,512]{1,0:T(8,128)(2,1)S(1)}, u32[]{:S(2)}, u32[]{:S(2)}) collective-permute-start(bf16[272,512]{1,0:T(8,128)(2,1)S(1)} %get-tuple-element.103), channel_id=1, source_target_pairs={{0,24},{2,26},{4,28},{6,30},{8,16},{10,18},{12,20},{14,22},{16,8},... | collective-permute-start | bytes 835592 | tf_op jit(solution)/shard_map/ppermute | solution.py:410
  29.3 131.6 %all-to-all-start = ((bf16[16,64,2816]{2,1,0:T(8,128)(2,1)}), bf16[16,64,2816]{2,1,0:T(8,128)(2,1)}, u32[]{:S(2)}, u32[]{:S(2)}) async-start(bf16[16,64,2816]{2,1,0:T(8,128)(2,1)} %pad_maximum_fusion.1), calls=%async_computation | async-start | bytes 11534336 | tf_op jit(solution)/shard_map/all_to_all | solution.py:345
  34.5 71.0 %collective-permute-start.1 = (bf16[256,1024]{1,0:T(8,128)(2,1)S(1)}, bf16[256,1024]{1,0:T(8,128)(2,1)}, u32[]{:S(2)}, u32[]{:S(2)}) collective-permute-start(bf16[256,1024]{1,0:T(8,128)(2,1)S(1)} %copy-done.4), channel_id=1, source_target_pairs={{0,1},{1,0},{2,3},{3,2},{4,5},{5,4},{6,7},{7,6},{8,9},{9,8},{10,11... | collective-permute-start | bytes 1572872 | tf_op jit(solution)/shard_map/ppermute | solution.py:324
  37.5 63.3 %collective-permute-start.6 = (bf16[4,272,512]{2,1,0:T(8,128)(2,1)S(1)}, bf16[4,272,512]{2,1,0:T(8,128)(2,1)}, u32[]{:S(2)}, u32[]{:S(2)}) collective-permute-start(bf16[4,272,512]{2,1,0:T(8,128)(2,1)S(1)} %pad_maximum_fusion.5.refs_0_), channel_id=1, source_target_pairs={{0,4},{2,6},{4,0},{6,2},{8,12},{10,14},{12,8},{14,10},{16,20},{18,... | collective-permute-start | bytes 3342344 | tf_op jit(solution)/shard_map/ppermute | solution.py:415
  40.0 62.6 %collective-permute-start = (bf16[256,512]{1,0:T(8,128)(2,1)}, bf16[256,512]{1,0:T(8,128)(2,1)}, u32[]{:S(2)}, u32[]{:S(2)}) collective-permute-start(bf16[256,512]{1,0:T(8,128)(2,1)} %get-tuple-element.101), channel_id=1, source_target_pairs={{0,1},{1,0},{2,3},{3,2},{4,5},{5,4},{6,7},{7,6},{8,9},{9,8},{10,11... | collective-permute-start | bytes 786440 | tf_op jit(solution)/shard_map/ppermute | solution.py:324
  44.6 62.6 %collective-permute-start.5 = (bf16[4,272,512]{2,1,0:T(8,128)(2,1)S(1)}, bf16[4,272,512]{2,1,0:T(8,128)(2,1)}, u32[]{:S(2)}, u32[]{:S(2)}) collective-permute-start(bf16[4,272,512]{2,1,0:T(8,128)(2,1)S(1)} %pad_maximum_fusion.5.refs_0_), channel_id=1, source_target_pairs={{0,2},{2,0},{4,6},{6,4},{8,10},{10,8},{12,14},{14,12},{16,18},{18,... | collective-permute-start | bytes 3342344 | tf_op jit(solution)/shard_map/ppermute | solution.py:417
  160.9 32.8 %all-to-all-start.1 = ((bf16[16,72,512]{2,1,0:T(8,128)(2,1)}), bf16[16,72,512]{2,1,0:T(8,128)(2,1)}, u32[]{:S(2)}, u32[]{:S(2)}) async-start(bf16[16,72,512]{2,1,0:T(8,128)(2,1)} %bitcast.11), calls=%async_computation.1 | async-start | bytes 2359296 | tf_op jit(solution)/shard_map/all_to_all | solution.py:345
  193.7 33.9 %all-to-all-start.2 = ((bf16[16,72,512]{2,1,0:T(8,128)(2,1)}), bf16[16,72,512]{2,1,0:T(8,128)(2,1)}, u32[]{:S(2)}, u32[]{:S(2)}) async-start(bf16[16,72,512]{2,1,0:T(8,128)(2,1)} %bitcast.77), calls=%async_computation.2 | async-start | bytes 2359296 | tf_op jit(solution)/shard_map/all_to_all | solution.py:345
  199.3 28.3 %collective-permute-start.10 = (bf16[1152,512]{1,0:T(8,128)(2,1)}, bf16[1152,512]{1,0:T(8,128)(2,1)}, u32[]{:S(2)}, u32[]{:S(2)}) collective-permute-start(bf16[1152,512]{1,0:T(8,128)(2,1)} %bitcast.12), channel_id=1, source_target_pairs={{0,1},{1,0},{2,3},{3,2},{4,5},{5,4},{6,7},{7,6},{8,9},{9,8},{10,11... | collective-permute-start | bytes 3538952 | tf_op jit(solution)/shard_map/ppermute | solution.py:324
  227.6 27.6 %collective-permute-start.11 = (bf16[1152,512]{1,0:T(8,128)(2,1)}, bf16[1152,512]{1,0:T(8,128)(2,1)}, u32[]{:S(2)}, u32[]{:S(2)}) collective-permute-start(bf16[1152,512]{1,0:T(8,128)(2,1)} %bitcast.14), channel_id=1, source_target_pairs={{0,1},{1,0},{2,3},{3,2},{4,5},{5,4},{6,7},{7,6},{8,9},{9,8},{10,11... | collective-permute-start | bytes 3538952 | tf_op jit(solution)/shard_map/ppermute | solution.py:324
  229.1 82.3 %all-to-all-start.3 = ((bf16[16,64,1408]{2,1,0:T(8,128)(2,1)}), bf16[16,64,1408]{2,1,0:T(8,128)(2,1)}, u32[]{:S(2)}, u32[]{:S(2)}) async-start(bf16[16,64,1408]{2,1,0:T(8,128)(2,1)} %param.25), calls=%async_computation.3 | async-start | bytes 5767168 | tf_op jit(solution)/shard_map/all_to_all | solution.py:345
  311.4 69.3 %all-to-all-start.4 = ((bf16[16,64,1408]{2,1,0:T(8,128)(2,1)}), bf16[16,64,1408]{2,1,0:T(8,128)(2,1)}, u32[]{:S(2)}, u32[]{:S(2)}) async-start(bf16[16,64,1408]{2,1,0:T(8,128)(2,1)} %bitcast.75), calls=%async_computation.4 | async-start | bytes 5767168 | tf_op jit(solution)/shard_map/all_to_all | solution.py:345
  340.6 28.1 %collective-permute-start.12 = (bf16[1152,512]{1,0:T(8,128)(2,1)S(1)}, bf16[1152,512]{1,0:T(8,128)(2,1)S(1)}, u32[]{:S(2)}, u32[]{:S(2)}) collective-permute-start(bf16[1152,512]{1,0:T(8,128)(2,1)S(1)} %dynamic-slice_convert_fusion.1), channel_id=1, source_target_pairs={{0,1},{1,0},{2,3},{3,2},{4,5},{5,4},{6,7},{7,6},{8,9},{9,8},{10,11... | collective-permute-start | bytes 3538952 | tf_op jit(solution)/shard_map/ppermute | solution.py:324
  380.7 36.1 %all-to-all-start.5 = ((bf16[16,72,512]{2,1,0:T(8,128)(2,1)}), bf16[16,72,512]{2,1,0:T(8,128)(2,1)}, u32[]{:S(2)}, u32[]{:S(2)}) async-start(bf16[16,72,512]{2,1,0:T(8,128)(2,1)} %bitcast.17), calls=%async_computation.5 | async-start | bytes 2359296 | tf_op jit(solution)/shard_map/all_to_all | solution.py:345
  385.4 28.2 %collective-permute-start.13 = (bf16[1152,512]{1,0:T(8,128)(2,1)}, bf16[1152,512]{1,0:T(8,128)(2,1)S(1)}, u32[]{:S(2)}, u32[]{:S(2)}) collective-permute-start(bf16[1152,512]{1,0:T(8,128)(2,1)} %dynamic-slice_convert_fusion), channel_id=1, source_target_pairs={{0,1},{1,0},{2,3},{3,2},{4,5},{5,4},{6,7},{7,6},{8,9},{9,8},{10,11... | collective-permute-start | bytes 3538952 | tf_op jit(solution)/shard_map/ppermute | solution.py:324
  416.8 34.5 %all-to-all-start.6 = ((bf16[16,72,512]{2,1,0:T(8,128)(2,1)}), bf16[16,72,512]{2,1,0:T(8,128)(2,1)}, u32[]{:S(2)}, u32[]{:S(2)}) async-start(bf16[16,72,512]{2,1,0:T(8,128)(2,1)} %bitcast.19), calls=%async_computation.6 | async-start | bytes 2359296 | tf_op jit(solution)/shard_map/all_to_all | solution.py:345
  451.3 164.3 %all-to-all-start.7 = ((bf16[16,64,2816]{2,1,0:T(8,128)(2,1)}), bf16[16,64,2816]{2,1,0:T(8,128)(2,1)}, u32[]{:S(2)}, u32[]{:S(2)}) async-start(bf16[16,64,2816]{2,1,0:T(8,128)(2,1)} %bitcast.74), calls=%async_computation.7 | async-start | bytes 11534336 | tf_op jit(solution)/shard_map/all_to_all | solution.py:345
  532.0 53.5 %collective-permute-start.19 = (bf16[4,64,2048]{2,1,0:T(8,128)(2,1)}, bf16[4,64,2048]{2,1,0:T(8,128)(2,1)}, u32[]{:S(2)}, u32[]{:S(2)}) collective-permute-start(bf16[4,64,2048]{2,1,0:T(8,128)(2,1)} %dynamic-slice_bitcast_fusion.1), channel_id=1, source_target_pairs={{0,4},{2,6},{4,0},{6,2},{8,12},{10,14},{12,8},{14,10},{16,20},{18,... | collective-permute-start | bytes 3145736 | tf_op jit(solution)/shard_map/ppermute | solution.py:547
  534.6 49.3 %collective-permute-start.17 = (bf16[256,1024]{1,0:T(8,128)(2,1)}, bf16[256,1024]{1,0:T(8,128)(2,1)S(1)}, u32[]{:S(2)}, u32[]{:S(2)}) collective-permute-start(bf16[256,1024]{1,0:T(8,128)(2,1)} %dynamic-slice_convert_fusion.2), channel_id=1, source_target_pairs={{0,1},{1,0},{2,3},{3,2},{4,5},{5,4},{6,7},{7,6},{8,9},{9,8},{10,11... | collective-permute-start | bytes 1572872 | tf_op jit(solution)/shard_map/ppermute | solution.py:324
  538.3 43.1 %collective-permute-start.27 = (f32[18,128]{1,0:T(8,128)S(1)}, f32[18,128]{1,0:T(8,128)S(1)}, u32[]{:S(2)}, u32[]{:S(2)}) collective-permute-start(f32[18,128]{1,0:T(8,128)S(1)} %add.231), channel_id=1, source_target_pairs={{0,16},{2,18},{4,20},{6,22},{8,24},{10,26},{12,28},{14,30},{16,0},... | collective-permute-start | bytes 27656 | tf_op jit(solution)/shard_map/ppermute | solution.py:591
  538.3 44.3 %collective-permute-start.28 = (f32[18,128]{1,0:T(8,128)S(1)}, f32[18,128]{1,0:T(8,128)S(1)}, u32[]{:S(2)}, u32[]{:S(2)}) collective-permute-start(f32[18,128]{1,0:T(8,128)S(1)} %add.231), channel_id=1, source_target_pairs={{0,24},{2,26},{4,28},{6,30},{8,16},{10,18},{12,20},{14,22},{16,8},... | collective-permute-start | bytes 27656 | tf_op jit(solution)/shard_map/ppermute | solution.py:591
  588.8 19.5 %collective-permute-start.21 = (bf16[64,2048]{1,0:T(8,128)(2,1)S(1)}, bf16[64,2048]{1,0:T(8,128)(2,1)S(1)}, u32[]{:S(2)}, u32[]{:S(2)}) collective-permute-start(bf16[64,2048]{1,0:T(8,128)(2,1)S(1)} %get-tuple-element.96), channel_id=1, source_target_pairs={{0,16},{2,18},{4,20},{6,22},{8,24},{10,26},{12,28},{14,30},{16,0},... | collective-permute-start | bytes 786440 | tf_op jit(solution)/shard_map/ppermute | solution.py:557
  590.4 23.1 %collective-permute-start.22 = (bf16[64,2048]{1,0:T(8,128)(2,1)S(1)}, bf16[64,2048]{1,0:T(8,128)(2,1)S(1)}, u32[]{:S(2)}, u32[]{:S(2)}) collective-permute-start(bf16[64,2048]{1,0:T(8,128)(2,1)S(1)} %get-tuple-element.95), channel_id=1, source_target_pairs={{0,24},{2,26},{4,28},{6,30},{8,16},{10,18},{12,20},{14,22},{16,8},... | collective-permute-start | bytes 786440 | tf_op jit(solution)/shard_map/ppermute | solution.py:557
  (39 other events, 515.1 us)

commit v3 on v2

--- a/solution.py
+++ b/solution.py
@@ -357,6 +357,20 @@
         arrived = exchange(rows.reshape(dp_count, slot_count, rows.shape[1]))
         return arrived.reshape(total_slots, rows.shape[1])
 
+    spare = slot_count - shard_rows
+    fold = shard_rows // spare
+
+    def pack(rows):
+        blocks = rows.reshape(dp_count, slot_count, half)
+        tail = blocks[:, shard_rows:].reshape(dp_count, spare, fold, half // fold)
+        tail = tail.transpose(0, 2, 1, 3).reshape(dp_count, shard_rows, half // fold)
+        return jnp.concatenate([blocks[:, :shard_rows], tail], axis=2)
+
+    def unpack(packed):
+        tail = packed[:, :, half:].reshape(dp_count, fold, spare, half // fold)
+        tail = tail.transpose(0, 2, 1, 3).reshape(dp_count, spare, half)
+        return jnp.concatenate([packed[:, :, :half], tail], axis=1).reshape(total_slots, half)
+
     def regroup(arrived):
         return jnp.sum(
             arrived.astype(jnp.float32).reshape(
@@ -404,7 +418,9 @@
         pick_gate, ordered(own_part(mix_grad, 1), mix_other, 0)
     ).astype(jnp.bfloat16)
     residual, out_grad_cols = chain(tokens, out_grad_cols)
-    gate_up = jnp.concatenate([gate_weight, up_weight], axis=2)
+    gate_up = jnp.concatenate(
+        [home_order(gate_weight), home_order(up_weight), pack(out_grad_cols)], axis=2
+    )
     if dp_count == 16:
         across = [
             lax.ppermute(layer_shard, "dp", [(i, i ^ (4 * k)) for i in range(16)])
@@ -428,8 +444,9 @@
         )
         out_all = layer_all[:, 3 * shard_rows : 4 * shard_rows].reshape(width, head_cols)
         gain_rows = layer_all[:, 4 * shard_rows :]
-    out_grad_cols, gate_up_all = chain(out_grad_cols, fetch(gate_up))
-    slot_grad_half = route(out_grad_cols)
+    arrived = exchange(gate_up)
+    gate_up_all = arrived.reshape(width, arrived.shape[2])
+    slot_grad_half = unpack(arrived[:, :, 2 * hidden_cols :])
 
     distance = jnp.arange(2 * seq, dtype=jnp.int32)
     table_reversed = jnp.concatenate(
@@ -455,8 +472,7 @@
     mid = inputs + own_valid * (own_part(branch, 0) + branch_other.astype(jnp.float32))
     mid_scale = lax.rsqrt(jnp.mean(mid * mid, axis=-1, keepdims=True) + EPSILON)
     norm_two = (mid * mid_scale * gain_two).astype(jnp.bfloat16)
-    norm_two_away, gate_up_all = chain(other_part(norm_two, 1), gate_up_all)
-    norm_two_cols = ordered(own_part(norm_two, 1), swap(norm_two_away), 0)
+    norm_two_cols = ordered(own_part(norm_two, 1), swap(other_part(norm_two, 1)), 0)
     expert_rows, slot_grad_half = chain(
         dot_nn(pick, norm_two_cols).astype(jnp.bfloat16), slot_grad_half
     )
@@ -470,7 +486,7 @@
 
     pre = dot_nn(expert_in, gate_up_all)
     gate_pre = pre[:, :hidden_cols]
-    up_pre = pre[:, hidden_cols:]
+    up_pre = pre[:, hidden_cols : 2 * hidden_cols]
     gelu, slope = gelu_parts(gate_pre)
     hidden = lax.optimization_barrier((gelu * up_pre).astype(jnp.bfloat16))
     down_grad, down_all = chain(dot_tn(slot_grad, hidden).astype(jnp.bfloat16), down_all)
@@ -480,6 +496,7 @@
         [
             (hidden_grad * up_pre * slope).astype(jnp.bfloat16),
             (hidden_grad * gelu).astype(jnp.bfloat16),
+            jnp.zeros((total_slots, half + half // fold), jnp.bfloat16),
         ],
         axis=1,
     )
@@ -498,17 +515,18 @@
         own_part(expert_out_part, 1) + swap(expert_out_away).astype(jnp.float32)
     ).astype(jnp.bfloat16)
     slot_back_half, down_back = chain(slot_back_half, down_back)
-    expert_out_half, slot_back = chain(expert_out_half, route(slot_back_half))
-    gate_up_grad, returned = chain(
-        dot_tn(expert_in, pre_grad).astype(jnp.bfloat16), route(expert_out_half)
-    )
-    gate_up_back = send_grad(gate_up_grad)
-
-    mix_cols = dot_tn(pick_gate, returned)
-    mix_own = ordered(
-        own_part(mix_cols, 0), swap(other_part(mix_cols, 0).astype(jnp.bfloat16)).astype(jnp.float32), 1
-    )
-    mixed = (mid + own_valid * mix_own).astype(jnp.bfloat16)
+    last, slot_back = chain(
+        lax.dynamic_update_slice(
+            dot_tn(expert_in, pre_grad)
+            .astype(jnp.bfloat16)
+            .reshape(dp_count, shard_rows, pre_grad.shape[1]),
+            pack(expert_out_half),
+            (0, 0, 2 * hidden_cols),
+        ),
+        route(slot_back_half),
+    )
+    arrived_back = exchange(last)
+
     back_cols = dot_tn(pick, slot_back)
     norm_two_grad = ordered(
         own_part(back_cols, 0), swap(other_part(back_cols, 0).astype(jnp.bfloat16)).astype(jnp.float32), 1
@@ -537,26 +555,81 @@
         ],
         axis=1,
     )
+    gain_one_grad = jnp.sum(norm_one_part * (inputs_all * scale_all), axis=0)
+    norm_one_grad = own_part(norm_one_part, 0) + swap(
+        other_part(norm_one_part, 0).astype(jnp.bfloat16)
+    ).astype(jnp.float32)
+    scale = lax.rsqrt(jnp.mean(inputs * inputs, axis=-1, keepdims=True) + EPSILON)
+    unit = inputs * scale
+    inner = norm_one_grad * gain_one
+    input_grad = mid_grad + scale * (
+        inner - unit * jnp.mean(inner * unit, axis=-1, keepdims=True)
+    )
+    gain_part = jnp.concatenate([gain_one_grad, gain_two_grad]).reshape(-1, LANES)
+    small = jnp.concatenate(
+        [gain_part + swap(gain_part), bias_grad.reshape(-1, LANES)], axis=0
+    )
+
+    def partner(block, offset):
+        return lax.ppermute(block, "dp", [(i, i ^ offset) for i in range(dp_count)])
+
+    row_size = layer_part.shape[1]
+    small = jnp.pad(small.reshape(-1), (0, -small.size % row_size)).reshape(-1, row_size)
+    small_rows = small.shape[0]
+
+    def with_small(block):
+        high = lax.reduce_precision(small, 8, 7)
+        rows = jnp.concatenate([high, small - high], axis=0).astype(jnp.bfloat16)
+        rows = jnp.pad(rows, ((0, -rows.shape[0] % 8), (0, 0)))
+        return jnp.concatenate([block, rows], axis=0)
+
+    def small_of(block, first):
+        rows = block[first : first + 2 * small_rows].astype(jnp.float32)
+        return rows[:small_rows] + rows[small_rows:]
+
     if dp_count == 16:
-        blocks = layer_part.reshape(dp_count, shard_rows, layer_part.shape[1])
+        blocks = layer_part.reshape(dp_count, shard_rows, row_size)
         for step in (1, 2):
-            pieces = blocks.reshape(-1, 2, shard_rows, blocks.shape[2])
+            pieces = blocks.reshape(-1, 2, shard_rows, row_size)
             bit = (dp_index // step) % 2
             away = lax.dynamic_index_in_dim(pieces, 1 - bit, 1, keepdims=False)
             stay = lax.dynamic_index_in_dim(pieces, bit, 1, keepdims=False)
-            arrived = lax.ppermute(away, "dp", [(i, i ^ step) for i in range(dp_count)])
-            blocks = (stay.astype(jnp.float32) + arrived.astype(jnp.float32)).astype(
-                jnp.bfloat16
-            )
-        place_out = dp_index // 4
-        layer_grad = lax.dynamic_index_in_dim(blocks, place_out, 0, keepdims=False).astype(
-            jnp.float32
+            if step == 1:
+                came = partner(away, step)
+                small = small + partner(small, step)
+            else:
+                came = partner(with_small(away.reshape(-1, row_size)), step)
+                came = chain(came, input_grad)[0]
+                small = small + small_of(came, away.shape[0] * shard_rows)
+                came = came[: away.shape[0] * shard_rows].reshape(away.shape)
+            blocks = (stay.astype(jnp.float32) + came.astype(jnp.float32)).astype(jnp.bfloat16)
+        outer = dp_index // 4
+        leaving = [
+            with_small(lax.dynamic_index_in_dim(blocks, outer ^ k, 0, keepdims=False))
+            for k in range(1, 4)
+        ]
+        stay = lax.dynamic_index_in_dim(blocks, outer, 0, keepdims=False)
+        arrived_back = chain(arrived_back, leaving)[0]
+        came = [partner(piece, 4 * k) for k, piece in zip(range(1, 4), leaving, strict=True)]
+    else:
+        step = 1
+        while step < dp_count:
+            small = small + partner(small, step)
+            step *= 2
+    returned = unpack(arrived_back[:, :, 2 * hidden_cols :])
+    mix_cols = dot_tn(pick_gate, returned)
+    mix_away = other_part(mix_cols, 0).astype(jnp.bfloat16)
+    arrived_back = chain(arrived_back, mix_away)[0]
+    gate_grad = regroup(arrived_back[:, :, :hidden_cols])
+    up_grad = regroup(arrived_back[:, :, hidden_cols : 2 * hidden_cols])
+    mix_own = ordered(own_part(mix_cols, 0), swap(mix_away).astype(jnp.float32), 1)
+    mixed = (mid + own_valid * mix_own).astype(jnp.bfloat16)
+    if dp_count == 16:
+        came = chain(came, (gate_grad, up_grad, mixed))[0]
+        small = small + sum(small_of(piece, shard_rows) for piece in came)
+        layer_grad = stay.astype(jnp.float32) + sum(
+            piece[:shard_rows].astype(jnp.float32) for piece in came
         )
-        for k in range(1, 4):
-            away = lax.dynamic_index_in_dim(blocks, place_out ^ k, 0, keepdims=False)
-            layer_grad = layer_grad + lax.ppermute(
-                away, "dp", [(i, i ^ (4 * k)) for i in range(dp_count)]
-            ).astype(jnp.float32)
     else:
         layer_grad = lax.psum_scatter(
             layer_part, "dp", scatter_dimension=0, tiled=True
@@ -568,32 +641,11 @@
         .reshape(3, shard_rows, head_cols)
     )
     out_grad = layer_grad[:, 3 * head_cols :]
-    gain_one_grad = jnp.sum(norm_one_part * (inputs_all * scale_all), axis=0)
-    norm_one_grad = own_part(norm_one_part, 0) + swap(
-        other_part(norm_one_part, 0).astype(jnp.bfloat16)
-    ).astype(jnp.float32)
-    scale = lax.rsqrt(jnp.mean(inputs * inputs, axis=-1, keepdims=True) + EPSILON)
-    unit = inputs * scale
-    inner = norm_one_grad * gain_one
-    input_grad = mid_grad + scale * (
-        inner - unit * jnp.mean(inner * unit, axis=-1, keepdims=True)
-    )
-
     gain_size = 2 * width
-    gain_part = jnp.concatenate([gain_one_grad, gain_two_grad]).reshape(-1, LANES)
-    small = jnp.concatenate(
-        [gain_part + swap(gain_part), bias_grad.reshape(-1, LANES)], axis=0
-    )
-    step = 1
-    while step < dp_count:
-        last = min(4, dp_count // step) if step >= 4 else 2
-        small = small + sum(
-            lax.ppermute(small, "dp", [(i, i ^ (k * step)) for i in range(dp_count)])
-            for k in range(1, last)
-        )
-        step *= last
     gain_sums = small.reshape(-1)[:gain_size].reshape(2, width)
-    bias_out = small.reshape(-1)[gain_size:].reshape(head_count, bucket_count)
+    bias_out = small.reshape(-1)[gain_size : gain_size + head_count * bucket_count].reshape(
+        head_count, bucket_count
+    )
     gains_grad = lax.dynamic_slice_in_dim(gain_sums, dp_index * shard_rows, shard_rows, 1)
     return (
         mixed,
@@ -602,8 +654,8 @@
         out_grad,
         gains_grad,
         bias_out,
-        regroup(gate_up_back[:, :, :hidden_cols]),
-        regroup(gate_up_back[:, :, hidden_cols:]),
+        gate_grad,
+        up_grad,
         regroup(down_back),
     )
 

time: 629 us -> 606 us (0.963)
  waiting for transfers between devices: 347 us -> 303 us
  starting transfers between devices: 80.4 us -> 62 us
  local copies, waits for them, and re-layouts: 26.6 us -> 41.5 us
  matrix products: 89.7 us -> 99.6 us
  other arithmetic: 44.5 us -> 53.5 us
    all_to_all x8 -> x6, waiting for transfers between devices: 82.4 us -> 60.5 us  [exchange(): return lax.all_to_all(block, 'dp', split_axis=0, concat_axis=0, tiled=True)]
    all_to_all x8 -> x6, starting transfers between devices: 53.9 us -> 32 us  [exchange(): return lax.all_to_all(block, 'dp', split_axis=0, concat_axis=0, tiled=True)]
    ppermute x10 -> x6, waiting for transfers between devices: 61.2 us -> 40.7 us  [partner(): return lax.ppermute(block, 'dp', [(i, i ^ offset) for i in range(dp_count)])]
    ppermute x1, waiting for transfers between devices: 56.2 us -> 70.3 us  [on_device(): side = lax.ppermute(near, 'dp', [(i, i ^ 2) for i in range(16)])]
    ppermute x3, waiting for transfers between devices: 18.3 us -> 6.25 us  [on_device(): lax.ppermute(layer_shard, 'dp', [(i, i ^ 4 * k) for i in range(16)])]
    convert_element_type x1 -> x2, local copies, waits for them, and re-layouts: 0.04 us -> 9.7 us  [the longest x1 9.66 us: on_device(): last, slot_back = chain(lax.dynamic_update_slice(dot_tn(expert_in, pre_gr...]
    ppermute x13, starting transfers between devices: 12.2 us -> 19.8 us  [swap(): return lax.ppermute(block, 'tensor', [(0, 1), (1, 0)])]
    unnamed x55 -> x75, local copies, waits for them, and re-layouts: 12.8 us -> 11.3 us
  transfers between devices with their start and end apart: 37 -> 31, of which waited for: 27 -> 18; matrix products, arithmetic and copies ran while one was open for 22% -> 29% of each run, Pallas kernels for 6% -> 6%
where the time goes in v3:
time: 606 us; the launch traced here: 596 us
  waiting for transfers between devices  303 us (50%)
  matrix products  99.6 us (16%)
  starting transfers between devices  62 us (10%)
  other arithmetic  53.5 us (9%)
  local copies, waits for them, and re-layouts  41.5 us (7%)
  Pallas kernels  34.5 us (6%)
    ppermute x13, waiting for transfers between devices, swap(): return lax.ppermute(block, 'tensor', [(0, 1), (1, 0)])  125 us
    ppermute x1, waiting for transfers between devices, on_device(): side = lax.ppermute(near, 'dp', [(i, i ^ 2) for i in range(16)])  70.3 us
    all_to_all x6, waiting for transfers between devices, exchange(): return lax.all_to_all(block, 'dp', split_axis=0, concat_axis=0, tiled=True)  60.5 us
    dot_general x7, matrix products, dot_nn(): lax.dot_general(left, right, (((1,), (0,)), ((), ())), preferred_element_...  40.8 us
    ppermute x6, waiting for transfers between devices, partner(): return lax.ppermute(block, 'dp', [(i, i ^ offset) for i in range(dp_count)])  40.7 us
    dot_general x6, matrix products, dot_tn(): lax.dot_general(left, right, (((0,), (0,)), ((), ())), preferred_element_...  32.8 us
    all_to_all x6, starting transfers between devices, exchange(): return lax.all_to_all(block, 'dp', split_axis=0, concat_axis=0, tiled=True)  32 us
    dot_general x4, matrix products, dot_nt(): lax.dot_general(left, right, (((1,), (1,)), ((), ())), preferred_element_...  25.6 us
  transfers between devices with their start and end apart: 31, of which 18 were waited for; matrix products, arithmetic and copies ran while one was open for 29% of the time, Pallas kernels for 6%

profile of v3, /device:TPU:16, one launch (start us, length us, event | category | flops | bytes accessed | tf_op | source)
XLA Modules:
  0.0 596.0 jit_solution(8730341162369572810)
XLA Ops:
  23.0 6.2 %collective-permute-done.4 = bf16[272,512]{1,0:T(8,128)(2,1)S(1)} collective-permute-done((bf16[272,512]{1,0:T(8,128)(2,1)S(1)}, bf16[272,512]{1,0:T(8,128)(2,1)S(1)}, u32[]{:S(2)}, u32[]{:S(2)}) %collective-permute-start.4) | collective-permute-done | bytes 278560 | tf_op jit(solution)/shard_map/ppermute | solution.py:426
  36.2 70.3 %collective-permute-done.6.refs_2_ = bf16[4,272,512]{2,1,0:T(8,128)(2,1)} collective-permute-done((bf16[4,272,512]{2,1,0:T(8,128)(2,1)S(1)}, bf16[4,272,512]{2,1,0:T(8,128)(2,1)}, u32[]{:S(2)}, u32[]{:S(2)}) %collective-permute-start.6) | collective-permute-done | bytes 1114144 | tf_op jit(solution)/shard_map/ppermute | solution.py:431
  109.6 11.2 %collective-permute-done.1 = bf16[256,1024]{1,0:T(8,128)(2,1)S(1)} collective-permute-done((bf16[256,1024]{1,0:T(8,128)(2,1)S(1)}, bf16[256,1024]{1,0:T(8,128)(2,1)S(1)}, u32[]{:S(2)}, u32[]{:S(2)}) %collective-permute-start.1) | collective-permute-done | bytes 524320 | tf_op jit(solution)/shard_map/ppermute | solution.py:324
  121.3 10.2 %assemble.1 = (bf16[1024,1536]{1,0:T(8,128)(2,1)}, bf16[1024,512]{1,0:T(8,128)(2,1)}, bf16[16,16,512]{2,1,0:T(8,128)(2,1)}) custom-call(s32[2]{0:T(128)} %pad_add_fusion.1.place_ref, bf16[4,272,512]{2,1,0:T(8,128)(2,1)} %copy-done.6, bf16[4,272,512]{2,1,0:T(8,128)(2,1)} %collective-permute-done.5.refs_1_, ...), custom_call_target="tpu_custom_call" | custom-call | tf_op jit(solution)/shard_map/assemble/pallas_call | solution.py:255
  137.4 11.1 %attend_forward.1 = (bf16[512,512]{1,0:T(8,128)(2,1)}, f32[4,2,512]{2,1,0:T(2,128)}) custom-call(s32[1]{0:T(128)} %dynamic_slice.84.length_ref, bf16[512,1536]{1,0:T(8,128)(2,1)} %convolution_convert_fusion.4.joined_ref, f32[4,2,1024]{2,1,0:T(2,128)} %reshape.217.bias_ref), custom_call_target="tpu_custom_call" | custom-call | flops 2147483648 | bytes 2097152 | tf_op jit(solution)/shard_map/attend_forward/pallas_call | solution.py:103
  153.4 12.1 %collective-permute-done.8 = bf16[256,1024]{1,0:T(8,128)(2,1)S(1)} collective-permute-done((bf16[256,1024]{1,0:T(8,128)(2,1)S(1)}, bf16[256,1024]{1,0:T(8,128)(2,1)S(1)}, u32[]{:S(2)}, u32[]{:S(2)}) %collective-permute-start.8) | collective-permute-done | bytes 524320 | tf_op jit(solution)/shard_map/ppermute | solution.py:324
  176.3 12.6 %all-to-all-done = bf16[16,64,3392]{2,1,0:T(8,128)(2,1)} async-done(((bf16[16,64,3392]{2,1,0:T(8,128)(2,1)}), bf16[16,64,3392]{2,1,0:T(8,128)(2,1)}, u32[]{:S(2)}, u32[]{:S(2)}) %all-to-all-start) | async-done | bytes 6946848 | tf_op jit(solution)/shard_map/all_to_all | solution.py:345
  198.8 26.8 %collective-permute-done.10 = bf16[1152,512]{1,0:T(8,128)(2,1)} collective-permute-done((bf16[1152,512]{1,0:T(8,128)(2,1)}, bf16[1152,512]{1,0:T(8,128)(2,1)}, u32[]{:S(2)}, u32[]{:S(2)}) %collective-permute-start.10) | collective-permute-done | bytes 1179680 | tf_op jit(solution)/shard_map/ppermute | solution.py:324
  225.7 6.4 %all-to-all-start.2 = ((bf16[16,64,1408]{2,1,0:T(8,128)(2,1)}), bf16[16,64,1408]{2,1,0:T(8,128)(2,1)}, u32[]{:S(2)}, u32[]{:S(2)}) async-start(bf16[16,64,1408]{2,1,0:T(8,128)(2,1)} %param.25), calls=%async_computation.2 | async-start | bytes 5767168 | tf_op jit(solution)/shard_map/all_to_all | solution.py:345
  233.6 26.5 %collective-permute-done.11 = bf16[1152,512]{1,0:T(8,128)(2,1)S(1)} collective-permute-done((bf16[1152,512]{1,0:T(8,128)(2,1)S(1)}, bf16[1152,512]{1,0:T(8,128)(2,1)S(1)}, u32[]{:S(2)}, u32[]{:S(2)}) %collective-permute-start.11) | collective-permute-done | bytes 1179680 | tf_op jit(solution)/shard_map/ppermute | solution.py:324
  260.2 15.3 %fusion.67 = f32[1152,3392]{0,1:T(8,128)} fusion(bf16[1024,3392]{1,0:T(8,128)(2,1)} %bitcast.18, bf16[1152,512]{1,0:T(8,128)(2,1)S(1)} %collective-permute-done.11, bf16[1152,512]{1,0:T(8,128)(2,1)S(1)} %bitcast.107, pred[]{:T(512)S(6)} %eq.79), kind=kOutput, calls=%fused_computation.127 | convolution fusion | flops 8013348864 | bytes 24936448 | tf_op jit(solution)/shard_map/dot_general | solution.py:27
  283.2 7.4 %convolution_convert_fusion.2 = bf16[1024,1408]{1,0:T(8,128)(2,1)} fusion(bf16[1152,1408]{0,1:T(8,128)(2,1)S(1)} %multiply_convert_fusion.1, bf16[1152,512]{1,0:T(8,128)(2,1)} %collective-permute-done.10, bf16[1152,512]{1,0:T(8,128)(2,1)S(1)} %bitcast.110, pred[]{:T(512)S(6)} %eq.79), kind=kOutput, calls=%fused_computation.24 | convolution fusion | flops 3333947392 | bytes 8486913 | tf_op jit(solution)/shard_map/dot_general | solution.py:33
  301.2 14.6 %fusion.6 = (bf16[1152,1408]{0,1:T(8,128)(2,1)}, bf16[1152,1408]{0,1:T(8,128)(2,1)}) fusion(f32[1152,3392]{0,1:T(8,128)} %fusion.67, bf16[1024,1408]{1,0:T(8,128)(2,1)} %bitcast.19, bf16[1152,512]{1,0:T(8,128)(2,1)} %collective-permute-done.10, bf16[1152,512]{1,0:T(8,128)(2,1)S(1)} %bitcast.111, pred[]{:T(512)S(6)} %eq.79), kind=kOutput, calls=%fused_computation.11 | convolution fusion | flops 3369811968 | bytes 24707072 | tf_op jit(solution)/shard_map/dot_general | solution.py:27
  315.8 14.7 %fusion.7 = f32[1152,1024]{1,0:T(8,128)S(1)} fusion(bf16[1024,3392]{1,0:T(8,128)(2,1)} %bitcast.18, bf16[1152,1408]{0,1:T(8,128)(2,1)} %get-tuple-element.94, bf16[1152,1408]{0,1:T(8,128)(2,1)} %get-tuple-element.93, bf16[3392]{0:T(1024)(128)(2,1)S(1)} %pad.57.clone), kind=kOutput, calls=%fused_computation.15 | convolution fusion | flops 8026177536 | bytes 18160256 | tf_op jit(solution)/shard_map/dot_general | solution.py:21
  343.7 17.1 %collective-permute-done.12 = bf16[1152,512]{1,0:T(8,128)(2,1)S(1)} collective-permute-done((bf16[1152,512]{1,0:T(8,128)(2,1)S(1)}, bf16[1152,512]{1,0:T(8,128)(2,1)S(1)}, u32[]{:S(2)}, u32[]{:S(2)}) %collective-permute-start.12) | collective-permute-done | bytes 1179680 | tf_op jit(solution)/shard_map/ppermute | solution.py:324
  370.5 16.7 %convolution_convert_fusion = bf16[1024,3392]{0,1:T(8,128)(2,1)} fusion(bf16[1152,1408]{0,1:T(8,128)(2,1)} %get-tuple-element.94, bf16[1152,1408]{0,1:T(8,128)(2,1)} %get-tuple-element.93, bf16[3392]{0:T(1024)(128)(2,1)S(1)} %pad.57.clone, bf16[1152,512]{1,0:T(8,128)(2,1)} %copy-done.34, bf16[1152,512]{1,0:T(8,128)(2,1)} %bitcast.108, pred[]{:T(512)S(6)} %eq.79), kind=kOutput, calls=%fused_computation.3 | convolution fusion | flops 8040267776 | bytes 15800961 | tf_op jit(solution)/shard_map/dot_general | solution.py:33
  387.2 9.7 %copy.56 = bf16[1024,3392]{1,0:T(8,128)(2,1)} copy(bf16[1024,3392]{0,1:T(8,128)(2,1)} %convolution_convert_fusion) | data formatting | bytes 13893632 | tf_op jit(solution)/shard_map/convert_element_type | solution.py:521
  400.6 6.4 %all-to-all-start.5 = ((bf16[16,64,3392]{2,1,0:T(8,128)(2,1)}), bf16[16,64,3392]{2,1,0:T(8,128)(2,1)}, u32[]{:S(2)}, u32[]{:S(2)}) async-start(bf16[16,64,3392]{2,1,0:T(8,128)(2,1)} %maximum_dynamic-update-slice_fusion), calls=%async_computation.5 | async-start | bytes 14155776 | tf_op jit(solution)/shard_map/all_to_all | solution.py:345
  410.8 6.8 %collective-permute-done.14 = bf16[256,512]{1,0:T(8,128)(2,1)S(1)} collective-permute-done((bf16[256,512]{1,0:T(8,128)(2,1)S(1)}, bf16[256,512]{1,0:T(8,128)(2,1)S(1)}, u32[]{:S(2)}, u32[]{:S(2)}) %collective-permute-start.14) | collective-permute-done | bytes 262176 | tf_op jit(solution)/shard_map/ppermute | solution.py:324
  421.0 11.9 %collective-permute-done.15 = bf16[256,1024]{1,0:T(8,128)(2,1)} collective-permute-done((bf16[256,1024]{1,0:T(8,128)(2,1)S(1)}, bf16[256,1024]{1,0:T(8,128)(2,1)}, u32[]{:S(2)}, u32[]{:S(2)}) %collective-permute-start.15) | collective-permute-done | bytes 524320 | tf_op jit(solution)/shard_map/ppermute | solution.py:324
  438.0 13.1 %attend_backward.1 = (bf16[512,1536]{1,0:T(8,128)(2,1)}, f32[4,2,1024]{2,1,0:T(2,128)}) custom-call(s32[1]{0:T(128)} %dynamic_slice.84.length_ref, bf16[512,1536]{1,0:T(8,128)(2,1)} %convolution_convert_fusion.4.joined_ref, bf16[512,512]{1,0:T(8,128)(2,1)} %convolution_convert_fusion.7.grad_ref, f32[4,2,512]{2,1,0:T(2,128)} %get-tuple-element.67.total_ref, ...), custom_call_target="tpu_custom_call" | custom-call | flops 5368709120 | bytes 3670016 | tf_op jit(solution)/shard_map/attend_backward/pallas_call | solution.py:201
  486.8 40.7 %collective-permute-done.19 = bf16[264,2048]{1,0:T(8,128)(2,1)} collective-permute-done((bf16[264,2048]{1,0:T(8,128)(2,1)}, bf16[264,2048]{1,0:T(8,128)(2,1)}, u32[]{:S(2)}, u32[]{:S(2)}) %collective-permute-start.19) | collective-permute-done | bytes 1081376 | tf_op jit(solution)/shard_map/ppermute | solution.py:574
  534.8 39.7 %all-to-all-done.5 = bf16[16,64,3392]{2,1,0:T(8,128)(2,1)} async-done(((bf16[16,64,3392]{2,1,0:T(8,128)(2,1)}), bf16[16,64,3392]{2,1,0:T(8,128)(2,1)}, u32[]{:S(2)}, u32[]{:S(2)}) %all-to-all-start.5) | async-done | bytes 6946848 | tf_op jit(solution)/shard_map/all_to_all | solution.py:345
  579.7 8.6 %slice_convert_fusion = (f32[16,64,1408]{2,1,0:T(8,128)}, f32[16,64,1408]{2,1,0:T(8,128)}) fusion(bf16[16,64,3392]{2,1,0:T(8,128)(2,1)} %all-to-all-done.5), kind=kLoop, calls=%fused_computation.28 | loop fusion | flops 2883584 | bytes 17301504 | tf_op jit(solution)/shard_map/convert_element_type | solution.py:376
  (250 shorter events, 177.9 us)
Async XLA Ops:
  1.7 21.3 %collective-permute-start.2 = (bf16[272,512]{1,0:T(8,128)(2,1)S(1)}, bf16[272,512]{1,0:T(8,128)(2,1)S(1)}, u32[]{:S(2)}, u32[]{:S(2)}) collective-permute-start(bf16[272,512]{1,0:T(8,128)(2,1)S(1)} %get-tuple-element.106), channel_id=1, source_target_pairs={{0,8},{2,10},{4,12},{6,14},{8,0},{10,2},{12,4},{14,6},{16,24},{18,... | collective-permute-start | bytes 835592 | tf_op jit(solution)/shard_map/ppermute | solution.py:426
  3.3 19.7 %collective-permute-start.3 = (bf16[272,512]{1,0:T(8,128)(2,1)S(1)}, bf16[272,512]{1,0:T(8,128)(2,1)S(1)}, u32[]{:S(2)}, u32[]{:S(2)}) collective-permute-start(bf16[272,512]{1,0:T(8,128)(2,1)S(1)} %get-tuple-element.106), channel_id=1, source_target_pairs={{0,16},{2,18},{4,20},{6,22},{8,24},{10,26},{12,28},{14,30},{16,0},... | collective-permute-start | bytes 835592 | tf_op jit(solution)/shard_map/ppermute | solution.py:426
  3.7 25.6 %collective-permute-start.4 = (bf16[272,512]{1,0:T(8,128)(2,1)S(1)}, bf16[272,512]{1,0:T(8,128)(2,1)S(1)}, u32[]{:S(2)}, u32[]{:S(2)}) collective-permute-start(bf16[272,512]{1,0:T(8,128)(2,1)S(1)} %get-tuple-element.106), channel_id=1, source_target_pairs={{0,24},{2,26},{4,28},{6,30},{8,16},{10,18},{12,20},{14,22},{16,8},... | collective-permute-start | bytes 835592 | tf_op jit(solution)/shard_map/ppermute | solution.py:426
  29.3 159.7 %all-to-all-start = ((bf16[16,64,3392]{2,1,0:T(8,128)(2,1)}), bf16[16,64,3392]{2,1,0:T(8,128)(2,1)}, u32[]{:S(2)}, u32[]{:S(2)}) async-start(bf16[16,64,3392]{2,1,0:T(8,128)(2,1)} %pad_maximum_fusion), calls=%async_computation | async-start | bytes 14155776 | tf_op jit(solution)/shard_map/all_to_all | solution.py:345
  34.6 71.9 %collective-permute-start.6 = (bf16[4,272,512]{2,1,0:T(8,128)(2,1)S(1)}, bf16[4,272,512]{2,1,0:T(8,128)(2,1)}, u32[]{:S(2)}, u32[]{:S(2)}) collective-permute-start(bf16[4,272,512]{2,1,0:T(8,128)(2,1)S(1)} %pad_maximum_fusion.4.refs_0_), channel_id=1, source_target_pairs={{0,4},{2,6},{4,0},{6,2},{8,12},{10,14},{12,8},{14,10},{16,20},{18,... | collective-permute-start | bytes 3342344 | tf_op jit(solution)/shard_map/ppermute | solution.py:431
  36.1 85.1 %collective-permute-start.5 = (bf16[4,272,512]{2,1,0:T(8,128)(2,1)S(1)}, bf16[4,272,512]{2,1,0:T(8,128)(2,1)}, u32[]{:S(2)}, u32[]{:S(2)}) collective-permute-start(bf16[4,272,512]{2,1,0:T(8,128)(2,1)S(1)} %pad_maximum_fusion.4.refs_0_), channel_id=1, source_target_pairs={{0,2},{2,0},{4,6},{6,4},{8,10},{10,8},{12,14},{14,12},{16,18},{18,... | collective-permute-start | bytes 3342344 | tf_op jit(solution)/shard_map/ppermute | solution.py:433
  106.5 14.8 %collective-permute-start.7 = (bf16[4,272,512]{2,1,0:T(8,128)(2,1)}, bf16[4,272,512]{2,1,0:T(8,128)(2,1)}, u32[]{:S(2)}, u32[]{:S(2)}) collective-permute-start(bf16[4,272,512]{2,1,0:T(8,128)(2,1)} %collective-permute-done.6.refs_2_), channel_id=1, source_target_pairs={{0,2},{2,0},{4,6},{6,4},{8,10},{10,8},{12,14},{14,12},{16,18},{18,... | collective-permute-start | bytes 3342344 | tf_op jit(solution)/shard_map/ppermute | solution.py:433
  106.5 14.3 %collective-permute-start.1 = (bf16[256,1024]{1,0:T(8,128)(2,1)S(1)}, bf16[256,1024]{1,0:T(8,128)(2,1)S(1)}, u32[]{:S(2)}, u32[]{:S(2)}) collective-permute-start(bf16[256,1024]{1,0:T(8,128)(2,1)S(1)} %copy-done.3), channel_id=1, source_target_pairs={{0,1},{1,0},{2,3},{3,2},{4,5},{5,4},{6,7},{7,6},{8,9},{9,8},{10,11... | collective-permute-start | bytes 1572872 | tf_op jit(solution)/shard_map/ppermute | solution.py:324
  151.7 13.7 %collective-permute-start.8 = (bf16[256,1024]{1,0:T(8,128)(2,1)S(1)}, bf16[256,1024]{1,0:T(8,128)(2,1)S(1)}, u32[]{:S(2)}, u32[]{:S(2)}) collective-permute-start(bf16[256,1024]{1,0:T(8,128)(2,1)S(1)} %dynamic-slice_convert_fusion.3), channel_id=1, source_target_pairs={{0,1},{1,0},{2,3},{3,2},{4,5},{5,4},{6,7},{7,6},{8,9},{9,8},{10,11... | collective-permute-start | bytes 1572872 | tf_op jit(solution)/shard_map/ppermute | solution.py:324
  192.6 33.1 %all-to-all-start.1 = ((bf16[16,72,512]{2,1,0:T(8,128)(2,1)}), bf16[16,72,512]{2,1,0:T(8,128)(2,1)S(1)}, u32[]{:S(2)}, u32[]{:S(2)}) async-start(bf16[16,72,512]{2,1,0:T(8,128)(2,1)} %bitcast.112), calls=%async_computation.1 | async-start | bytes 2359296 | tf_op jit(solution)/shard_map/all_to_all | solution.py:345
  197.3 28.3 %collective-permute-start.10 = (bf16[1152,512]{1,0:T(8,128)(2,1)}, bf16[1152,512]{1,0:T(8,128)(2,1)}, u32[]{:S(2)}, u32[]{:S(2)}) collective-permute-start(bf16[1152,512]{1,0:T(8,128)(2,1)} %bitcast.109), channel_id=1, source_target_pairs={{0,1},{1,0},{2,3},{3,2},{4,5},{5,4},{6,7},{7,6},{8,9},{9,8},{10,11... | collective-permute-start | bytes 3538952 | tf_op jit(solution)/shard_map/ppermute | solution.py:324
  225.7 70.8 %all-to-all-start.2 = ((bf16[16,64,1408]{2,1,0:T(8,128)(2,1)}), bf16[16,64,1408]{2,1,0:T(8,128)(2,1)}, u32[]{:S(2)}, u32[]{:S(2)}) async-start(bf16[16,64,1408]{2,1,0:T(8,128)(2,1)} %param.25), calls=%async_computation.2 | async-start | bytes 5767168 | tf_op jit(solution)/shard_map/all_to_all | solution.py:345
  232.1 28.1 %collective-permute-start.11 = (bf16[1152,512]{1,0:T(8,128)(2,1)S(1)}, bf16[1152,512]{1,0:T(8,128)(2,1)S(1)}, u32[]{:S(2)}, u32[]{:S(2)}) collective-permute-start(bf16[1152,512]{1,0:T(8,128)(2,1)S(1)} %bitcast.106), channel_id=1, source_target_pairs={{0,1},{1,0},{2,3},{3,2},{4,5},{5,4},{6,7},{7,6},{8,9},{9,8},{10,11... | collective-permute-start | bytes 3538952 | tf_op jit(solution)/shard_map/ppermute | solution.py:324
  296.5 69.3 %all-to-all-start.3 = ((bf16[16,64,1408]{2,1,0:T(8,128)(2,1)}), bf16[16,64,1408]{2,1,0:T(8,128)(2,1)}, u32[]{:S(2)}, u32[]{:S(2)}) async-start(bf16[16,64,1408]{2,1,0:T(8,128)(2,1)} %bitcast.104), calls=%async_computation.3 | async-start | bytes 5767168 | tf_op jit(solution)/shard_map/all_to_all | solution.py:345
  332.7 28.0 %collective-permute-start.12 = (bf16[1152,512]{1,0:T(8,128)(2,1)S(1)}, bf16[1152,512]{1,0:T(8,128)(2,1)S(1)}, u32[]{:S(2)}, u32[]{:S(2)}) collective-permute-start(bf16[1152,512]{1,0:T(8,128)(2,1)S(1)} %dynamic-slice_convert_fusion.1), channel_id=1, source_target_pairs={{0,1},{1,0},{2,3},{3,2},{4,5},{5,4},{6,7},{7,6},{8,9},{9,8},{10,11... | collective-permute-start | bytes 3538952 | tf_op jit(solution)/shard_map/ppermute | solution.py:324
  360.7 36.1 %collective-permute-start.13 = (bf16[1152,512]{1,0:T(8,128)(2,1)}, bf16[1152,512]{1,0:T(8,128)(2,1)S(1)}, u32[]{:S(2)}, u32[]{:S(2)}) collective-permute-start(bf16[1152,512]{1,0:T(8,128)(2,1)} %dynamic-slice_convert_fusion), channel_id=1, source_target_pairs={{0,1},{1,0},{2,3},{3,2},{4,5},{5,4},{6,7},{7,6},{8,9},{9,8},{10,11... | collective-permute-start | bytes 3538952 | tf_op jit(solution)/shard_map/ppermute | solution.py:324
  365.8 34.7 %all-to-all-start.4 = ((bf16[16,72,512]{2,1,0:T(8,128)(2,1)}), bf16[16,72,512]{2,1,0:T(8,128)(2,1)}, u32[]{:S(2)}, u32[]{:S(2)}) async-start(bf16[16,72,512]{2,1,0:T(8,128)(2,1)} %bitcast.25), calls=%async_computation.4 | async-start | bytes 2359296 | tf_op jit(solution)/shard_map/all_to_all | solution.py:345
  400.6 173.9 %all-to-all-start.5 = ((bf16[16,64,3392]{2,1,0:T(8,128)(2,1)}), bf16[16,64,3392]{2,1,0:T(8,128)(2,1)}, u32[]{:S(2)}, u32[]{:S(2)}) async-start(bf16[16,64,3392]{2,1,0:T(8,128)(2,1)} %maximum_dynamic-update-slice_fusion), calls=%async_computation.5 | async-start | bytes 14155776 | tf_op jit(solution)/shard_map/all_to_all | solution.py:345
  419.5 13.4 %collective-permute-start.15 = (bf16[256,1024]{1,0:T(8,128)(2,1)S(1)}, bf16[256,1024]{1,0:T(8,128)(2,1)}, u32[]{:S(2)}, u32[]{:S(2)}) collective-permute-start(bf16[256,1024]{1,0:T(8,128)(2,1)S(1)} %get-tuple-element.89), channel_id=1, source_target_pairs={{0,1},{1,0},{2,3},{3,2},{4,5},{5,4},{6,7},{7,6},{8,9},{9,8},{10,11... | collective-permute-start | bytes 1572872 | tf_op jit(solution)/shard_map/ppermute | solution.py:324
  468.4 14.6 %collective-permute-start.20 = (bf16[256,1024]{1,0:T(8,128)(2,1)}, bf16[256,1024]{1,0:T(8,128)(2,1)}, u32[]{:S(2)}, u32[]{:S(2)}) collective-permute-start(bf16[256,1024]{1,0:T(8,128)(2,1)} %dynamic-slice_convert_fusion.2), channel_id=1, source_target_pairs={{0,1},{1,0},{2,3},{3,2},{4,5},{5,4},{6,7},{7,6},{8,9},{9,8},{10,11... | collective-permute-start | bytes 1572872 | tf_op jit(solution)/shard_map/ppermute | solution.py:324
  474.2 53.4 %collective-permute-start.19 = (bf16[264,2048]{1,0:T(8,128)(2,1)}, bf16[264,2048]{1,0:T(8,128)(2,1)}, u32[]{:S(2)}, u32[]{:S(2)}) collective-permute-start(bf16[264,2048]{1,0:T(8,128)(2,1)} %pad_maximum_fusion.5), channel_id=1, source_target_pairs={{0,4},{2,6},{4,0},{6,2},{8,12},{10,14},{12,8},{14,10},{16,20},{18,... | collective-permute-start | bytes 3244040 | tf_op jit(solution)/shard_map/ppermute | solution.py:574
  531.2 58.1 %collective-permute-start.22 = (bf16[72,2048]{1,0:T(8,128)(2,1)S(1)}, bf16[72,2048]{1,0:T(8,128)(2,1)}, u32[]{:S(2)}, u32[]{:S(2)}) collective-permute-start(bf16[72,2048]{1,0:T(8,128)(2,1)S(1)} %get-tuple-element.109), channel_id=1, source_target_pairs={{0,8},{2,10},{4,12},{6,14},{8,0},{10,2},{12,4},{14,6},{16,24},{18,... | collective-permute-start | bytes 884744 | tf_op jit(solution)/shard_map/ppermute | solution.py:574
  531.3 58.0 %collective-permute-start.23 = (bf16[72,2048]{1,0:T(8,128)(2,1)S(1)}, bf16[72,2048]{1,0:T(8,128)(2,1)}, u32[]{:S(2)}, u32[]{:S(2)}) collective-permute-start(bf16[72,2048]{1,0:T(8,128)(2,1)S(1)} %get-tuple-element.108), channel_id=1, source_target_pairs={{0,16},{2,18},{4,20},{6,22},{8,24},{10,26},{12,28},{14,30},{16,0},... | collective-permute-start | bytes 884744 | tf_op jit(solution)/shard_map/ppermute | solution.py:574
  533.6 55.7 %collective-permute-start.24 = (bf16[72,2048]{1,0:T(8,128)(2,1)S(1)}, bf16[72,2048]{1,0:T(8,128)(2,1)}, u32[]{:S(2)}, u32[]{:S(2)}) collective-permute-start(bf16[72,2048]{1,0:T(8,128)(2,1)S(1)} %get-tuple-element.107), channel_id=1, source_target_pairs={{0,24},{2,26},{4,28},{6,30},{8,16},{10,18},{12,20},{14,22},{16,8},... | collective-permute-start | bytes 884744 | tf_op jit(solution)/shard_map/ppermute | solution.py:574
  (43 other events, 675.4 us)

commit v4 on v3

--- a/solution.py
+++ b/solution.py
@@ -15,6 +15,7 @@
 GELU_SCALE = 0.7978845608028654
 GELU_CUBIC = 0.044715
 GAIN_ROWS = 16
+VMEM_BYTES = 48 * 2**20
 
 
 def dot_nt(left, right):
@@ -284,6 +285,146 @@
     return gelu, slope
 
 
+def expert_forward_kernel(
+    side_ref, near_ref, far_ref, gate_near, up_near, gate_far, up_far, hidden_ref, slope_ref, gelu_ref
+):
+    near = near_ref[...]
+    far = far_ref[...]
+    gate_pre = dot_nn(near, gate_near[...]) + dot_nn(far, gate_far[...])
+    up_pre = dot_nn(near, up_near[...]) + dot_nn(far, up_far[...])
+    gelu, slope = gelu_parts(gate_pre)
+    hidden_ref[...] = (gelu * up_pre).astype(jnp.bfloat16)
+    slope_ref[...] = slope * up_pre
+    gelu_ref[...] = gelu
+
+
+def slot_block(slots):
+    return 288 if slots % 288 == 0 else slots
+
+
+def expert_forward(side, near, far, weights, hidden_cols):
+    slots, half = near.shape
+    rows = slot_block(slots)
+    row_spec = pl.BlockSpec((rows, half), lambda i, side_ref: (i, 0))
+    wide_spec = pl.BlockSpec((rows, hidden_cols), lambda i, side_ref: (i, 0))
+
+    def weight_spec(other, column):
+        return pl.BlockSpec(
+            (half, hidden_cols),
+            lambda i, side_ref: (side_ref[0] ^ other, column),
+            pipeline_mode=pl.Buffered(1),
+        )
+
+    return pl.pallas_call(
+        expert_forward_kernel,
+        grid_spec=pltpu.PrefetchScalarGridSpec(
+            num_scalar_prefetch=1,
+            grid=(slots // rows,),
+            in_specs=[
+                row_spec,
+                row_spec,
+                weight_spec(0, 0),
+                weight_spec(0, 1),
+                weight_spec(1, 0),
+                weight_spec(1, 1),
+            ],
+            out_specs=[wide_spec] * 3,
+        ),
+        out_shape=[
+            jax.ShapeDtypeStruct((slots, hidden_cols), jnp.bfloat16),
+            jax.ShapeDtypeStruct((slots, hidden_cols), jnp.float32),
+            jax.ShapeDtypeStruct((slots, hidden_cols), jnp.float32),
+        ],
+        compiler_params=pltpu.CompilerParams(vmem_limit_bytes=VMEM_BYTES),
+        cost_estimate=pl.CostEstimate(
+            flops=8 * slots * half * hidden_cols,
+            transcendentals=slots * hidden_cols,
+            bytes_accessed=10 * slots * hidden_cols + 8 * half * hidden_cols,
+        ),
+        name="expert_forward",
+    )(side, near, far, weights, weights, weights, weights)
+
+
+def expert_backward_kernel(
+    side_ref,
+    near_ref,
+    far_ref,
+    slope_ref,
+    gelu_ref,
+    down_near,
+    down_far,
+    gate_near,
+    up_near,
+    gate_far,
+    up_far,
+    pre_grad_ref,
+    stay_ref,
+    away_ref,
+):
+    cols = slope_ref.shape[1]
+    hidden_grad = dot_nn(near_ref[...], down_near[...]) + dot_nn(far_ref[...], down_far[...])
+    gate_grad = (hidden_grad * slope_ref[...]).astype(jnp.bfloat16)
+    up_grad = (hidden_grad * gelu_ref[...]).astype(jnp.bfloat16)
+    pre_grad_ref[:, :cols] = gate_grad
+    pre_grad_ref[:, cols:] = up_grad
+    away_ref[...] = (dot_nt(gate_grad, gate_far[...]) + dot_nt(up_grad, up_far[...])).astype(
+        jnp.bfloat16
+    )
+    stay_ref[...] = dot_nt(gate_grad, gate_near[...]) + dot_nt(up_grad, up_near[...])
+
+
+def expert_backward(side, near, far, slope, gelu, down, weights):
+    slots, half = near.shape
+    hidden_cols = slope.shape[1]
+    rows = slot_block(slots)
+    row_spec = pl.BlockSpec((rows, half), lambda i, side_ref: (i, 0))
+    wide_spec = pl.BlockSpec((rows, hidden_cols), lambda i, side_ref: (i, 0))
+
+    def weight_spec(other, column):
+        return pl.BlockSpec(
+            (half, hidden_cols),
+            lambda i, side_ref: (side_ref[0] ^ other, column),
+            pipeline_mode=pl.Buffered(1),
+        )
+
+    return pl.pallas_call(
+        expert_backward_kernel,
+        grid_spec=pltpu.PrefetchScalarGridSpec(
+            num_scalar_prefetch=1,
+            grid=(slots // rows,),
+            in_specs=[
+                row_spec,
+                row_spec,
+                wide_spec,
+                wide_spec,
+                weight_spec(0, 0),
+                weight_spec(1, 0),
+                weight_spec(0, 0),
+                weight_spec(0, 1),
+                weight_spec(1, 0),
+                weight_spec(1, 1),
+            ],
+            out_specs=[
+                pl.BlockSpec((rows, 2 * hidden_cols), lambda i, side_ref: (i, 0)),
+                row_spec,
+                row_spec,
+            ],
+        ),
+        out_shape=[
+            jax.ShapeDtypeStruct((slots, 2 * hidden_cols), jnp.bfloat16),
+            jax.ShapeDtypeStruct((slots, half), jnp.float32),
+            jax.ShapeDtypeStruct((slots, half), jnp.bfloat16),
+        ],
+        compiler_params=pltpu.CompilerParams(vmem_limit_bytes=VMEM_BYTES),
+        cost_estimate=pl.CostEstimate(
+            flops=12 * slots * half * hidden_cols,
+            transcendentals=0,
+            bytes_accessed=12 * slots * hidden_cols + 12 * half * hidden_cols,
+        ),
+        name="expert_backward",
+    )(side, near, far, slope, gelu, down, down, weights, weights, weights, weights)
+
+
 def on_device(
     tokens,
     cotangent,
@@ -481,27 +622,18 @@
         down_weight, (route(expert_rows), slot_grad_other)
     )
     down_all = fetch(down_late)
-    expert_in = ordered(expert_half, swap(expert_half), 1)
+    expert_other = swap(expert_half)
+
+    side = tensor_index[None]
+    hidden, slope, gelu = expert_forward(
+        side, expert_half, expert_other, gate_up_all, hidden_cols
+    )
     slot_grad = ordered(slot_grad_half, slot_grad_other, 1)
-
-    pre = dot_nn(expert_in, gate_up_all)
-    gate_pre = pre[:, :hidden_cols]
-    up_pre = pre[:, hidden_cols : 2 * hidden_cols]
-    gelu, slope = gelu_parts(gate_pre)
-    hidden = lax.optimization_barrier((gelu * up_pre).astype(jnp.bfloat16))
     down_grad, down_all = chain(dot_tn(slot_grad, hidden).astype(jnp.bfloat16), down_all)
     down_back = send_grad(down_grad)
-    hidden_grad = dot_nn(slot_grad, down_all)
-    pre_grad = jnp.concatenate(
-        [
-            (hidden_grad * up_pre * slope).astype(jnp.bfloat16),
-            (hidden_grad * gelu).astype(jnp.bfloat16),
-            jnp.zeros((total_slots, half + half // fold), jnp.bfloat16),
-        ],
-        axis=1,
-    )
-    slot_back_part = dot_nt(pre_grad, gate_up_all)
-    slot_back_away = other_part(slot_back_part, 1).astype(jnp.bfloat16)
+    pre_grad, slot_back_stay, slot_back_away = expert_backward(
+        side, slot_grad_half, slot_grad_other, slope, gelu, down_all, gate_up_all
+    )
     hidden_late, slot_back_away = chain(hidden, slot_back_away)
     slot_back_other = swap(slot_back_away)
     expert_out_part = dot_nt(hidden_late, down_all)
@@ -509,19 +641,21 @@
         other_part(expert_out_part, 1).astype(jnp.bfloat16), slot_back_other
     )
     slot_back_half = (
-        own_part(slot_back_part, 1) + slot_back_other.astype(jnp.float32)
+        slot_back_stay + slot_back_other.astype(jnp.float32)
     ).astype(jnp.bfloat16)
     expert_out_half = (
         own_part(expert_out_part, 1) + swap(expert_out_away).astype(jnp.float32)
     ).astype(jnp.bfloat16)
     slot_back_half, down_back = chain(slot_back_half, down_back)
     last, slot_back = chain(
-        lax.dynamic_update_slice(
-            dot_tn(expert_in, pre_grad)
-            .astype(jnp.bfloat16)
-            .reshape(dp_count, shard_rows, pre_grad.shape[1]),
-            pack(expert_out_half),
-            (0, 0, 2 * hidden_cols),
+        jnp.concatenate(
+            [
+                dot_tn(ordered(expert_half, expert_other, 1), pre_grad)
+                .astype(jnp.bfloat16)
+                .reshape(dp_count, shard_rows, 2 * hidden_cols),
+                pack(expert_out_half),
+            ],
+            axis=2,
         ),
         route(slot_back_half),
     )

time: 606 us -> 602 us (level)
  matrix products: 99.6 us -> 52.1 us
  Pallas kernels: 34.5 us -> 64.7 us
  waiting for transfers between devices: 303 us -> 333 us
  local copies, waits for them, and re-layouts: 41.5 us -> 27.3 us
    pallas_call x0 -> x2, Pallas kernels: none -> 30.2 us  [the longest x1 17.3 us: expert_backward(): pl.pallas_call(expert_backward_kernel, grid_spec=pltpu.PrefetchScalarGrid...]
    dot_general x7 -> x5, matrix products: 40.8 us -> 12 us  [dot_nn(): lax.dot_general(left, right, (((1,), (0,)), ((), ())), preferred_element_...]
    all_to_all x6, waiting for transfers between devices: 60.5 us -> 89.2 us  [exchange(): return lax.all_to_all(block, 'dp', split_axis=0, concat_axis=0, tiled=True)]
    dot_general x4 -> x3, matrix products: 25.6 us -> 11 us  [dot_nt(): lax.dot_general(left, right, (((1,), (1,)), ((), ())), preferred_element_...]
    convert_element_type x2 -> x0, local copies, waits for them, and re-layouts: 9.84 us -> none  [the longest x1 9.66 us: on_device(): last, slot_back = chain(lax.dynamic_update_slice(dot_tn(expert_in, pre_gr...]
  transfers between devices with their start and end apart: 31 -> 31, of which waited for: 18 -> 19; matrix products, arithmetic and copies ran while one was open for 29% -> 19% of each run, Pallas kernels for 6% -> 11%
where the time goes in v4:
time: 602 us; the launch traced here: 592 us
  waiting for transfers between devices  333 us (55%)
  Pallas kernels  64.7 us (11%)
  starting transfers between devices  60.8 us (10%)
  matrix products  52.1 us (9%)
  other arithmetic  51.8 us (9%)
  local copies, waits for them, and re-layouts  27.3 us (5%)
    ppermute x13, waiting for transfers between devices, swap(): return lax.ppermute(block, 'tensor', [(0, 1), (1, 0)])  128 us
    all_to_all x6, waiting for transfers between devices, exchange(): return lax.all_to_all(block, 'dp', split_axis=0, concat_axis=0, tiled=True)  89.2 us
    ppermute x1, waiting for transfers between devices, on_device(): side = lax.ppermute(near, 'dp', [(i, i ^ 2) for i in range(16)])  70.3 us
    ppermute x6, waiting for transfers between devices, partner(): return lax.ppermute(block, 'dp', [(i, i ^ offset) for i in range(dp_count)])  40.5 us
    all_to_all x6, starting transfers between devices, exchange(): return lax.all_to_all(block, 'dp', split_axis=0, concat_axis=0, tiled=True)  30.8 us
    dot_general x6, matrix products, dot_tn(): lax.dot_general(left, right, (((0,), (0,)), ((), ())), preferred_element_...  28.8 us
    ppermute x13, starting transfers between devices, swap(): return lax.ppermute(block, 'tensor', [(0, 1), (1, 0)])  19.8 us
    pallas_call x1, Pallas kernels, expert_backward(): pl.pallas_call(expert_backward_kernel, grid_spec=pltpu.PrefetchScalarGrid...  17.3 us
  transfers between devices with their start and end apart: 31, of which 19 were waited for; matrix products, arithmetic and copies ran while one was open for 19% of the time, Pallas kernels for 11%

profile of v4, /device:TPU:16, one launch (start us, length us, event | category | flops | bytes accessed | tf_op | source)
XLA Modules:
  0.0 591.6 jit_solution(18361233103849068300)
XLA Ops:
  36.2 70.3 %collective-permute-done.6.refs_2_ = bf16[4,272,512]{2,1,0:T(8,128)(2,1)S(1)} collective-permute-done((bf16[4,272,512]{2,1,0:T(8,128)(2,1)S(1)}, bf16[4,272,512]{2,1,0:T(8,128)(2,1)S(1)}, u32[]{:S(2)}, u32[]{:S(2)}) %collective-permute-start.6) | collective-permute-done | bytes 1114144 | tf_op jit(solution)/shard_map/ppermute | solution.py:572
  109.6 11.2 %collective-permute-done.1 = bf16[256,1024]{1,0:T(8,128)(2,1)S(1)} collective-permute-done((bf16[256,1024]{1,0:T(8,128)(2,1)S(1)}, bf16[256,1024]{1,0:T(8,128)(2,1)S(1)}, u32[]{:S(2)}, u32[]{:S(2)}) %collective-permute-start.1) | collective-permute-done | bytes 524320 | tf_op jit(solution)/shard_map/ppermute | solution.py:465
  121.3 10.2 %assemble.1 = (bf16[1024,1536]{1,0:T(8,128)(2,1)}, bf16[1024,512]{1,0:T(8,128)(2,1)}, bf16[16,16,512]{2,1,0:T(8,128)(2,1)}) custom-call(s32[2]{0:T(128)} %pad_add_fusion.1.place_ref, bf16[4,272,512]{2,1,0:T(8,128)(2,1)} %copy-done.10, bf16[4,272,512]{2,1,0:T(8,128)(2,1)} %collective-permute-done.5.refs_1_, bf16[4,272,512]{2,1,0:T(8,128)(2,1)} %copy-done.16, ...), custom_call_target="tpu_custom_call" | custom-call | tf_op jit(solution)/shard_map/assemble/pallas_call | solution.py:256
  137.4 11.0 %attend_forward.1 = (bf16[512,512]{1,0:T(8,128)(2,1)}, f32[4,2,512]{2,1,0:T(2,128)}) custom-call(s32[1]{0:T(128)} %dynamic_slice.78.length_ref, bf16[512,1536]{1,0:T(8,128)(2,1)} %convolution_convert_fusion.4.joined_ref, f32[4,2,1024]{2,1,0:T(2,128)} %reshape.217.bias_ref), custom_call_target="tpu_custom_call" | custom-call | flops 2147483648 | bytes 2097152 | tf_op jit(solution)/shard_map/attend_forward/pallas_call | solution.py:104
  152.2 12.2 %collective-permute-done.8 = bf16[256,1024]{1,0:T(8,128)(2,1)} collective-permute-done((bf16[256,1024]{1,0:T(8,128)(2,1)S(1)}, bf16[256,1024]{1,0:T(8,128)(2,1)}, u32[]{:S(2)}, u32[]{:S(2)}) %collective-permute-start.8) | collective-permute-done | bytes 524320 | tf_op jit(solution)/shard_map/ppermute | solution.py:465
  176.7 12.3 %all-to-all-done = bf16[16,64,3392]{2,1,0:T(8,128)(2,1)} async-done(((bf16[16,64,3392]{2,1,0:T(8,128)(2,1)}), bf16[16,64,3392]{2,1,0:T(8,128)(2,1)}, u32[]{:S(2)}, u32[]{:S(2)}) %all-to-all-start) | async-done | bytes 6946848 | tf_op jit(solution)/shard_map/all_to_all | solution.py:486
  197.9 26.6 %collective-permute-done.10.far_ref = bf16[1152,512]{1,0:T(8,128)(2,1)} collective-permute-done((bf16[1152,512]{1,0:T(8,128)(2,1)S(1)}, bf16[1152,512]{1,0:T(8,128)(2,1)}, u32[]{:S(2)}, u32[]{:S(2)}) %collective-permute-start.10) | collective-permute-done | bytes 1179680 | tf_op jit(solution)/shard_map/ppermute | solution.py:465
  224.5 6.3 %all-to-all-start.2 = ((bf16[16,64,1408]{2,1,0:T(8,128)(2,1)}), bf16[16,64,1408]{2,1,0:T(8,128)(2,1)}, u32[]{:S(2)}, u32[]{:S(2)}) async-start(bf16[16,64,1408]{2,1,0:T(8,128)(2,1)} %param.25), calls=%async_computation.2 | async-start | bytes 5767168 | tf_op jit(solution)/shard_map/all_to_all | solution.py:486
  232.4 26.5 %collective-permute-done.11.far_ref = bf16[1152,512]{1,0:T(8,128)(2,1)S(1)} collective-permute-done((bf16[1152,512]{1,0:T(8,128)(2,1)S(1)}, bf16[1152,512]{1,0:T(8,128)(2,1)S(1)}, u32[]{:S(2)}, u32[]{:S(2)}) %collective-permute-start.11) | collective-permute-done | bytes 1179680 | tf_op jit(solution)/shard_map/ppermute | solution.py:465
  258.9 12.9 %expert_forward.1 = (bf16[1152,1408]{1,0:T(8,128)(2,1)S(1)}, f32[1152,1408]{1,0:T(8,128)}, f32[1152,1408]{1,0:T(8,128)}) custom-call(s32[1]{0:T(128)} %bitcast.18.side_ref, bf16[1152,512]{1,0:T(8,128)(2,1)S(1)} %bitcast.95, bf16[1152,512]{1,0:T(8,128)(2,1)S(1)} %collective-permute-done.11.far_ref, ...), custom_call_target="tpu_custom_call" | custom-call | flops 6643777536 | bytes 21987328 | tf_op jit(solution)/shard_map/expert_forward/pallas_call | solution.py:318
  273.5 7.5 %convolution_convert_fusion.2 = bf16[1024,1408]{1,0:T(8,128)(2,1)} fusion(bf16[1152,1408]{1,0:T(8,128)(2,1)S(1)} %get-tuple-element.70, bf16[1152,512]{1,0:T(8,128)(2,1)} %collective-permute-done.10.far_ref, bf16[1152,512]{1,0:T(8,128)(2,1)S(1)} %bitcast.98, pred[]{:T(512)S(6)} %eq.79), kind=kOutput, calls=%fused_computation.9 | convolution fusion | flops 3333947392 | bytes 8486913 | tf_op jit(solution)/shard_map/dot_general | solution.py:34
  281.0 14.3 %all-to-all-done.2 = bf16[16,64,1408]{2,1,0:T(8,128)(2,1)} async-done(((bf16[16,64,1408]{2,1,0:T(8,128)(2,1)}), bf16[16,64,1408]{2,1,0:T(8,128)(2,1)}, u32[]{:S(2)}, u32[]{:S(2)}) %all-to-all-start.2) | async-done | bytes 2883616 | tf_op jit(solution)/shard_map/all_to_all | solution.py:486
  300.0 17.3 %expert_backward.1 = (bf16[1152,2816]{1,0:T(8,128)(2,1)}, f32[1152,512]{1,0:T(8,128)S(1)}, bf16[1152,512]{1,0:T(8,128)(2,1)S(1)}) custom-call(s32[1]{0:T(128)} %bitcast.18.side_ref, bf16[1152,512]{1,0:T(8,128)(2,1)S(1)} %bitcast.99, bf16[1152,512]{1,0:T(8,128)(2,1)} %collective-permute-done.10.far_ref, f32[1152,1408]{1,0:T(8,128)} %get-tuple-element.63.slope_ref, ...), custom_call_target="tpu_custom_call" | custom-call | flops 9965666304 | bytes 28114944 | tf_op jit(solution)/shard_map/expert_backward/pallas_call | solution.py:390
  326.0 19.4 %collective-permute-done.12 = bf16[1152,512]{1,0:T(8,128)(2,1)S(1)} collective-permute-done((bf16[1152,512]{1,0:T(8,128)(2,1)S(1)}, bf16[1152,512]{1,0:T(8,128)(2,1)S(1)}, u32[]{:S(2)}, u32[]{:S(2)}) %collective-permute-start.12) | collective-permute-done | bytes 1179680 | tf_op jit(solution)/shard_map/ppermute | solution.py:465
  348.3 16.2 %all-to-all-done.3 = bf16[16,64,1408]{2,1,0:T(8,128)(2,1)} async-done(((bf16[16,64,1408]{2,1,0:T(8,128)(2,1)}), bf16[16,64,1408]{2,1,0:T(8,128)(2,1)}, u32[]{:S(2)}, u32[]{:S(2)}) %all-to-all-start.3) | async-done | bytes 2883616 | tf_op jit(solution)/shard_map/all_to_all | solution.py:486
  369.6 12.6 %convolution_convert_fusion = bf16[1024,2816]{1,0:T(8,128)(2,1)} fusion(bf16[1152,2816]{1,0:T(8,128)(2,1)} %get-tuple-element.68, bf16[1152,512]{1,0:T(8,128)(2,1)S(1)} %collective-permute-done.11.far_ref, bf16[1152,512]{1,0:T(8,128)(2,1)S(1)} %bitcast.96, pred[]{:T(512)S(6)} %eq.79), kind=kOutput, calls=%fused_computation.2 | convolution fusion | flops 6657277952 | bytes 14614529 | tf_op jit(solution)/shard_map/dot_general | solution.py:34
  384.8 6.0 %pad_maximum_fusion.1 = bf16[16,64,3392]{2,1,0:T(8,128)(2,1)} fusion(bf16[16,64,64]{2,1,0:T(8,128)(2,1)S(1)} %bitcast.114, bf16[16,64,512]{2,1,0:T(8,128)(2,1)S(1)} %slice.169, bf16[16,64,2816]{2,1,0:T(8,128)(2,1)} %bitcast.104), kind=kLoop, calls=%fused_computation.1 | loop fusion | flops 20840448 | bytes 13893632 | tf_op jit(solution)/shard_map/concatenate | solution.py:651
  390.8 6.7 %all-to-all-done.4 = bf16[16,72,512]{2,1,0:T(8,128)(2,1)} async-done(((bf16[16,72,512]{2,1,0:T(8,128)(2,1)}), bf16[16,72,512]{2,1,0:T(8,128)(2,1)}, u32[]{:S(2)}, u32[]{:S(2)}) %all-to-all-start.4) | async-done | bytes 1179680 | tf_op jit(solution)/shard_map/all_to_all | solution.py:486
  406.2 6.8 %collective-permute-done.14 = bf16[256,512]{1,0:T(8,128)(2,1)S(1)} collective-permute-done((bf16[256,512]{1,0:T(8,128)(2,1)S(1)}, bf16[256,512]{1,0:T(8,128)(2,1)S(1)}, u32[]{:S(2)}, u32[]{:S(2)}) %collective-permute-start.14) | collective-permute-done | bytes 262176 | tf_op jit(solution)/shard_map/ppermute | solution.py:465
  416.5 11.9 %collective-permute-done.15 = bf16[256,1024]{1,0:T(8,128)(2,1)} collective-permute-done((bf16[256,1024]{1,0:T(8,128)(2,1)S(1)}, bf16[256,1024]{1,0:T(8,128)(2,1)}, u32[]{:S(2)}, u32[]{:S(2)}) %collective-permute-start.15) | collective-permute-done | bytes 524320 | tf_op jit(solution)/shard_map/ppermute | solution.py:465
  433.4 13.3 %attend_backward.1 = (bf16[512,1536]{1,0:T(8,128)(2,1)}, f32[4,2,1024]{2,1,0:T(2,128)}) custom-call(s32[1]{0:T(128)} %dynamic_slice.78.length_ref, bf16[512,1536]{1,0:T(8,128)(2,1)} %convolution_convert_fusion.4.joined_ref, bf16[512,512]{1,0:T(8,128)(2,1)} %convolution_convert_fusion.7.grad_ref, f32[4,2,512]{2,1,0:T(2,128)} %get-tuple-element.79.total_ref, ...), custom_call_target="tpu_custom_call" | custom-call | flops 5368709120 | bytes 3670016 | tf_op jit(solution)/shard_map/attend_backward/pallas_call | solution.py:202
  482.6 40.5 %collective-permute-done.19 = bf16[264,2048]{1,0:T(8,128)(2,1)} collective-permute-done((bf16[264,2048]{1,0:T(8,128)(2,1)}, bf16[264,2048]{1,0:T(8,128)(2,1)}, u32[]{:S(2)}, u32[]{:S(2)}) %collective-permute-start.19) | collective-permute-done | bytes 1081376 | tf_op jit(solution)/shard_map/ppermute | solution.py:708
  530.3 39.7 %all-to-all-done.5 = bf16[16,64,3392]{2,1,0:T(8,128)(2,1)} async-done(((bf16[16,64,3392]{2,1,0:T(8,128)(2,1)}), bf16[16,64,3392]{2,1,0:T(8,128)(2,1)}, u32[]{:S(2)}, u32[]{:S(2)}) %all-to-all-start.5) | async-done | bytes 6946848 | tf_op jit(solution)/shard_map/all_to_all | solution.py:486
  575.2 8.6 %slice_convert_fusion = (f32[16,64,1408]{2,1,0:T(8,128)}, f32[16,64,1408]{2,1,0:T(8,128)}) fusion(bf16[16,64,3392]{2,1,0:T(8,128)(2,1)} %all-to-all-done.5), kind=kLoop, calls=%fused_computation.13 | loop fusion | flops 2883584 | bytes 17301504 | tf_op jit(solution)/shard_map/convert_element_type | solution.py:517
  (256 shorter events, 169.1 us)
Async XLA Ops:
  1.7 22.4 %collective-permute-start.2 = (bf16[272,512]{1,0:T(8,128)(2,1)S(1)}, bf16[272,512]{1,0:T(8,128)(2,1)S(1)}, u32[]{:S(2)}, u32[]{:S(2)}) collective-permute-start(bf16[272,512]{1,0:T(8,128)(2,1)S(1)} %get-tuple-element.116), channel_id=1, source_target_pairs={{0,8},{2,10},{4,12},{6,14},{8,0},{10,2},{12,4},{14,6},{16,24},{18,... | collective-permute-start | bytes 835592 | tf_op jit(solution)/shard_map/ppermute | solution.py:567
  3.3 20.7 %collective-permute-start.3 = (bf16[272,512]{1,0:T(8,128)(2,1)S(1)}, bf16[272,512]{1,0:T(8,128)(2,1)S(1)}, u32[]{:S(2)}, u32[]{:S(2)}) collective-permute-start(bf16[272,512]{1,0:T(8,128)(2,1)S(1)} %get-tuple-element.116), channel_id=1, source_target_pairs={{0,16},{2,18},{4,20},{6,22},{8,24},{10,26},{12,28},{14,30},{16,0},... | collective-permute-start | bytes 835592 | tf_op jit(solution)/shard_map/ppermute | solution.py:567
  3.7 25.6 %collective-permute-start.4 = (bf16[272,512]{1,0:T(8,128)(2,1)S(1)}, bf16[272,512]{1,0:T(8,128)(2,1)S(1)}, u32[]{:S(2)}, u32[]{:S(2)}) collective-permute-start(bf16[272,512]{1,0:T(8,128)(2,1)S(1)} %get-tuple-element.116), channel_id=1, source_target_pairs={{0,24},{2,26},{4,28},{6,30},{8,16},{10,18},{12,20},{14,22},{16,8},... | collective-permute-start | bytes 835592 | tf_op jit(solution)/shard_map/ppermute | solution.py:567
  29.3 159.7 %all-to-all-start = ((bf16[16,64,3392]{2,1,0:T(8,128)(2,1)}), bf16[16,64,3392]{2,1,0:T(8,128)(2,1)}, u32[]{:S(2)}, u32[]{:S(2)}) async-start(bf16[16,64,3392]{2,1,0:T(8,128)(2,1)} %pad_maximum_fusion), calls=%async_computation | async-start | bytes 14155776 | tf_op jit(solution)/shard_map/all_to_all | solution.py:486
  34.6 71.8 %collective-permute-start.6 = (bf16[4,272,512]{2,1,0:T(8,128)(2,1)S(1)}, bf16[4,272,512]{2,1,0:T(8,128)(2,1)S(1)}, u32[]{:S(2)}, u32[]{:S(2)}) collective-permute-start(bf16[4,272,512]{2,1,0:T(8,128)(2,1)S(1)} %pad_maximum_fusion.5.refs_0_), channel_id=1, source_target_pairs={{0,4},{2,6},{4,0},{6,2},{8,12},{10,14},{12,8},{14,10},{16,20},{18,... | collective-permute-start | bytes 3342344 | tf_op jit(solution)/shard_map/ppermute | solution.py:572
  36.2 85.1 %collective-permute-start.5 = (bf16[4,272,512]{2,1,0:T(8,128)(2,1)S(1)}, bf16[4,272,512]{2,1,0:T(8,128)(2,1)}, u32[]{:S(2)}, u32[]{:S(2)}) collective-permute-start(bf16[4,272,512]{2,1,0:T(8,128)(2,1)S(1)} %pad_maximum_fusion.5.refs_0_), channel_id=1, source_target_pairs={{0,2},{2,0},{4,6},{6,4},{8,10},{10,8},{12,14},{14,12},{16,18},{18,... | collective-permute-start | bytes 3342344 | tf_op jit(solution)/shard_map/ppermute | solution.py:574
  106.5 14.8 %collective-permute-start.7 = (bf16[4,272,512]{2,1,0:T(8,128)(2,1)S(1)}, bf16[4,272,512]{2,1,0:T(8,128)(2,1)}, u32[]{:S(2)}, u32[]{:S(2)}) collective-permute-start(bf16[4,272,512]{2,1,0:T(8,128)(2,1)S(1)} %collective-permute-done.6.refs_2_), channel_id=1, source_target_pairs={{0,2},{2,0},{4,6},{6,4},{8,10},{10,8},{12,14},{14,12},{16,18},{18,... | collective-permute-start | bytes 3342344 | tf_op jit(solution)/shard_map/ppermute | solution.py:574
  106.5 14.3 %collective-permute-start.1 = (bf16[256,1024]{1,0:T(8,128)(2,1)S(1)}, bf16[256,1024]{1,0:T(8,128)(2,1)S(1)}, u32[]{:S(2)}, u32[]{:S(2)}) collective-permute-start(bf16[256,1024]{1,0:T(8,128)(2,1)S(1)} %copy-done.7), channel_id=1, source_target_pairs={{0,1},{1,0},{2,3},{3,2},{4,5},{5,4},{6,7},{7,6},{8,9},{9,8},{10,11... | collective-permute-start | bytes 1572872 | tf_op jit(solution)/shard_map/ppermute | solution.py:465
  150.6 13.8 %collective-permute-start.8 = (bf16[256,1024]{1,0:T(8,128)(2,1)S(1)}, bf16[256,1024]{1,0:T(8,128)(2,1)}, u32[]{:S(2)}, u32[]{:S(2)}) collective-permute-start(bf16[256,1024]{1,0:T(8,128)(2,1)S(1)} %dynamic-slice_convert_fusion.2), channel_id=1, source_target_pairs={{0,1},{1,0},{2,3},{3,2},{4,5},{5,4},{6,7},{7,6},{8,9},{9,8},{10,11... | collective-permute-start | bytes 1572872 | tf_op jit(solution)/shard_map/ppermute | solution.py:465
  191.6 32.9 %all-to-all-start.1 = ((bf16[16,72,512]{2,1,0:T(8,128)(2,1)}), bf16[16,72,512]{2,1,0:T(8,128)(2,1)S(1)}, u32[]{:S(2)}, u32[]{:S(2)}) async-start(bf16[16,72,512]{2,1,0:T(8,128)(2,1)} %bitcast.16), calls=%async_computation.1 | async-start | bytes 2359296 | tf_op jit(solution)/shard_map/all_to_all | solution.py:486
  196.4 28.1 %collective-permute-start.10 = (bf16[1152,512]{1,0:T(8,128)(2,1)S(1)}, bf16[1152,512]{1,0:T(8,128)(2,1)}, u32[]{:S(2)}, u32[]{:S(2)}) collective-permute-start(bf16[1152,512]{1,0:T(8,128)(2,1)S(1)} %bitcast.97), channel_id=1, source_target_pairs={{0,1},{1,0},{2,3},{3,2},{4,5},{5,4},{6,7},{7,6},{8,9},{9,8},{10,11... | collective-permute-start | bytes 3538952 | tf_op jit(solution)/shard_map/ppermute | solution.py:465
  224.5 70.8 %all-to-all-start.2 = ((bf16[16,64,1408]{2,1,0:T(8,128)(2,1)}), bf16[16,64,1408]{2,1,0:T(8,128)(2,1)}, u32[]{:S(2)}, u32[]{:S(2)}) async-start(bf16[16,64,1408]{2,1,0:T(8,128)(2,1)} %param.25), calls=%async_computation.2 | async-start | bytes 5767168 | tf_op jit(solution)/shard_map/all_to_all | solution.py:486
  230.8 28.1 %collective-permute-start.11 = (bf16[1152,512]{1,0:T(8,128)(2,1)S(1)}, bf16[1152,512]{1,0:T(8,128)(2,1)S(1)}, u32[]{:S(2)}, u32[]{:S(2)}) collective-permute-start(bf16[1152,512]{1,0:T(8,128)(2,1)S(1)} %bitcast.94), channel_id=1, source_target_pairs={{0,1},{1,0},{2,3},{3,2},{4,5},{5,4},{6,7},{7,6},{8,9},{9,8},{10,11... | collective-permute-start | bytes 3538952 | tf_op jit(solution)/shard_map/ppermute | solution.py:465
  295.3 69.3 %all-to-all-start.3 = ((bf16[16,64,1408]{2,1,0:T(8,128)(2,1)}), bf16[16,64,1408]{2,1,0:T(8,128)(2,1)}, u32[]{:S(2)}, u32[]{:S(2)}) async-start(bf16[16,64,1408]{2,1,0:T(8,128)(2,1)} %bitcast.109), calls=%async_computation.3 | async-start | bytes 5767168 | tf_op jit(solution)/shard_map/all_to_all | solution.py:486
  317.3 28.1 %collective-permute-start.12 = (bf16[1152,512]{1,0:T(8,128)(2,1)S(1)}, bf16[1152,512]{1,0:T(8,128)(2,1)S(1)}, u32[]{:S(2)}, u32[]{:S(2)}) collective-permute-start(bf16[1152,512]{1,0:T(8,128)(2,1)S(1)} %get-tuple-element.71), channel_id=1, source_target_pairs={{0,1},{1,0},{2,3},{3,2},{4,5},{5,4},{6,7},{7,6},{8,9},{9,8},{10,11... | collective-permute-start | bytes 3538952 | tf_op jit(solution)/shard_map/ppermute | solution.py:465
  345.4 36.9 %collective-permute-start.13 = (bf16[1152,512]{1,0:T(8,128)(2,1)}, bf16[1152,512]{1,0:T(8,128)(2,1)S(1)}, u32[]{:S(2)}, u32[]{:S(2)}) collective-permute-start(bf16[1152,512]{1,0:T(8,128)(2,1)} %dynamic-slice_convert_fusion), channel_id=1, source_target_pairs={{0,1},{1,0},{2,3},{3,2},{4,5},{5,4},{6,7},{7,6},{8,9},{9,8},{10,11... | collective-permute-start | bytes 3538952 | tf_op jit(solution)/shard_map/ppermute | solution.py:465
  364.6 33.0 %all-to-all-start.4 = ((bf16[16,72,512]{2,1,0:T(8,128)(2,1)}), bf16[16,72,512]{2,1,0:T(8,128)(2,1)}, u32[]{:S(2)}, u32[]{:S(2)}) async-start(bf16[16,72,512]{2,1,0:T(8,128)(2,1)} %bitcast.26), calls=%async_computation.4 | async-start | bytes 2359296 | tf_op jit(solution)/shard_map/all_to_all | solution.py:486
  397.5 172.5 %all-to-all-start.5 = ((bf16[16,64,3392]{2,1,0:T(8,128)(2,1)}), bf16[16,64,3392]{2,1,0:T(8,128)(2,1)}, u32[]{:S(2)}, u32[]{:S(2)}) async-start(bf16[16,64,3392]{2,1,0:T(8,128)(2,1)} %pad_maximum_fusion.1), calls=%async_computation.5 | async-start | bytes 14155776 | tf_op jit(solution)/shard_map/all_to_all | solution.py:486
  452.3 13.4 %collective-permute-start.16 = (bf16[8,64,2048]{2,1,0:T(8,128)(2,1)}, bf16[8,64,2048]{2,1,0:T(8,128)(2,1)}, u32[]{:S(2)}, u32[]{:S(2)}) collective-permute-start(bf16[8,64,2048]{2,1,0:T(8,128)(2,1)} %dynamic-slice_bitcast_fusion), channel_id=1, source_target_pairs={{0,2},{2,0},{4,6},{6,4},{8,10},{10,8},{12,14},{14,12},{16,18},{18,... | collective-permute-start | bytes 6291464 | tf_op jit(solution)/shard_map/ppermute | solution.py:708
  464.1 14.6 %collective-permute-start.20 = (bf16[256,1024]{1,0:T(8,128)(2,1)}, bf16[256,1024]{1,0:T(8,128)(2,1)}, u32[]{:S(2)}, u32[]{:S(2)}) collective-permute-start(bf16[256,1024]{1,0:T(8,128)(2,1)} %dynamic-slice_convert_fusion.1), channel_id=1, source_target_pairs={{0,1},{1,0},{2,3},{3,2},{4,5},{5,4},{6,7},{7,6},{8,9},{9,8},{10,11... | collective-permute-start | bytes 1572872 | tf_op jit(solution)/shard_map/ppermute | solution.py:465
  469.9 53.2 %collective-permute-start.19 = (bf16[264,2048]{1,0:T(8,128)(2,1)}, bf16[264,2048]{1,0:T(8,128)(2,1)}, u32[]{:S(2)}, u32[]{:S(2)}) collective-permute-start(bf16[264,2048]{1,0:T(8,128)(2,1)} %pad_maximum_fusion.6), channel_id=1, source_target_pairs={{0,4},{2,6},{4,0},{6,2},{8,12},{10,14},{12,8},{14,10},{16,20},{18,... | collective-permute-start | bytes 3244040 | tf_op jit(solution)/shard_map/ppermute | solution.py:708
  526.8 58.1 %collective-permute-start.22 = (bf16[72,2048]{1,0:T(8,128)(2,1)S(1)}, bf16[72,2048]{1,0:T(8,128)(2,1)}, u32[]{:S(2)}, u32[]{:S(2)}) collective-permute-start(bf16[72,2048]{1,0:T(8,128)(2,1)S(1)} %get-tuple-element.119), channel_id=1, source_target_pairs={{0,8},{2,10},{4,12},{6,14},{8,0},{10,2},{12,4},{14,6},{16,24},{18,... | collective-permute-start | bytes 884744 | tf_op jit(solution)/shard_map/ppermute | solution.py:708
  526.8 58.0 %collective-permute-start.23 = (bf16[72,2048]{1,0:T(8,128)(2,1)S(1)}, bf16[72,2048]{1,0:T(8,128)(2,1)}, u32[]{:S(2)}, u32[]{:S(2)}) collective-permute-start(bf16[72,2048]{1,0:T(8,128)(2,1)S(1)} %get-tuple-element.118), channel_id=1, source_target_pairs={{0,16},{2,18},{4,20},{6,22},{8,24},{10,26},{12,28},{14,30},{16,0},... | collective-permute-start | bytes 884744 | tf_op jit(solution)/shard_map/ppermute | solution.py:708
  529.3 55.6 %collective-permute-start.24 = (bf16[72,2048]{1,0:T(8,128)(2,1)S(1)}, bf16[72,2048]{1,0:T(8,128)(2,1)}, u32[]{:S(2)}, u32[]{:S(2)}) collective-permute-start(bf16[72,2048]{1,0:T(8,128)(2,1)S(1)} %get-tuple-element.117), channel_id=1, source_target_pairs={{0,24},{2,26},{4,28},{6,30},{8,16},{10,18},{12,20},{14,22},{16,8},... | collective-permute-start | bytes 884744 | tf_op jit(solution)/shard_map/ppermute | solution.py:708
  (49 other events, 1153.5 us)

commit v5 on v4

--- a/solution.py
+++ b/solution.py
@@ -229,42 +229,36 @@
 
 def assemble_kernel(place_ref, *refs):
     parts, (weight_ref, out_ref, gain_ref) = refs[:-3], refs[-3:]
-    rows = weight_ref.shape[0]
+    rows = weight_ref.shape[0] // len(parts)
     pairs = weight_ref.shape[1] // (3 * LANES)
-    wanted = pl.program_id(1) ^ place_ref[1]
     for index, part_ref in enumerate(parts):
-
-        @pl.when(wanted == index)
-        def _(part_ref=part_ref):
-            for kind in range(3):
-                for pair in range(pairs):
-                    first = (3 * pair + kind) * LANES
-                    weight_ref[:, first : first + LANES] = part_ref[
-                        0, kind * rows : (kind + 1) * rows, pair * LANES : (pair + 1) * LANES
-                    ]
-            out_ref[...] = part_ref[0, 3 * rows : 4 * rows, :]
-            gain_ref[0] = part_ref[0, 4 * rows :, :]
+        inner = index ^ place_ref[1]
+        block = pl.ds(pl.multiple_of(inner * rows, rows), rows)
+        for kind in range(3):
+            for pair in range(pairs):
+                first = (3 * pair + kind) * LANES
+                weight_ref[block, first : first + LANES] = part_ref[
+                    0, kind * rows : (kind + 1) * rows, pair * LANES : (pair + 1) * LANES
+                ]
+        out_ref[block, :] = part_ref[0, 3 * rows : 4 * rows, :]
+        gain_ref[pl.ds(inner, 1)] = part_ref[:, 4 * rows :, :]
 
 
 def assemble(place, parts):
     outer, block_rows, cols = parts[0].shape
     inner = len(parts)
     rows = (block_rows - GAIN_ROWS) // 4
-    block = pl.BlockSpec(
-        (1, block_rows, cols), lambda i, j, place_ref: (i ^ place_ref[0], 0, 0)
-    )
+    block = pl.BlockSpec((1, block_rows, cols), lambda i, place_ref: (i ^ place_ref[0], 0, 0))
     return pl.pallas_call(
         assemble_kernel,
         grid_spec=pltpu.PrefetchScalarGridSpec(
             num_scalar_prefetch=1,
-            grid=(outer, inner),
+            grid=(outer,),
             in_specs=[block] * inner,
             out_specs=[
-                pl.BlockSpec((rows, 3 * cols), lambda i, j, place_ref: (i * inner + j, 0)),
-                pl.BlockSpec((rows, cols), lambda i, j, place_ref: (i * inner + j, 0)),
-                pl.BlockSpec(
-                    (1, GAIN_ROWS, cols), lambda i, j, place_ref: (i * inner + j, 0, 0)
-                ),
+                pl.BlockSpec((inner * rows, 3 * cols), lambda i, place_ref: (i, 0)),
+                pl.BlockSpec((inner * rows, cols), lambda i, place_ref: (i, 0)),
+                pl.BlockSpec((inner, GAIN_ROWS, cols), lambda i, place_ref: (i, 0, 0)),
             ],
         ),
         out_shape=[
@@ -464,6 +458,9 @@
     def swap(block):
         return lax.ppermute(block, "tensor", [(0, 1), (1, 0)])
 
+    def partner(block, offset):
+        return lax.ppermute(block, "dp", [(i, i ^ offset) for i in range(dp_count)])
+
     def chain(block, earlier):
         return lax.optimization_barrier((block, earlier))
 
@@ -550,33 +547,28 @@
         jnp.where(second_hit, gate_values[:, 1][None, :], no_gate),
     )
 
-    tokens_other = swap(tokens)
     mix_grad = lax.optimization_barrier(
         (own_valid * cotangent.astype(jnp.float32)).astype(jnp.bfloat16)
     )
-    mix_other = swap(other_part(mix_grad, 1))
+    mix_away = other_part(mix_grad, 1)
+    mix_other = swap(mix_away)
+    tokens_other = swap(chain(tokens, mix_away)[0])
     out_grad_cols = dot_nn(
         pick_gate, ordered(own_part(mix_grad, 1), mix_other, 0)
     ).astype(jnp.bfloat16)
     residual, out_grad_cols = chain(tokens, out_grad_cols)
-    gate_up = jnp.concatenate(
-        [home_order(gate_weight), home_order(up_weight), pack(out_grad_cols)], axis=2
-    )
+    gate_up = jnp.concatenate([home_order(gate_weight), home_order(up_weight)], axis=2)
     if dp_count == 16:
-        across = [
-            lax.ppermute(layer_shard, "dp", [(i, i ^ (4 * k)) for i in range(16)])
-            for k in range(1, 4)
-        ]
-        gate_up, across = chain(gate_up, across)
+        across = [partner(layer_shard, 4 * k) for k in range(1, 4)]
+        gate_up = chain(gate_up, across)[0]
         near = jnp.stack([layer_shard, *across])
-        side = lax.ppermute(near, "dp", [(i, i ^ 2) for i in range(16)])
-        core = [(i, i ^ 1) for i in range(16)]
-        parts = [near, lax.ppermute(near, "dp", core), side, lax.ppermute(side, "dp", core)]
+        side = partner(near, 2)
+        parts = [near, partner(near, 1), side, partner(side, 1)]
         place = jnp.stack([dp_index // 4, dp_index % 4])
         projection, out_all, gain_rows = assemble(place, parts)
     else:
         layer_all = lax.all_gather(layer_shard, "dp", axis=0, tiled=False)
-        gate_up, layer_all = chain(gate_up, layer_all)
+        gate_up = chain(gate_up, layer_all)[0]
         projection = (
             layer_all[:, : 3 * shard_rows]
             .reshape(dp_count, 3, shard_rows, pairs, LANES)
@@ -585,9 +577,7 @@
         )
         out_all = layer_all[:, 3 * shard_rows : 4 * shard_rows].reshape(width, head_cols)
         gain_rows = layer_all[:, 4 * shard_rows :]
-    arrived = exchange(gate_up)
-    gate_up_all = arrived.reshape(width, arrived.shape[2])
-    slot_grad_half = unpack(arrived[:, :, 2 * hidden_cols :])
+    gate_up_all = exchange(gate_up).reshape(width, 2 * hidden_cols)
 
     distance = jnp.arange(2 * seq, dtype=jnp.int32)
     table_reversed = jnp.concatenate(
@@ -614,15 +604,18 @@
     mid_scale = lax.rsqrt(jnp.mean(mid * mid, axis=-1, keepdims=True) + EPSILON)
     norm_two = (mid * mid_scale * gain_two).astype(jnp.bfloat16)
     norm_two_cols = ordered(own_part(norm_two, 1), swap(other_part(norm_two, 1)), 0)
-    expert_rows, slot_grad_half = chain(
-        dot_nn(pick, norm_two_cols).astype(jnp.bfloat16), slot_grad_half
-    )
+    slot_rows, gate_up_all = chain(
+        jnp.concatenate(
+            [dot_nn(pick, norm_two_cols).astype(jnp.bfloat16), out_grad_cols], axis=1
+        ),
+        gate_up_all,
+    )
+    down_late, slot_rows = chain(down_weight, route(slot_rows))
+    down_all = fetch(down_late)
+    expert_half = slot_rows[:, :half]
+    expert_other = swap(expert_half)
+    slot_grad_half = chain(slot_rows[:, half:], expert_other)[0]
     slot_grad_other = swap(slot_grad_half)
-    down_late, (expert_half, slot_grad_other) = chain(
-        down_weight, (route(expert_rows), slot_grad_other)
-    )
-    down_all = fetch(down_late)
-    expert_other = swap(expert_half)
 
     side = tensor_index[None]
     hidden, slope, gelu = expert_forward(
@@ -703,9 +696,6 @@
     small = jnp.concatenate(
         [gain_part + swap(gain_part), bias_grad.reshape(-1, LANES)], axis=0
     )
-
-    def partner(block, offset):
-        return lax.ppermute(block, "dp", [(i, i ^ offset) for i in range(dp_count)])
 
     row_size = layer_part.shape[1]
     small = jnp.pad(small.reshape(-1), (0, -small.size % row_size)).reshape(-1, row_size)

time: 602 us -> 597 us (level)
  blocking collectives: 0 us -> 59.2 us
  waiting for transfers between devices: 333 us -> 283 us
    ppermute x6 -> x12, waiting for transfers between devices: 40.5 us -> 118 us  [partner(): return lax.ppermute(block, 'dp', [(i, i ^ offset) for i in range(dp_count)])]
    ppermute x6 -> x0, waiting for transfers between devices: 75.5 us -> none  [the longest x1 70.3 us: on_device(): side = lax.ppermute(near, 'dp', [(i, i ^ 2) for i in range(16)])]
    all_to_all x0 -> x1, blocking collectives: none -> 59.2 us  [exchange(): return lax.all_to_all(block, 'dp', split_axis=0, concat_axis=0, tiled=True)]
    ppermute x13, waiting for transfers between devices: 128 us -> 96.8 us  [swap(): return lax.ppermute(block, 'tensor', [(0, 1), (1, 0)])]
    all_to_all x6 -> x5, waiting for transfers between devices: 89.2 us -> 68 us  [exchange(): return lax.all_to_all(block, 'dp', split_axis=0, concat_axis=0, tiled=True)]
    all_to_all x6 -> x5, starting transfers between devices: 30.8 us -> 26.2 us  [exchange(): return lax.all_to_all(block, 'dp', split_axis=0, concat_axis=0, tiled=True)]
  transfers between devices with their start and end apart: 31 -> 30, of which waited for: 19 -> 20; matrix products, arithmetic and copies ran while one was open for 19% -> 19% of each run, Pallas kernels for 11% -> 10%
where the time goes in v5:
time: 597 us; the launch traced here: 588 us
  waiting for transfers between devices  283 us (47%)
  Pallas kernels  59.5 us (10%)
  blocking collectives  59.2 us (10%)
  starting transfers between devices  55.3 us (9%)
  other arithmetic  50.8 us (9%)
  matrix products  50.5 us (8%)
  local copies, waits for them, and re-layouts  27.5 us (5%)
    ppermute x12, waiting for transfers between devices, partner(): return lax.ppermute(block, 'dp', [(i, i ^ offset) for i in range(dp_count)])  118 us
    ppermute x13, waiting for transfers between devices, swap(): return lax.ppermute(block, 'tensor', [(0, 1), (1, 0)])  96.8 us
    all_to_all x5, waiting for transfers between devices, exchange(): return lax.all_to_all(block, 'dp', split_axis=0, concat_axis=0, tiled=True)  68 us
    all_to_all x1, blocking collectives, exchange(): return lax.all_to_all(block, 'dp', split_axis=0, concat_axis=0, tiled=True)  59.2 us
    dot_general x6, matrix products, dot_tn(): lax.dot_general(left, right, (((0,), (0,)), ((), ())), preferred_element_...  27.2 us
    all_to_all x5, starting transfers between devices, exchange(): return lax.all_to_all(block, 'dp', split_axis=0, concat_axis=0, tiled=True)  26.2 us
    ppermute x13, starting transfers between devices, swap(): return lax.ppermute(block, 'tensor', [(0, 1), (1, 0)])  18.9 us
    pallas_call x1, Pallas kernels, expert_backward(): pl.pallas_call(expert_backward_kernel, grid_spec=pltpu.PrefetchScalarGrid...  16.7 us
  transfers between devices with their start and end apart: 30, of which 20 were waited for; matrix products, arithmetic and copies ran while one was open for 19% of the time, Pallas kernels for 10%

profile of v5, /device:TPU:16, one launch (start us, length us, event | category | flops | bytes accessed | tf_op | source)
XLA Modules:
  0.0 587.5 jit_solution(11266506961072803684)
XLA Ops:
  13.9 8.8 %collective-permute-done.3 = bf16[272,512]{1,0:T(8,128)(2,1)S(1)} collective-permute-done((bf16[272,512]{1,0:T(8,128)(2,1)S(1)}, bf16[272,512]{1,0:T(8,128)(2,1)S(1)}, u32[]{:S(2)}, u32[]{:S(2)}) %collective-permute-start.3) | collective-permute-done | bytes 278560 | tf_op jit(solution)/shard_map/ppermute | solution.py:462
  22.7 6.6 %collective-permute-done.4 = bf16[272,512]{1,0:T(8,128)(2,1)S(1)} collective-permute-done((bf16[272,512]{1,0:T(8,128)(2,1)S(1)}, bf16[272,512]{1,0:T(8,128)(2,1)S(1)}, u32[]{:S(2)}, u32[]{:S(2)}) %collective-permute-start.4) | collective-permute-done | bytes 278560 | tf_op jit(solution)/shard_map/ppermute | solution.py:462
  42.8 58.0 %collective-permute-done.6.refs_2_ = bf16[4,272,512]{2,1,0:T(8,128)(2,1)} collective-permute-done((bf16[4,272,512]{2,1,0:T(8,128)(2,1)S(1)}, bf16[4,272,512]{2,1,0:T(8,128)(2,1)}, u32[]{:S(2)}, u32[]{:S(2)}) %collective-permute-start.6) | collective-permute-done | bytes 1114144 | tf_op jit(solution)/shard_map/ppermute | solution.py:462
  115.5 11.0 %attend_forward.1 = (bf16[512,512]{1,0:T(8,128)(2,1)}, f32[4,2,512]{2,1,0:T(2,128)}) custom-call(s32[1]{0:T(128)} %dynamic_slice.78.length_ref, bf16[512,1536]{1,0:T(8,128)(2,1)} %convolution_convert_fusion.4.joined_ref, f32[4,2,1024]{2,1,0:T(2,128)} %reshape.196.bias_ref), custom_call_target="tpu_custom_call" | custom-call | flops 2147483648 | bytes 2097152 | tf_op jit(solution)/shard_map/attend_forward/pallas_call | solution.py:104
  133.6 9.2 %collective-permute-done.8 = bf16[256,1024]{1,0:T(8,128)(2,1)} collective-permute-done((bf16[256,1024]{1,0:T(8,128)(2,1)S(1)}, bf16[256,1024]{1,0:T(8,128)(2,1)}, u32[]{:S(2)}, u32[]{:S(2)}) %collective-permute-start.8) | collective-permute-done | bytes 524320 | tf_op jit(solution)/shard_map/ppermute | solution.py:459
  147.7 6.0 %collective-permute-done.9 = bf16[256,512]{1,0:T(8,128)(2,1)S(1)} collective-permute-done((bf16[256,512]{1,0:T(8,128)(2,1)S(1)}, bf16[256,512]{1,0:T(8,128)(2,1)S(1)}, u32[]{:S(2)}, u32[]{:S(2)}) %collective-permute-start.9) | collective-permute-done | bytes 262176 | tf_op jit(solution)/shard_map/ppermute | solution.py:459
  160.9 59.2 %all_to_all.30 = bf16[16,72,1024]{2,1,0:T(8,128)(2,1)} all-to-all(bf16[16,72,1024]{2,1,0:T(8,128)(2,1)S(1)} %bitcast.84), channel_id=1, replica_groups=mesh['dp'=16,'tensor'=2] {'dp'}, dimensions={0} | all-to-all | bytes 4718592 | tf_op jit(solution)/shard_map/all_to_all | solution.py:483
  228.9 26.5 %collective-permute-done.10.far_ref = bf16[1152,512]{1,0:T(8,128)(2,1)S(1)} collective-permute-done((bf16[1152,512]{1,0:T(8,128)(2,1)S(1)}, bf16[1152,512]{1,0:T(8,128)(2,1)S(1)}, u32[]{:S(2)}, u32[]{:S(2)}) %collective-permute-start.10) | collective-permute-done | bytes 1179680 | tf_op jit(solution)/shard_map/ppermute | solution.py:459
  257.0 12.9 %expert_forward.1 = (bf16[1152,1408]{1,0:T(8,128)(2,1)S(1)}, f32[1152,1408]{1,0:T(8,128)}, f32[1152,1408]{1,0:T(8,128)}) custom-call(s32[1]{0:T(128)} %bitcast.13.side_ref, bf16[1152,512]{1,0:T(8,128)(2,1)S(1)} %get-tuple-element.104.near_ref, bf16[1152,512]{1,0:T(8,128)(2,1)S(1)} %collective-permute-done.10.far_ref, ...), custom_call_target="tpu_custom_call" | custom-call | flops 6643777536 | bytes 21987328 | tf_op jit(solution)/shard_map/expert_forward/pallas_call | solution.py:312
  269.9 12.8 %collective-permute-done.11.far_ref = bf16[1152,512]{1,0:T(8,128)(2,1)S(1)} collective-permute-done((bf16[1152,512]{1,0:T(8,128)(2,1)S(1)}, bf16[1152,512]{1,0:T(8,128)(2,1)S(1)}, u32[]{:S(2)}, u32[]{:S(2)}) %collective-permute-start.11) | collective-permute-done | bytes 1179680 | tf_op jit(solution)/shard_map/ppermute | solution.py:459
  282.7 6.0 %convolution_convert_fusion.2 = bf16[1024,1408]{1,0:T(8,128)(2,1)} fusion(bf16[1152,1408]{1,0:T(8,128)(2,1)S(1)} %get-tuple-element.66, bf16[1152,512]{1,0:T(8,128)(2,1)S(1)} %collective-permute-done.11.far_ref, bf16[1152,512]{1,0:T(8,128)(2,1)S(1)} %get-tuple-element.57.near_ref, pred[]{:T(512)S(6)} %eq.79), kind=kOutput, calls=%fused_computation.9 | convolution fusion | flops 3333947392 | bytes 8486913 | tf_op jit(solution)/shard_map/dot_general | solution.py:34
  290.0 5.8 all-to-all-start.3
  297.1 16.7 %expert_backward.1 = (bf16[1152,2816]{1,0:T(8,128)(2,1)}, f32[1152,512]{1,0:T(8,128)S(1)}, bf16[1152,512]{1,0:T(8,128)(2,1)S(1)}) custom-call(s32[1]{0:T(128)} %bitcast.13.side_ref, bf16[1152,512]{1,0:T(8,128)(2,1)S(1)} %get-tuple-element.57.near_ref, bf16[1152,512]{1,0:T(8,128)(2,1)S(1)} %copy-done.3, f32[1152,1408]{1,0:T(8,128)} %get-tuple-element.59.slope_ref, ...), custom_call_target="tpu_custom_call" | custom-call | flops 9965666304 | bytes 28114944 | tf_op jit(solution)/shard_map/expert_backward/pallas_call | solution.py:384
  322.6 19.4 %collective-permute-done.12 = bf16[1152,512]{1,0:T(8,128)(2,1)S(1)} collective-permute-done((bf16[1152,512]{1,0:T(8,128)(2,1)S(1)}, bf16[1152,512]{1,0:T(8,128)(2,1)S(1)}, u32[]{:S(2)}, u32[]{:S(2)}) %collective-permute-start.12) | collective-permute-done | bytes 1179680 | tf_op jit(solution)/shard_map/ppermute | solution.py:459
  344.9 15.6 %all-to-all-done.3 = bf16[16,64,1408]{2,1,0:T(8,128)(2,1)} async-done(((bf16[16,64,1408]{2,1,0:T(8,128)(2,1)}), bf16[16,64,1408]{2,1,0:T(8,128)(2,1)}, u32[]{:S(2)}, u32[]{:S(2)}) %all-to-all-start.3) | async-done | bytes 2883616 | tf_op jit(solution)/shard_map/all_to_all | solution.py:483
  365.5 12.6 %convolution_convert_fusion = bf16[1024,2816]{1,0:T(8,128)(2,1)} fusion(bf16[1152,2816]{1,0:T(8,128)(2,1)} %get-tuple-element.64, bf16[1152,512]{1,0:T(8,128)(2,1)S(1)} %collective-permute-done.10.far_ref, bf16[1152,512]{1,0:T(8,128)(2,1)S(1)} %get-tuple-element.104.near_ref, pred[]{:T(512)S(6)} %eq.79), kind=kOutput, calls=%fused_computation.2 | convolution fusion | flops 6657277952 | bytes 14614529 | tf_op jit(solution)/shard_map/dot_general | solution.py:34
  380.6 6.0 %pad_maximum_fusion = bf16[16,64,3392]{2,1,0:T(8,128)(2,1)} fusion(bf16[16,64,64]{2,1,0:T(8,128)(2,1)S(1)} %bitcast.95, bf16[16,64,512]{2,1,0:T(8,128)(2,1)S(1)} %slice.154, bf16[16,64,2816]{2,1,0:T(8,128)(2,1)} %bitcast.87), kind=kLoop, calls=%fused_computation | loop fusion | flops 20840448 | bytes 13893632 | tf_op jit(solution)/shard_map/concatenate | solution.py:644
  386.7 6.8 %all-to-all-done.4 = bf16[16,72,512]{2,1,0:T(8,128)(2,1)} async-done(((bf16[16,72,512]{2,1,0:T(8,128)(2,1)}), bf16[16,72,512]{2,1,0:T(8,128)(2,1)}, u32[]{:S(2)}, u32[]{:S(2)}) %all-to-all-start.4) | async-done | bytes 1179680 | tf_op jit(solution)/shard_map/all_to_all | solution.py:483
  402.1 6.8 %collective-permute-done.14 = bf16[256,512]{1,0:T(8,128)(2,1)S(1)} collective-permute-done((bf16[256,512]{1,0:T(8,128)(2,1)S(1)}, bf16[256,512]{1,0:T(8,128)(2,1)S(1)}, u32[]{:S(2)}, u32[]{:S(2)}) %collective-permute-start.14) | collective-permute-done | bytes 262176 | tf_op jit(solution)/shard_map/ppermute | solution.py:459
  412.4 11.9 %collective-permute-done.15 = bf16[256,1024]{1,0:T(8,128)(2,1)} collective-permute-done((bf16[256,1024]{1,0:T(8,128)(2,1)S(1)}, bf16[256,1024]{1,0:T(8,128)(2,1)}, u32[]{:S(2)}, u32[]{:S(2)}) %collective-permute-start.15) | collective-permute-done | bytes 524320 | tf_op jit(solution)/shard_map/ppermute | solution.py:459
  429.1 13.3 %attend_backward.1 = (bf16[512,1536]{1,0:T(8,128)(2,1)}, f32[4,2,1024]{2,1,0:T(2,128)}) custom-call(s32[1]{0:T(128)} %dynamic_slice.78.length_ref, bf16[512,1536]{1,0:T(8,128)(2,1)} %convolution_convert_fusion.4.joined_ref, bf16[512,512]{1,0:T(8,128)(2,1)} %convolution_convert_fusion.7.grad_ref, f32[4,2,512]{2,1,0:T(2,128)} %get-tuple-element.75.total_ref, ...), custom_call_target="tpu_custom_call" | custom-call | flops 5368709120 | bytes 3670016 | tf_op jit(solution)/shard_map/attend_backward/pallas_call | solution.py:202
  478.3 40.7 %collective-permute-done.19 = bf16[264,2048]{1,0:T(8,128)(2,1)} collective-permute-done((bf16[264,2048]{1,0:T(8,128)(2,1)}, bf16[264,2048]{1,0:T(8,128)(2,1)}, u32[]{:S(2)}, u32[]{:S(2)}) %collective-permute-start.19) | collective-permute-done | bytes 1081376 | tf_op jit(solution)/shard_map/ppermute | solution.py:462
  526.2 39.7 %all-to-all-done.5 = bf16[16,64,3392]{2,1,0:T(8,128)(2,1)} async-done(((bf16[16,64,3392]{2,1,0:T(8,128)(2,1)}), bf16[16,64,3392]{2,1,0:T(8,128)(2,1)}, u32[]{:S(2)}, u32[]{:S(2)}) %all-to-all-start.5) | async-done | bytes 6946848 | tf_op jit(solution)/shard_map/all_to_all | solution.py:483
  571.1 8.6 %slice_convert_fusion = (f32[16,64,1408]{2,1,0:T(8,128)}, f32[16,64,1408]{2,1,0:T(8,128)}) fusion(bf16[16,64,3392]{2,1,0:T(8,128)(2,1)} %all-to-all-done.5), kind=kLoop, calls=%fused_computation.13 | loop fusion | flops 2883584 | bytes 17301504 | tf_op jit(solution)/shard_map/convert_element_type | solution.py:514
  (258 shorter events, 164.6 us)
Async XLA Ops:
  1.7 12.2 %collective-permute-start.2 = (bf16[272,512]{1,0:T(8,128)(2,1)S(1)}, bf16[272,512]{1,0:T(8,128)(2,1)S(1)}, u32[]{:S(2)}, u32[]{:S(2)}) collective-permute-start(bf16[272,512]{1,0:T(8,128)(2,1)S(1)} %get-tuple-element.114), channel_id=1, source_target_pairs={{0,8},{2,10},{4,12},{6,14},{8,0},{10,2},{12,4},{14,6},{16,24},{18,... | collective-permute-start | bytes 835592 | tf_op jit(solution)/shard_map/ppermute | solution.py:462
  3.3 19.4 %collective-permute-start.3 = (bf16[272,512]{1,0:T(8,128)(2,1)S(1)}, bf16[272,512]{1,0:T(8,128)(2,1)S(1)}, u32[]{:S(2)}, u32[]{:S(2)}) collective-permute-start(bf16[272,512]{1,0:T(8,128)(2,1)S(1)} %get-tuple-element.114), channel_id=1, source_target_pairs={{0,16},{2,18},{4,20},{6,22},{8,24},{10,26},{12,28},{14,30},{16,0},... | collective-permute-start | bytes 835592 | tf_op jit(solution)/shard_map/ppermute | solution.py:462
  3.7 25.6 %collective-permute-start.4 = (bf16[272,512]{1,0:T(8,128)(2,1)S(1)}, bf16[272,512]{1,0:T(8,128)(2,1)S(1)}, u32[]{:S(2)}, u32[]{:S(2)}) collective-permute-start(bf16[272,512]{1,0:T(8,128)(2,1)S(1)} %get-tuple-element.114), channel_id=1, source_target_pairs={{0,24},{2,26},{4,28},{6,30},{8,16},{10,18},{12,20},{14,22},{16,8},... | collective-permute-start | bytes 835592 | tf_op jit(solution)/shard_map/ppermute | solution.py:462
  29.3 131.6 %all-to-all-start = ((bf16[16,64,2816]{2,1,0:T(8,128)(2,1)}), bf16[16,64,2816]{2,1,0:T(8,128)(2,1)}, u32[]{:S(2)}, u32[]{:S(2)}) async-start(bf16[16,64,2816]{2,1,0:T(8,128)(2,1)} %pad_maximum_fusion.1), calls=%async_computation | async-start | bytes 11534336 | tf_op jit(solution)/shard_map/all_to_all | solution.py:483
  34.7 66.2 %collective-permute-start.6 = (bf16[4,272,512]{2,1,0:T(8,128)(2,1)S(1)}, bf16[4,272,512]{2,1,0:T(8,128)(2,1)}, u32[]{:S(2)}, u32[]{:S(2)}) collective-permute-start(bf16[4,272,512]{2,1,0:T(8,128)(2,1)S(1)} %pad_maximum_fusion.5.refs_0_), channel_id=1, source_target_pairs={{0,4},{2,6},{4,0},{6,2},{8,12},{10,14},{12,8},{14,10},{16,20},{18,... | collective-permute-start | bytes 3342344 | tf_op jit(solution)/shard_map/ppermute | solution.py:462
  38.6 92.1 %collective-permute-start = (bf16[256,512]{1,0:T(8,128)(2,1)}, bf16[256,512]{1,0:T(8,128)(2,1)}, u32[]{:S(2)}, u32[]{:S(2)}) collective-permute-start(bf16[256,512]{1,0:T(8,128)(2,1)} %get-tuple-element.112), channel_id=1, source_target_pairs={{0,1},{1,0},{2,3},{3,2},{4,5},{5,4},{6,7},{7,6},{8,9},{9,8},{10,11... | collective-permute-start | bytes 786440 | tf_op jit(solution)/shard_map/ppermute | solution.py:459
  40.0 62.6 %collective-permute-start.1 = (bf16[256,1024]{1,0:T(8,128)(2,1)S(1)}, bf16[256,1024]{1,0:T(8,128)(2,1)S(1)}, u32[]{:S(2)}, u32[]{:S(2)}) collective-permute-start(bf16[256,1024]{1,0:T(8,128)(2,1)S(1)} %copy-done.9), channel_id=1, source_target_pairs={{0,1},{1,0},{2,3},{3,2},{4,5},{5,4},{6,7},{7,6},{8,9},{9,8},{10,11... | collective-permute-start | bytes 1572872 | tf_op jit(solution)/shard_map/ppermute | solution.py:459
  42.8 60.3 %collective-permute-start.5 = (bf16[4,272,512]{2,1,0:T(8,128)(2,1)S(1)}, bf16[4,272,512]{2,1,0:T(8,128)(2,1)}, u32[]{:S(2)}, u32[]{:S(2)}) collective-permute-start(bf16[4,272,512]{2,1,0:T(8,128)(2,1)S(1)} %pad_maximum_fusion.5.refs_0_), channel_id=1, source_target_pairs={{0,2},{2,0},{4,6},{6,4},{8,10},{10,8},{12,14},{14,12},{16,18},{18,... | collective-permute-start | bytes 3342344 | tf_op jit(solution)/shard_map/ppermute | solution.py:462
  128.7 14.1 %collective-permute-start.8 = (bf16[256,1024]{1,0:T(8,128)(2,1)S(1)}, bf16[256,1024]{1,0:T(8,128)(2,1)}, u32[]{:S(2)}, u32[]{:S(2)}) collective-permute-start(bf16[256,1024]{1,0:T(8,128)(2,1)S(1)} %dynamic-slice_convert_fusion.2), channel_id=1, source_target_pairs={{0,1},{1,0},{2,3},{3,2},{4,5},{5,4},{6,7},{7,6},{8,9},{9,8},{10,11... | collective-permute-start | bytes 1572872 | tf_op jit(solution)/shard_map/ppermute | solution.py:459
  220.1 69.9 %all-to-all-start.2 = ((bf16[16,64,1408]{2,1,0:T(8,128)(2,1)}), bf16[16,64,1408]{2,1,0:T(8,128)(2,1)}, u32[]{:S(2)}, u32[]{:S(2)}) async-start(bf16[16,64,1408]{2,1,0:T(8,128)(2,1)} %param.25), calls=%async_computation.2 | async-start | bytes 5767168 | tf_op jit(solution)/shard_map/all_to_all | solution.py:483
  227.4 28.1 %collective-permute-start.10 = (bf16[1152,512]{1,0:T(8,128)(2,1)S(1)}, bf16[1152,512]{1,0:T(8,128)(2,1)S(1)}, u32[]{:S(2)}, u32[]{:S(2)}) collective-permute-start(bf16[1152,512]{1,0:T(8,128)(2,1)S(1)} %get-tuple-element.104.near_ref), channel_id=1, source_target_pairs={{0,1},{1,0},{2,3},{3,2},{4,5},{5,4},{6,7},{7,6},{8,9},{9,8},{10,11... | collective-permute-start | bytes 3538952 | tf_op jit(solution)/shard_map/ppermute | solution.py:459
  255.5 27.2 %collective-permute-start.11 = (bf16[1152,512]{1,0:T(8,128)(2,1)S(1)}, bf16[1152,512]{1,0:T(8,128)(2,1)S(1)}, u32[]{:S(2)}, u32[]{:S(2)}) collective-permute-start(bf16[1152,512]{1,0:T(8,128)(2,1)S(1)} %get-tuple-element.57.near_ref), channel_id=1, source_target_pairs={{0,1},{1,0},{2,3},{3,2},{4,5},{5,4},{6,7},{7,6},{8,9},{9,8},{10,11... | collective-permute-start | bytes 3538952 | tf_op jit(solution)/shard_map/ppermute | solution.py:459
  290.0 70.4 %all-to-all-start.3 = ((bf16[16,64,1408]{2,1,0:T(8,128)(2,1)}), bf16[16,64,1408]{2,1,0:T(8,128)(2,1)}, u32[]{:S(2)}, u32[]{:S(2)}) async-start(bf16[16,64,1408]{2,1,0:T(8,128)(2,1)} %bitcast.92), calls=%async_computation.3 | async-start | bytes 5767168 | tf_op jit(solution)/shard_map/all_to_all | solution.py:483
  313.8 28.1 %collective-permute-start.12 = (bf16[1152,512]{1,0:T(8,128)(2,1)S(1)}, bf16[1152,512]{1,0:T(8,128)(2,1)S(1)}, u32[]{:S(2)}, u32[]{:S(2)}) collective-permute-start(bf16[1152,512]{1,0:T(8,128)(2,1)S(1)} %get-tuple-element.67), channel_id=1, source_target_pairs={{0,1},{1,0},{2,3},{3,2},{4,5},{5,4},{6,7},{7,6},{8,9},{9,8},{10,11... | collective-permute-start | bytes 3538952 | tf_op jit(solution)/shard_map/ppermute | solution.py:459
  341.9 36.2 %collective-permute-start.13 = (bf16[1152,512]{1,0:T(8,128)(2,1)}, bf16[1152,512]{1,0:T(8,128)(2,1)S(1)}, u32[]{:S(2)}, u32[]{:S(2)}) collective-permute-start(bf16[1152,512]{1,0:T(8,128)(2,1)} %dynamic-slice_convert_fusion), channel_id=1, source_target_pairs={{0,1},{1,0},{2,3},{3,2},{4,5},{5,4},{6,7},{7,6},{8,9},{9,8},{10,11... | collective-permute-start | bytes 3538952 | tf_op jit(solution)/shard_map/ppermute | solution.py:459
  360.4 33.0 %all-to-all-start.4 = ((bf16[16,72,512]{2,1,0:T(8,128)(2,1)}), bf16[16,72,512]{2,1,0:T(8,128)(2,1)}, u32[]{:S(2)}, u32[]{:S(2)}) async-start(bf16[16,72,512]{2,1,0:T(8,128)(2,1)} %bitcast.20), calls=%async_computation.4 | async-start | bytes 2359296 | tf_op jit(solution)/shard_map/all_to_all | solution.py:483
  393.4 172.5 %all-to-all-start.5 = ((bf16[16,64,3392]{2,1,0:T(8,128)(2,1)}), bf16[16,64,3392]{2,1,0:T(8,128)(2,1)}, u32[]{:S(2)}, u32[]{:S(2)}) async-start(bf16[16,64,3392]{2,1,0:T(8,128)(2,1)} %pad_maximum_fusion), calls=%async_computation.5 | async-start | bytes 14155776 | tf_op jit(solution)/shard_map/all_to_all | solution.py:483
  410.9 13.4 %collective-permute-start.15 = (bf16[256,1024]{1,0:T(8,128)(2,1)S(1)}, bf16[256,1024]{1,0:T(8,128)(2,1)}, u32[]{:S(2)}, u32[]{:S(2)}) collective-permute-start(bf16[256,1024]{1,0:T(8,128)(2,1)S(1)} %get-tuple-element.97), channel_id=1, source_target_pairs={{0,1},{1,0},{2,3},{3,2},{4,5},{5,4},{6,7},{7,6},{8,9},{9,8},{10,11... | collective-permute-start | bytes 1572872 | tf_op jit(solution)/shard_map/ppermute | solution.py:459
  448.0 13.4 %collective-permute-start.16 = (bf16[8,64,2048]{2,1,0:T(8,128)(2,1)}, bf16[8,64,2048]{2,1,0:T(8,128)(2,1)}, u32[]{:S(2)}, u32[]{:S(2)}) collective-permute-start(bf16[8,64,2048]{2,1,0:T(8,128)(2,1)} %dynamic-slice_bitcast_fusion), channel_id=1, source_target_pairs={{0,2},{2,0},{4,6},{6,4},{8,10},{10,8},{12,14},{14,12},{16,18},{18,... | collective-permute-start | bytes 6291464 | tf_op jit(solution)/shard_map/ppermute | solution.py:462
  459.8 14.6 %collective-permute-start.20 = (bf16[256,1024]{1,0:T(8,128)(2,1)}, bf16[256,1024]{1,0:T(8,128)(2,1)}, u32[]{:S(2)}, u32[]{:S(2)}) collective-permute-start(bf16[256,1024]{1,0:T(8,128)(2,1)} %dynamic-slice_convert_fusion.1), channel_id=1, source_target_pairs={{0,1},{1,0},{2,3},{3,2},{4,5},{5,4},{6,7},{7,6},{8,9},{9,8},{10,11... | collective-permute-start | bytes 1572872 | tf_op jit(solution)/shard_map/ppermute | solution.py:459
  465.6 53.3 %collective-permute-start.19 = (bf16[264,2048]{1,0:T(8,128)(2,1)}, bf16[264,2048]{1,0:T(8,128)(2,1)}, u32[]{:S(2)}, u32[]{:S(2)}) collective-permute-start(bf16[264,2048]{1,0:T(8,128)(2,1)} %pad_maximum_fusion.6), channel_id=1, source_target_pairs={{0,4},{2,6},{4,0},{6,2},{8,12},{10,14},{12,8},{14,10},{16,20},{18,... | collective-permute-start | bytes 3244040 | tf_op jit(solution)/shard_map/ppermute | solution.py:462
  522.6 58.1 %collective-permute-start.22 = (bf16[72,2048]{1,0:T(8,128)(2,1)S(1)}, bf16[72,2048]{1,0:T(8,128)(2,1)}, u32[]{:S(2)}, u32[]{:S(2)}) collective-permute-start(bf16[72,2048]{1,0:T(8,128)(2,1)S(1)} %get-tuple-element.117), channel_id=1, source_target_pairs={{0,8},{2,10},{4,12},{6,14},{8,0},{10,2},{12,4},{14,6},{16,24},{18,... | collective-permute-start | bytes 884744 | tf_op jit(solution)/shard_map/ppermute | solution.py:462
  522.7 58.1 %collective-permute-start.23 = (bf16[72,2048]{1,0:T(8,128)(2,1)S(1)}, bf16[72,2048]{1,0:T(8,128)(2,1)}, u32[]{:S(2)}, u32[]{:S(2)}) collective-permute-start(bf16[72,2048]{1,0:T(8,128)(2,1)S(1)} %get-tuple-element.116), channel_id=1, source_target_pairs={{0,16},{2,18},{4,20},{6,22},{8,24},{10,26},{12,28},{14,30},{16,0},... | collective-permute-start | bytes 884744 | tf_op jit(solution)/shard_map/ppermute | solution.py:462
  525.1 55.7 %collective-permute-start.24 = (bf16[72,2048]{1,0:T(8,128)(2,1)S(1)}, bf16[72,2048]{1,0:T(8,128)(2,1)}, u32[]{:S(2)}, u32[]{:S(2)}) collective-permute-start(bf16[72,2048]{1,0:T(8,128)(2,1)S(1)} %get-tuple-element.115), channel_id=1, source_target_pairs={{0,24},{2,26},{4,28},{6,30},{8,16},{10,18},{12,20},{14,22},{16,8},... | collective-permute-start | bytes 884744 | tf_op jit(solution)/shard_map/ppermute | solution.py:462
  (53 other events, 578.4 us)

commit v6 on v5

--- a/solution.py
+++ b/solution.py
@@ -419,6 +419,46 @@
     )(side, near, far, slope, gelu, down, down, weights, weights, weights, weights)
 
 
+def finish_kernel(place_ref, stay_ref, *refs):
+    arrivals, small_ref, qkv_ref, out_ref, gain_ref, bias_ref = refs[:3], *refs[3:]
+    kinds, rows, cols = qkv_ref.shape
+    small_rows = small_ref.shape[0]
+    total = stay_ref[...].astype(jnp.float32)
+    small = small_ref[...]
+    for arrival in arrivals:
+        total = total + arrival[:rows].astype(jnp.float32)
+        extra = arrival[rows : rows + 2 * small_rows].astype(jnp.float32)
+        small = small + extra[:small_rows] + extra[small_rows:]
+    for kind in range(kinds):
+        for pair in range(cols // LANES):
+            first = (kinds * pair + kind) * LANES
+            qkv_ref[kind, :, pair * LANES : (pair + 1) * LANES] = total[:, first : first + LANES]
+    out_ref[...] = total[:, kinds * cols :]
+    width = small.shape[1] // 2
+    gains = jnp.concatenate([small[:1, :width], small[:1, width:]], axis=0)
+    gain_ref[...] = pltpu.roll(gains, width - place_ref[0] * rows, 1)[:, :rows]
+    heads, buckets = bias_ref.shape
+    for head in range(heads):
+        bias_ref[head : head + 1, :] = small[1:2, head * buckets : (head + 1) * buckets]
+
+
+def finish(place, stay, arrivals, small, cols, bias_shape):
+    rows = stay.shape[0]
+    whole = pl.BlockSpec(memory_space=pltpu.VMEM)
+    return pl.pallas_call(
+        finish_kernel,
+        in_specs=[pl.BlockSpec(memory_space=pltpu.SMEM), *[whole] * 5],
+        out_specs=[whole] * 4,
+        out_shape=[
+            jax.ShapeDtypeStruct((3, rows, cols), jnp.float32),
+            jax.ShapeDtypeStruct((rows, cols), jnp.float32),
+            jax.ShapeDtypeStruct((2, rows), jnp.float32),
+            jax.ShapeDtypeStruct(bias_shape, jnp.float32),
+        ],
+        name="finish",
+    )(place, stay, *arrivals, small)
+
+
 def on_device(
     tokens,
     cotangent,
@@ -743,34 +783,31 @@
     returned = unpack(arrived_back[:, :, 2 * hidden_cols :])
     mix_cols = dot_tn(pick_gate, returned)
     mix_away = other_part(mix_cols, 0).astype(jnp.bfloat16)
+    mix_other = swap(mix_away)
     arrived_back = chain(arrived_back, mix_away)[0]
     gate_grad = regroup(arrived_back[:, :, :hidden_cols])
     up_grad = regroup(arrived_back[:, :, hidden_cols : 2 * hidden_cols])
-    mix_own = ordered(own_part(mix_cols, 0), swap(mix_away).astype(jnp.float32), 1)
+    mix_own = ordered(own_part(mix_cols, 0), mix_other.astype(jnp.float32), 1)
     mixed = (mid + own_valid * mix_own).astype(jnp.bfloat16)
     if dp_count == 16:
         came = chain(came, (gate_grad, up_grad, mixed))[0]
-        small = small + sum(small_of(piece, shard_rows) for piece in came)
-        layer_grad = stay.astype(jnp.float32) + sum(
-            piece[:shard_rows].astype(jnp.float32) for piece in came
+        qkv_grad, out_grad, gains_grad, bias_out = finish(
+            dp_index[None], stay, came, small, head_cols, bias_grad.shape
         )
     else:
         layer_grad = lax.psum_scatter(
             layer_part, "dp", scatter_dimension=0, tiled=True
         ).astype(jnp.float32)
-    qkv_grad = (
-        layer_grad[:, : 3 * head_cols]
-        .reshape(shard_rows, pairs, 3, LANES)
-        .transpose(2, 0, 1, 3)
-        .reshape(3, shard_rows, head_cols)
-    )
-    out_grad = layer_grad[:, 3 * head_cols :]
-    gain_size = 2 * width
-    gain_sums = small.reshape(-1)[:gain_size].reshape(2, width)
-    bias_out = small.reshape(-1)[gain_size : gain_size + head_count * bucket_count].reshape(
-        head_count, bucket_count
-    )
-    gains_grad = lax.dynamic_slice_in_dim(gain_sums, dp_index * shard_rows, shard_rows, 1)
+        qkv_grad = (
+            layer_grad[:, : 3 * head_cols]
+            .reshape(shard_rows, pairs, 3, LANES)
+            .transpose(2, 0, 1, 3)
+            .reshape(3, shard_rows, head_cols)
+        )
+        out_grad = layer_grad[:, 3 * head_cols :]
+        gain_sums = small[:1].reshape(2, width)
+        gains_grad = lax.dynamic_slice_in_dim(gain_sums, dp_index * shard_rows, shard_rows, 1)
+        bias_out = small[1, : head_count * bucket_count].reshape(head_count, bucket_count)
     return (
         mixed,
         input_grad,

time: 597 us -> 594 us (level)
  transfers between devices with their start and end apart: 30 -> 30, of which waited for: 20 -> 20; matrix products, arithmetic and copies ran while one was open for 19% -> 20% of each run, Pallas kernels for 10% -> 10%
where the time goes in v6:
time: 594 us; the launch traced here: 584 us
  waiting for transfers between devices  282 us (47%)
  Pallas kernels  61.7 us (10%)
  blocking collectives  59.2 us (10%)
  starting transfers between devices  55.3 us (9%)
  matrix products  50.4 us (8%)
  other arithmetic  48.8 us (8%)
  local copies, waits for them, and re-layouts  24.7 us (4%)
    ppermute x12, waiting for transfers between devices, partner(): return lax.ppermute(block, 'dp', [(i, i ^ offset) for i in range(dp_count)])  118 us
    ppermute x13, waiting for transfers between devices, swap(): return lax.ppermute(block, 'tensor', [(0, 1), (1, 0)])  96.8 us
    all_to_all x5, waiting for transfers between devices, exchange(): return lax.all_to_all(block, 'dp', split_axis=0, concat_axis=0, tiled=True)  67.5 us
    all_to_all x1, blocking collectives, exchange(): return lax.all_to_all(block, 'dp', split_axis=0, concat_axis=0, tiled=True)  59.2 us
    dot_general x6, matrix products, dot_tn(): lax.dot_general(left, right, (((0,), (0,)), ((), ())), preferred_element_...  27.2 us
    all_to_all x5, starting transfers between devices, exchange(): return lax.all_to_all(block, 'dp', split_axis=0, concat_axis=0, tiled=True)  26.2 us
    ppermute x13, starting transfers between devices, swap(): return lax.ppermute(block, 'tensor', [(0, 1), (1, 0)])  18.9 us
    pallas_call x1, Pallas kernels, expert_backward(): pl.pallas_call(expert_backward_kernel, grid_spec=pltpu.PrefetchScalarGrid...  16.7 us
  transfers between devices with their start and end apart: 30, of which 20 were waited for; matrix products, arithmetic and copies ran while one was open for 20% of the time, Pallas kernels for 10%

profile of v6, /device:TPU:16, one launch (start us, length us, event | category | flops | bytes accessed | tf_op | source)
XLA Modules:
  0.0 584.2 jit_solution(5446601900554063611)
XLA Ops:
  13.9 8.8 %collective-permute-done.3 = bf16[272,512]{1,0:T(8,128)(2,1)S(1)} collective-permute-done((bf16[272,512]{1,0:T(8,128)(2,1)S(1)}, bf16[272,512]{1,0:T(8,128)(2,1)S(1)}, u32[]{:S(2)}, u32[]{:S(2)}) %collective-permute-start.3) | collective-permute-done | bytes 278560 | tf_op jit(solution)/shard_map/ppermute | solution.py:502
  22.7 6.6 %collective-permute-done.4 = bf16[272,512]{1,0:T(8,128)(2,1)S(1)} collective-permute-done((bf16[272,512]{1,0:T(8,128)(2,1)S(1)}, bf16[272,512]{1,0:T(8,128)(2,1)S(1)}, u32[]{:S(2)}, u32[]{:S(2)}) %collective-permute-start.4) | collective-permute-done | bytes 278560 | tf_op jit(solution)/shard_map/ppermute | solution.py:502
  42.8 58.0 %collective-permute-done.6.refs_2_ = bf16[4,272,512]{2,1,0:T(8,128)(2,1)} collective-permute-done((bf16[4,272,512]{2,1,0:T(8,128)(2,1)S(1)}, bf16[4,272,512]{2,1,0:T(8,128)(2,1)}, u32[]{:S(2)}, u32[]{:S(2)}) %collective-permute-start.6) | collective-permute-done | bytes 1114144 | tf_op jit(solution)/shard_map/ppermute | solution.py:502
  115.4 11.0 %attend_forward.1 = (bf16[512,512]{1,0:T(8,128)(2,1)}, f32[4,2,512]{2,1,0:T(2,128)}) custom-call(s32[1]{0:T(128)} %dynamic_slice.75.length_ref, bf16[512,1536]{1,0:T(8,128)(2,1)} %convolution_convert_fusion.4.joined_ref, f32[4,2,1024]{2,1,0:T(2,128)} %reshape.178.bias_ref), custom_call_target="tpu_custom_call" | custom-call | flops 2147483648 | bytes 2097152 | tf_op jit(solution)/shard_map/attend_forward/pallas_call | solution.py:104
  133.6 9.2 %collective-permute-done.8 = bf16[256,1024]{1,0:T(8,128)(2,1)} collective-permute-done((bf16[256,1024]{1,0:T(8,128)(2,1)S(1)}, bf16[256,1024]{1,0:T(8,128)(2,1)}, u32[]{:S(2)}, u32[]{:S(2)}) %collective-permute-start.8) | collective-permute-done | bytes 524320 | tf_op jit(solution)/shard_map/ppermute | solution.py:499
  147.7 6.0 %collective-permute-done.9 = bf16[256,512]{1,0:T(8,128)(2,1)S(1)} collective-permute-done((bf16[256,512]{1,0:T(8,128)(2,1)S(1)}, bf16[256,512]{1,0:T(8,128)(2,1)S(1)}, u32[]{:S(2)}, u32[]{:S(2)}) %collective-permute-start.9) | collective-permute-done | bytes 262176 | tf_op jit(solution)/shard_map/ppermute | solution.py:499
  160.9 59.2 %all_to_all.30 = bf16[16,72,1024]{2,1,0:T(8,128)(2,1)} all-to-all(bf16[16,72,1024]{2,1,0:T(8,128)(2,1)S(1)} %bitcast.83), channel_id=1, replica_groups=mesh['dp'=16,'tensor'=2] {'dp'}, dimensions={0} | all-to-all | bytes 4718592 | tf_op jit(solution)/shard_map/all_to_all | solution.py:523
  228.9 26.5 %collective-permute-done.10.far_ref = bf16[1152,512]{1,0:T(8,128)(2,1)S(1)} collective-permute-done((bf16[1152,512]{1,0:T(8,128)(2,1)S(1)}, bf16[1152,512]{1,0:T(8,128)(2,1)S(1)}, u32[]{:S(2)}, u32[]{:S(2)}) %collective-permute-start.10) | collective-permute-done | bytes 1179680 | tf_op jit(solution)/shard_map/ppermute | solution.py:499
  256.9 12.9 %expert_forward.1 = (bf16[1152,1408]{1,0:T(8,128)(2,1)S(1)}, f32[1152,1408]{1,0:T(8,128)}, f32[1152,1408]{1,0:T(8,128)}) custom-call(s32[1]{0:T(128)} %bitcast.13.side_ref, bf16[1152,512]{1,0:T(8,128)(2,1)S(1)} %get-tuple-element.112.near_ref, bf16[1152,512]{1,0:T(8,128)(2,1)S(1)} %collective-permute-done.10.far_ref, ...), custom_call_target="tpu_custom_call" | custom-call | flops 6643777536 | bytes 21987328 | tf_op jit(solution)/shard_map/expert_forward/pallas_call | solution.py:312
  269.9 12.8 %collective-permute-done.11.far_ref = bf16[1152,512]{1,0:T(8,128)(2,1)S(1)} collective-permute-done((bf16[1152,512]{1,0:T(8,128)(2,1)S(1)}, bf16[1152,512]{1,0:T(8,128)(2,1)S(1)}, u32[]{:S(2)}, u32[]{:S(2)}) %collective-permute-start.11) | collective-permute-done | bytes 1179680 | tf_op jit(solution)/shard_map/ppermute | solution.py:499
  282.6 6.0 %convolution_convert_fusion.2 = bf16[1024,1408]{1,0:T(8,128)(2,1)} fusion(bf16[1152,1408]{1,0:T(8,128)(2,1)S(1)} %get-tuple-element.70, bf16[1152,512]{1,0:T(8,128)(2,1)S(1)} %collective-permute-done.11.far_ref, bf16[1152,512]{1,0:T(8,128)(2,1)S(1)} %get-tuple-element.61.near_ref, pred[]{:T(512)S(6)} %eq.79), kind=kOutput, calls=%fused_computation.9 | convolution fusion | flops 3333947392 | bytes 8486913 | tf_op jit(solution)/shard_map/dot_general | solution.py:34
  290.0 5.8 all-to-all-start.3
  297.1 16.7 %expert_backward.1 = (bf16[1152,2816]{1,0:T(8,128)(2,1)}, f32[1152,512]{1,0:T(8,128)S(1)}, bf16[1152,512]{1,0:T(8,128)(2,1)S(1)}) custom-call(s32[1]{0:T(128)} %bitcast.13.side_ref, bf16[1152,512]{1,0:T(8,128)(2,1)S(1)} %get-tuple-element.61.near_ref, bf16[1152,512]{1,0:T(8,128)(2,1)S(1)} %copy-done.3, f32[1152,1408]{1,0:T(8,128)} %get-tuple-element.63.slope_ref, ...), custom_call_target="tpu_custom_call" | custom-call | flops 9965666304 | bytes 28114944 | tf_op jit(solution)/shard_map/expert_backward/pallas_call | solution.py:384
  322.5 19.4 %collective-permute-done.12 = bf16[1152,512]{1,0:T(8,128)(2,1)S(1)} collective-permute-done((bf16[1152,512]{1,0:T(8,128)(2,1)S(1)}, bf16[1152,512]{1,0:T(8,128)(2,1)S(1)}, u32[]{:S(2)}, u32[]{:S(2)}) %collective-permute-start.12) | collective-permute-done | bytes 1179680 | tf_op jit(solution)/shard_map/ppermute | solution.py:499
  344.9 15.6 %all-to-all-done.3 = bf16[16,64,1408]{2,1,0:T(8,128)(2,1)} async-done(((bf16[16,64,1408]{2,1,0:T(8,128)(2,1)}), bf16[16,64,1408]{2,1,0:T(8,128)(2,1)}, u32[]{:S(2)}, u32[]{:S(2)}) %all-to-all-start.3) | async-done | bytes 2883616 | tf_op jit(solution)/shard_map/all_to_all | solution.py:523
  365.5 12.6 %convolution_convert_fusion = bf16[1024,2816]{1,0:T(8,128)(2,1)} fusion(bf16[1152,2816]{1,0:T(8,128)(2,1)} %get-tuple-element.68, bf16[1152,512]{1,0:T(8,128)(2,1)S(1)} %collective-permute-done.10.far_ref, bf16[1152,512]{1,0:T(8,128)(2,1)S(1)} %get-tuple-element.112.near_ref, pred[]{:T(512)S(6)} %eq.79), kind=kOutput, calls=%fused_computation.2 | convolution fusion | flops 6657277952 | bytes 14614529 | tf_op jit(solution)/shard_map/dot_general | solution.py:34
  380.6 6.0 %pad_maximum_fusion = bf16[16,64,3392]{2,1,0:T(8,128)(2,1)} fusion(bf16[16,64,64]{2,1,0:T(8,128)(2,1)S(1)} %bitcast.93, bf16[16,64,512]{2,1,0:T(8,128)(2,1)S(1)} %slice.85, bf16[16,64,2816]{2,1,0:T(8,128)(2,1)} %bitcast.86), kind=kLoop, calls=%fused_computation | loop fusion | flops 20840448 | bytes 13893632 | tf_op jit(solution)/shard_map/concatenate | solution.py:684
  386.6 6.8 %all-to-all-done.4 = bf16[16,72,512]{2,1,0:T(8,128)(2,1)} async-done(((bf16[16,72,512]{2,1,0:T(8,128)(2,1)}), bf16[16,72,512]{2,1,0:T(8,128)(2,1)}, u32[]{:S(2)}, u32[]{:S(2)}) %all-to-all-start.4) | async-done | bytes 1179680 | tf_op jit(solution)/shard_map/all_to_all | solution.py:523
  402.1 6.8 %collective-permute-done.14 = bf16[256,512]{1,0:T(8,128)(2,1)S(1)} collective-permute-done((bf16[256,512]{1,0:T(8,128)(2,1)S(1)}, bf16[256,512]{1,0:T(8,128)(2,1)S(1)}, u32[]{:S(2)}, u32[]{:S(2)}) %collective-permute-start.14) | collective-permute-done | bytes 262176 | tf_op jit(solution)/shard_map/ppermute | solution.py:499
  412.4 11.9 %collective-permute-done.15 = bf16[256,1024]{1,0:T(8,128)(2,1)} collective-permute-done((bf16[256,1024]{1,0:T(8,128)(2,1)S(1)}, bf16[256,1024]{1,0:T(8,128)(2,1)}, u32[]{:S(2)}, u32[]{:S(2)}) %collective-permute-start.15) | collective-permute-done | bytes 524320 | tf_op jit(solution)/shard_map/ppermute | solution.py:499
  429.1 13.3 %attend_backward.1 = (bf16[512,1536]{1,0:T(8,128)(2,1)}, f32[4,2,1024]{2,1,0:T(2,128)}) custom-call(s32[1]{0:T(128)} %dynamic_slice.75.length_ref, bf16[512,1536]{1,0:T(8,128)(2,1)} %convolution_convert_fusion.4.joined_ref, bf16[512,512]{1,0:T(8,128)(2,1)} %convolution_convert_fusion.7.grad_ref, f32[4,2,512]{2,1,0:T(2,128)} %get-tuple-element.79.total_ref, ...), custom_call_target="tpu_custom_call" | custom-call | flops 5368709120 | bytes 3670016 | tf_op jit(solution)/shard_map/attend_backward/pallas_call | solution.py:202
  478.3 40.7 %collective-permute-done.19 = bf16[264,2048]{1,0:T(8,128)(2,1)} collective-permute-done((bf16[264,2048]{1,0:T(8,128)(2,1)}, bf16[264,2048]{1,0:T(8,128)(2,1)}, u32[]{:S(2)}, u32[]{:S(2)}) %collective-permute-start.19) | collective-permute-done | bytes 1081376 | tf_op jit(solution)/shard_map/ppermute | solution.py:502
  526.7 39.2 %all-to-all-done.5 = bf16[16,64,3392]{2,1,0:T(8,128)(2,1)} async-done(((bf16[16,64,3392]{2,1,0:T(8,128)(2,1)}), bf16[16,64,3392]{2,1,0:T(8,128)(2,1)}, u32[]{:S(2)}, u32[]{:S(2)}) %all-to-all-start.5) | async-done | bytes 6946848 | tf_op jit(solution)/shard_map/all_to_all | solution.py:523
  571.1 8.6 %slice_convert_fusion = (f32[16,64,1408]{2,1,0:T(8,128)}, f32[16,64,1408]{2,1,0:T(8,128)}) fusion(bf16[16,64,3392]{2,1,0:T(8,128)(2,1)} %all-to-all-done.5), kind=kLoop, calls=%fused_computation.13 | loop fusion | flops 2883584 | bytes 17301504 | tf_op jit(solution)/shard_map/convert_element_type | solution.py:554
  (249 shorter events, 161.8 us)
Async XLA Ops:
  1.7 12.2 %collective-permute-start.2 = (bf16[272,512]{1,0:T(8,128)(2,1)S(1)}, bf16[272,512]{1,0:T(8,128)(2,1)S(1)}, u32[]{:S(2)}, u32[]{:S(2)}) collective-permute-start(bf16[272,512]{1,0:T(8,128)(2,1)S(1)} %get-tuple-element.123), channel_id=1, source_target_pairs={{0,8},{2,10},{4,12},{6,14},{8,0},{10,2},{12,4},{14,6},{16,24},{18,... | collective-permute-start | bytes 835592 | tf_op jit(solution)/shard_map/ppermute | solution.py:502
  3.3 19.4 %collective-permute-start.3 = (bf16[272,512]{1,0:T(8,128)(2,1)S(1)}, bf16[272,512]{1,0:T(8,128)(2,1)S(1)}, u32[]{:S(2)}, u32[]{:S(2)}) collective-permute-start(bf16[272,512]{1,0:T(8,128)(2,1)S(1)} %get-tuple-element.123), channel_id=1, source_target_pairs={{0,16},{2,18},{4,20},{6,22},{8,24},{10,26},{12,28},{14,30},{16,0},... | collective-permute-start | bytes 835592 | tf_op jit(solution)/shard_map/ppermute | solution.py:502
  3.7 25.6 %collective-permute-start.4 = (bf16[272,512]{1,0:T(8,128)(2,1)S(1)}, bf16[272,512]{1,0:T(8,128)(2,1)S(1)}, u32[]{:S(2)}, u32[]{:S(2)}) collective-permute-start(bf16[272,512]{1,0:T(8,128)(2,1)S(1)} %get-tuple-element.123), channel_id=1, source_target_pairs={{0,24},{2,26},{4,28},{6,30},{8,16},{10,18},{12,20},{14,22},{16,8},... | collective-permute-start | bytes 835592 | tf_op jit(solution)/shard_map/ppermute | solution.py:502
  29.3 131.6 %all-to-all-start = ((bf16[16,64,2816]{2,1,0:T(8,128)(2,1)}), bf16[16,64,2816]{2,1,0:T(8,128)(2,1)}, u32[]{:S(2)}, u32[]{:S(2)}) async-start(bf16[16,64,2816]{2,1,0:T(8,128)(2,1)} %pad_maximum_fusion.1), calls=%async_computation | async-start | bytes 11534336 | tf_op jit(solution)/shard_map/all_to_all | solution.py:523
  34.7 66.2 %collective-permute-start.6 = (bf16[4,272,512]{2,1,0:T(8,128)(2,1)S(1)}, bf16[4,272,512]{2,1,0:T(8,128)(2,1)}, u32[]{:S(2)}, u32[]{:S(2)}) collective-permute-start(bf16[4,272,512]{2,1,0:T(8,128)(2,1)S(1)} %pad_maximum_fusion.5.refs_0_), channel_id=1, source_target_pairs={{0,4},{2,6},{4,0},{6,2},{8,12},{10,14},{12,8},{14,10},{16,20},{18,... | collective-permute-start | bytes 3342344 | tf_op jit(solution)/shard_map/ppermute | solution.py:502
  38.5 92.1 %collective-permute-start = (bf16[256,512]{1,0:T(8,128)(2,1)}, bf16[256,512]{1,0:T(8,128)(2,1)}, u32[]{:S(2)}, u32[]{:S(2)}) collective-permute-start(bf16[256,512]{1,0:T(8,128)(2,1)} %get-tuple-element.121), channel_id=1, source_target_pairs={{0,1},{1,0},{2,3},{3,2},{4,5},{5,4},{6,7},{7,6},{8,9},{9,8},{10,11... | collective-permute-start | bytes 786440 | tf_op jit(solution)/shard_map/ppermute | solution.py:499
  40.0 62.6 %collective-permute-start.1 = (bf16[256,1024]{1,0:T(8,128)(2,1)S(1)}, bf16[256,1024]{1,0:T(8,128)(2,1)S(1)}, u32[]{:S(2)}, u32[]{:S(2)}) collective-permute-start(bf16[256,1024]{1,0:T(8,128)(2,1)S(1)} %copy-done.9), channel_id=1, source_target_pairs={{0,1},{1,0},{2,3},{3,2},{4,5},{5,4},{6,7},{7,6},{8,9},{9,8},{10,11... | collective-permute-start | bytes 1572872 | tf_op jit(solution)/shard_map/ppermute | solution.py:499
  42.8 60.3 %collective-permute-start.5 = (bf16[4,272,512]{2,1,0:T(8,128)(2,1)S(1)}, bf16[4,272,512]{2,1,0:T(8,128)(2,1)}, u32[]{:S(2)}, u32[]{:S(2)}) collective-permute-start(bf16[4,272,512]{2,1,0:T(8,128)(2,1)S(1)} %pad_maximum_fusion.5.refs_0_), channel_id=1, source_target_pairs={{0,2},{2,0},{4,6},{6,4},{8,10},{10,8},{12,14},{14,12},{16,18},{18,... | collective-permute-start | bytes 3342344 | tf_op jit(solution)/shard_map/ppermute | solution.py:502
  128.7 14.1 %collective-permute-start.8 = (bf16[256,1024]{1,0:T(8,128)(2,1)S(1)}, bf16[256,1024]{1,0:T(8,128)(2,1)}, u32[]{:S(2)}, u32[]{:S(2)}) collective-permute-start(bf16[256,1024]{1,0:T(8,128)(2,1)S(1)} %dynamic-slice_convert_fusion.2), channel_id=1, source_target_pairs={{0,1},{1,0},{2,3},{3,2},{4,5},{5,4},{6,7},{7,6},{8,9},{9,8},{10,11... | collective-permute-start | bytes 1572872 | tf_op jit(solution)/shard_map/ppermute | solution.py:499
  220.1 69.9 %all-to-all-start.2 = ((bf16[16,64,1408]{2,1,0:T(8,128)(2,1)}), bf16[16,64,1408]{2,1,0:T(8,128)(2,1)}, u32[]{:S(2)}, u32[]{:S(2)}) async-start(bf16[16,64,1408]{2,1,0:T(8,128)(2,1)} %param.25), calls=%async_computation.2 | async-start | bytes 5767168 | tf_op jit(solution)/shard_map/all_to_all | solution.py:523
  227.4 28.1 %collective-permute-start.10 = (bf16[1152,512]{1,0:T(8,128)(2,1)S(1)}, bf16[1152,512]{1,0:T(8,128)(2,1)S(1)}, u32[]{:S(2)}, u32[]{:S(2)}) collective-permute-start(bf16[1152,512]{1,0:T(8,128)(2,1)S(1)} %get-tuple-element.112.near_ref), channel_id=1, source_target_pairs={{0,1},{1,0},{2,3},{3,2},{4,5},{5,4},{6,7},{7,6},{8,9},{9,8},{10,11... | collective-permute-start | bytes 3538952 | tf_op jit(solution)/shard_map/ppermute | solution.py:499
  255.4 27.2 %collective-permute-start.11 = (bf16[1152,512]{1,0:T(8,128)(2,1)S(1)}, bf16[1152,512]{1,0:T(8,128)(2,1)S(1)}, u32[]{:S(2)}, u32[]{:S(2)}) collective-permute-start(bf16[1152,512]{1,0:T(8,128)(2,1)S(1)} %get-tuple-element.61.near_ref), channel_id=1, source_target_pairs={{0,1},{1,0},{2,3},{3,2},{4,5},{5,4},{6,7},{7,6},{8,9},{9,8},{10,11... | collective-permute-start | bytes 3538952 | tf_op jit(solution)/shard_map/ppermute | solution.py:499
  290.0 70.4 %all-to-all-start.3 = ((bf16[16,64,1408]{2,1,0:T(8,128)(2,1)}), bf16[16,64,1408]{2,1,0:T(8,128)(2,1)}, u32[]{:S(2)}, u32[]{:S(2)}) async-start(bf16[16,64,1408]{2,1,0:T(8,128)(2,1)} %bitcast.91), calls=%async_computation.3 | async-start | bytes 5767168 | tf_op jit(solution)/shard_map/all_to_all | solution.py:523
  313.8 28.1 %collective-permute-start.12 = (bf16[1152,512]{1,0:T(8,128)(2,1)S(1)}, bf16[1152,512]{1,0:T(8,128)(2,1)S(1)}, u32[]{:S(2)}, u32[]{:S(2)}) collective-permute-start(bf16[1152,512]{1,0:T(8,128)(2,1)S(1)} %get-tuple-element.71), channel_id=1, source_target_pairs={{0,1},{1,0},{2,3},{3,2},{4,5},{5,4},{6,7},{7,6},{8,9},{9,8},{10,11... | collective-permute-start | bytes 3538952 | tf_op jit(solution)/shard_map/ppermute | solution.py:499
  341.9 36.2 %collective-permute-start.13 = (bf16[1152,512]{1,0:T(8,128)(2,1)}, bf16[1152,512]{1,0:T(8,128)(2,1)S(1)}, u32[]{:S(2)}, u32[]{:S(2)}) collective-permute-start(bf16[1152,512]{1,0:T(8,128)(2,1)} %dynamic-slice_convert_fusion), channel_id=1, source_target_pairs={{0,1},{1,0},{2,3},{3,2},{4,5},{5,4},{6,7},{7,6},{8,9},{9,8},{10,11... | collective-permute-start | bytes 3538952 | tf_op jit(solution)/shard_map/ppermute | solution.py:499
  360.4 33.0 %all-to-all-start.4 = ((bf16[16,72,512]{2,1,0:T(8,128)(2,1)}), bf16[16,72,512]{2,1,0:T(8,128)(2,1)}, u32[]{:S(2)}, u32[]{:S(2)}) async-start(bf16[16,72,512]{2,1,0:T(8,128)(2,1)} %bitcast.20), calls=%async_computation.4 | async-start | bytes 2359296 | tf_op jit(solution)/shard_map/all_to_all | solution.py:523
  393.4 172.5 %all-to-all-start.5 = ((bf16[16,64,3392]{2,1,0:T(8,128)(2,1)}), bf16[16,64,3392]{2,1,0:T(8,128)(2,1)}, u32[]{:S(2)}, u32[]{:S(2)}) async-start(bf16[16,64,3392]{2,1,0:T(8,128)(2,1)} %pad_maximum_fusion), calls=%async_computation.5 | async-start | bytes 14155776 | tf_op jit(solution)/shard_map/all_to_all | solution.py:523
  410.9 13.4 %collective-permute-start.15 = (bf16[256,1024]{1,0:T(8,128)(2,1)S(1)}, bf16[256,1024]{1,0:T(8,128)(2,1)}, u32[]{:S(2)}, u32[]{:S(2)}) collective-permute-start(bf16[256,1024]{1,0:T(8,128)(2,1)S(1)} %get-tuple-element.105), channel_id=1, source_target_pairs={{0,1},{1,0},{2,3},{3,2},{4,5},{5,4},{6,7},{7,6},{8,9},{9,8},{10,11... | collective-permute-start | bytes 1572872 | tf_op jit(solution)/shard_map/ppermute | solution.py:499
  448.0 13.4 %collective-permute-start.16 = (bf16[8,64,2048]{2,1,0:T(8,128)(2,1)}, bf16[8,64,2048]{2,1,0:T(8,128)(2,1)}, u32[]{:S(2)}, u32[]{:S(2)}) collective-permute-start(bf16[8,64,2048]{2,1,0:T(8,128)(2,1)} %dynamic-slice_bitcast_fusion), channel_id=1, source_target_pairs={{0,2},{2,0},{4,6},{6,4},{8,10},{10,8},{12,14},{14,12},{16,18},{18,... | collective-permute-start | bytes 6291464 | tf_op jit(solution)/shard_map/ppermute | solution.py:502
  459.8 14.6 %collective-permute-start.20 = (bf16[256,1024]{1,0:T(8,128)(2,1)}, bf16[256,1024]{1,0:T(8,128)(2,1)}, u32[]{:S(2)}, u32[]{:S(2)}) collective-permute-start(bf16[256,1024]{1,0:T(8,128)(2,1)} %dynamic-slice_convert_fusion.1), channel_id=1, source_target_pairs={{0,1},{1,0},{2,3},{3,2},{4,5},{5,4},{6,7},{7,6},{8,9},{9,8},{10,11... | collective-permute-start | bytes 1572872 | tf_op jit(solution)/shard_map/ppermute | solution.py:499
  465.6 53.4 %collective-permute-start.19 = (bf16[264,2048]{1,0:T(8,128)(2,1)}, bf16[264,2048]{1,0:T(8,128)(2,1)}, u32[]{:S(2)}, u32[]{:S(2)}) collective-permute-start(bf16[264,2048]{1,0:T(8,128)(2,1)} %pad_maximum_fusion.6), channel_id=1, source_target_pairs={{0,4},{2,6},{4,0},{6,2},{8,12},{10,14},{12,8},{14,10},{16,20},{18,... | collective-permute-start | bytes 3244040 | tf_op jit(solution)/shard_map/ppermute | solution.py:502
  523.2 57.6 %collective-permute-start.22 = (bf16[72,2048]{1,0:T(8,128)(2,1)}, bf16[72,2048]{1,0:T(8,128)(2,1)S(1)}, u32[]{:S(2)}, u32[]{:S(2)}) collective-permute-start(bf16[72,2048]{1,0:T(8,128)(2,1)} %get-tuple-element.126), channel_id=1, source_target_pairs={{0,8},{2,10},{4,12},{6,14},{8,0},{10,2},{12,4},{14,6},{16,24},{18,... | collective-permute-start | bytes 884744 | tf_op jit(solution)/shard_map/ppermute | solution.py:502
  523.2 57.6 %collective-permute-start.23 = (bf16[72,2048]{1,0:T(8,128)(2,1)}, bf16[72,2048]{1,0:T(8,128)(2,1)S(1)}, u32[]{:S(2)}, u32[]{:S(2)}) collective-permute-start(bf16[72,2048]{1,0:T(8,128)(2,1)} %get-tuple-element.125), channel_id=1, source_target_pairs={{0,16},{2,18},{4,20},{6,22},{8,24},{10,26},{12,28},{14,30},{16,0},... | collective-permute-start | bytes 884744 | tf_op jit(solution)/shard_map/ppermute | solution.py:502
  525.6 55.2 %collective-permute-start.24 = (bf16[72,2048]{1,0:T(8,128)(2,1)S(1)}, bf16[72,2048]{1,0:T(8,128)(2,1)}, u32[]{:S(2)}, u32[]{:S(2)}) collective-permute-start(bf16[72,2048]{1,0:T(8,128)(2,1)S(1)} %get-tuple-element.124), channel_id=1, source_target_pairs={{0,24},{2,26},{4,28},{6,30},{8,16},{10,18},{12,20},{14,22},{16,8},... | collective-permute-start | bytes 884744 | tf_op jit(solution)/shard_map/ppermute | solution.py:502
  (55 other events, 579.6 us)

commit v7 on v6

--- a/solution.py
+++ b/solution.py
@@ -14,7 +14,7 @@
 LANES = 128
 GELU_SCALE = 0.7978845608028654
 GELU_CUBIC = 0.044715
-GAIN_ROWS = 16
+GAIN_ROWS = 8
 VMEM_BYTES = 48 * 2**20
 
 
@@ -436,7 +436,8 @@
     out_ref[...] = total[:, kinds * cols :]
     width = small.shape[1] // 2
     gains = jnp.concatenate([small[:1, :width], small[:1, width:]], axis=0)
-    gain_ref[...] = pltpu.roll(gains, width - place_ref[0] * rows, 1)[:, :rows]
+    shift = lax.rem(width - place_ref[0] * rows, width)
+    gain_ref[...] = pltpu.roll(gains, shift, 1)[:, :rows]
     heads, buckets = bias_ref.shape
     for head in range(heads):
         bias_ref[head : head + 1, :] = small[1:2, head * buckets : (head + 1) * buckets]
@@ -762,8 +763,9 @@
                 came = partner(away, step)
                 small = small + partner(small, step)
             else:
-                came = partner(with_small(away.reshape(-1, row_size)), step)
-                came = chain(came, input_grad)[0]
+                down_out = regroup(down_back)
+                ready = with_small(away.reshape(-1, row_size))
+                came = partner(chain(ready, (down_out, input_grad))[0], step)
                 small = small + small_of(came, away.shape[0] * shard_rows)
                 came = came[: away.shape[0] * shard_rows].reshape(away.shape)
             blocks = (stay.astype(jnp.float32) + came.astype(jnp.float32)).astype(jnp.bfloat16)
@@ -817,7 +819,7 @@
         bias_out,
         gate_grad,
         up_grad,
-        regroup(down_back),
+        down_out if dp_count == 16 else regroup(down_back),
     )
 
 

time: 594 us -> 592 us (level)
    all_to_all x5, waiting for transfers between devices: 67.5 us -> 56 us  [exchange(): return lax.all_to_all(block, 'dp', split_axis=0, concat_axis=0, tiled=True)]
    ppermute x12, waiting for transfers between devices: 118 us -> 124 us  [partner(): return lax.ppermute(block, 'dp', [(i, i ^ offset) for i in range(dp_count)])]
  transfers between devices with their start and end apart: 30 -> 30, of which waited for: 20 -> 20; matrix products, arithmetic and copies ran while one was open for 20% -> 19% of each run, Pallas kernels for 10% -> 10%
where the time goes in v7:
time: 592 us; the launch traced here: 583 us
  waiting for transfers between devices  282 us (48%)
  Pallas kernels  61.7 us (10%)
  blocking collectives  58.5 us (10%)
  starting transfers between devices  55.4 us (9%)
  matrix products  51.4 us (9%)
  other arithmetic  46.2 us (8%)
  local copies, waits for them, and re-layouts  25.1 us (4%)
    ppermute x12, waiting for transfers between devices, partner(): return lax.ppermute(block, 'dp', [(i, i ^ offset) for i in range(dp_count)])  124 us
    ppermute x13, waiting for transfers between devices, swap(): return lax.ppermute(block, 'tensor', [(0, 1), (1, 0)])  102 us
    all_to_all x1, blocking collectives, exchange(): return lax.all_to_all(block, 'dp', split_axis=0, concat_axis=0, tiled=True)  58.5 us
    all_to_all x5, waiting for transfers between devices, exchange(): return lax.all_to_all(block, 'dp', split_axis=0, concat_axis=0, tiled=True)  56 us
    dot_general x6, matrix products, dot_tn(): lax.dot_general(left, right, (((0,), (0,)), ((), ())), preferred_element_...  28.2 us
    all_to_all x5, starting transfers between devices, exchange(): return lax.all_to_all(block, 'dp', split_axis=0, concat_axis=0, tiled=True)  26.2 us
    ppermute x13, starting transfers between devices, swap(): return lax.ppermute(block, 'tensor', [(0, 1), (1, 0)])  18.9 us
    pallas_call x1, Pallas kernels, expert_backward(): pl.pallas_call(expert_backward_kernel, grid_spec=pltpu.PrefetchScalarGrid...  16.7 us
  transfers between devices with their start and end apart: 30, of which 20 were waited for; matrix products, arithmetic and copies ran while one was open for 19% of the time, Pallas kernels for 10%

profile of v7, /device:TPU:16, one launch (start us, length us, event | category | flops | bytes accessed | tf_op | source)
XLA Modules:
  0.0 582.6 jit_solution(2750967196127092879)
XLA Ops:
  13.5 8.7 %collective-permute-done.3 = bf16[264,512]{1,0:T(8,128)(2,1)S(1)} collective-permute-done((bf16[264,512]{1,0:T(8,128)(2,1)S(1)}, bf16[264,512]{1,0:T(8,128)(2,1)S(1)}, u32[]{:S(2)}, u32[]{:S(2)}) %collective-permute-start.3) | collective-permute-done | bytes 270368 | tf_op jit(solution)/shard_map/ppermute | solution.py:503
  22.2 6.4 %collective-permute-done.4 = bf16[264,512]{1,0:T(8,128)(2,1)S(1)} collective-permute-done((bf16[264,512]{1,0:T(8,128)(2,1)S(1)}, bf16[264,512]{1,0:T(8,128)(2,1)S(1)}, u32[]{:S(2)}, u32[]{:S(2)}) %collective-permute-start.4) | collective-permute-done | bytes 270368 | tf_op jit(solution)/shard_map/ppermute | solution.py:503
  42.1 54.2 %collective-permute-done.6.refs_2_ = bf16[4,264,512]{2,1,0:T(8,128)(2,1)} collective-permute-done((bf16[4,264,512]{2,1,0:T(8,128)(2,1)S(1)}, bf16[4,264,512]{2,1,0:T(8,128)(2,1)}, u32[]{:S(2)}, u32[]{:S(2)}) %collective-permute-start.6) | collective-permute-done | bytes 1081376 | tf_op jit(solution)/shard_map/ppermute | solution.py:503
  110.7 11.0 %attend_forward.1 = (bf16[512,512]{1,0:T(8,128)(2,1)}, f32[4,2,512]{2,1,0:T(2,128)}) custom-call(s32[1]{0:T(128)} %dynamic_slice.75.length_ref, bf16[512,1536]{1,0:T(8,128)(2,1)} %convolution_convert_fusion.4.joined_ref, f32[4,2,1024]{2,1,0:T(2,128)} %reshape.178.bias_ref), custom_call_target="tpu_custom_call" | custom-call | flops 2147483648 | bytes 2097152 | tf_op jit(solution)/shard_map/attend_forward/pallas_call | solution.py:104
  128.9 9.2 %collective-permute-done.8 = bf16[256,1024]{1,0:T(8,128)(2,1)} collective-permute-done((bf16[256,1024]{1,0:T(8,128)(2,1)S(1)}, bf16[256,1024]{1,0:T(8,128)(2,1)}, u32[]{:S(2)}, u32[]{:S(2)}) %collective-permute-start.8) | collective-permute-done | bytes 524320 | tf_op jit(solution)/shard_map/ppermute | solution.py:500
  143.0 6.0 %collective-permute-done.9 = bf16[256,512]{1,0:T(8,128)(2,1)S(1)} collective-permute-done((bf16[256,512]{1,0:T(8,128)(2,1)S(1)}, bf16[256,512]{1,0:T(8,128)(2,1)S(1)}, u32[]{:S(2)}, u32[]{:S(2)}) %collective-permute-start.9) | collective-permute-done | bytes 262176 | tf_op jit(solution)/shard_map/ppermute | solution.py:500
  150.6 9.5 %all-to-all-done = bf16[16,64,2816]{2,1,0:T(8,128)(2,1)} async-done(((bf16[16,64,2816]{2,1,0:T(8,128)(2,1)}), bf16[16,64,2816]{2,1,0:T(8,128)(2,1)}, u32[]{:S(2)}, u32[]{:S(2)}) %all-to-all-start) | async-done | bytes 5767200 | tf_op jit(solution)/shard_map/all_to_all | solution.py:524
  160.1 58.5 %all_to_all.30 = bf16[16,72,1024]{2,1,0:T(8,128)(2,1)} all-to-all(bf16[16,72,1024]{2,1,0:T(8,128)(2,1)S(1)} %bitcast.83), channel_id=1, replica_groups=mesh['dp'=16,'tensor'=2] {'dp'}, dimensions={0} | all-to-all | bytes 4718592 | tf_op jit(solution)/shard_map/all_to_all | solution.py:524
  227.4 26.5 %collective-permute-done.10.far_ref = bf16[1152,512]{1,0:T(8,128)(2,1)S(1)} collective-permute-done((bf16[1152,512]{1,0:T(8,128)(2,1)S(1)}, bf16[1152,512]{1,0:T(8,128)(2,1)S(1)}, u32[]{:S(2)}, u32[]{:S(2)}) %collective-permute-start.10) | collective-permute-done | bytes 1179680 | tf_op jit(solution)/shard_map/ppermute | solution.py:500
  255.4 12.9 %expert_forward.1 = (bf16[1152,1408]{1,0:T(8,128)(2,1)S(1)}, f32[1152,1408]{1,0:T(8,128)}, f32[1152,1408]{1,0:T(8,128)}) custom-call(s32[1]{0:T(128)} %bitcast.13.side_ref, bf16[1152,512]{1,0:T(8,128)(2,1)S(1)} %get-tuple-element.112.near_ref, bf16[1152,512]{1,0:T(8,128)(2,1)S(1)} %collective-permute-done.10.far_ref, ...), custom_call_target="tpu_custom_call" | custom-call | flops 6643777536 | bytes 21987328 | tf_op jit(solution)/shard_map/expert_forward/pallas_call | solution.py:312
  268.3 12.8 %collective-permute-done.11.far_ref = bf16[1152,512]{1,0:T(8,128)(2,1)S(1)} collective-permute-done((bf16[1152,512]{1,0:T(8,128)(2,1)S(1)}, bf16[1152,512]{1,0:T(8,128)(2,1)S(1)}, u32[]{:S(2)}, u32[]{:S(2)}) %collective-permute-start.11) | collective-permute-done | bytes 1179680 | tf_op jit(solution)/shard_map/ppermute | solution.py:500
  281.1 6.0 %convolution_convert_fusion.2 = bf16[1024,1408]{1,0:T(8,128)(2,1)} fusion(bf16[1152,1408]{1,0:T(8,128)(2,1)S(1)} %get-tuple-element.70, bf16[1152,512]{1,0:T(8,128)(2,1)S(1)} %collective-permute-done.11.far_ref, bf16[1152,512]{1,0:T(8,128)(2,1)S(1)} %get-tuple-element.61.near_ref, pred[]{:T(512)S(6)} %eq.79), kind=kOutput, calls=%fused_computation.9 | convolution fusion | flops 3333947392 | bytes 8486913 | tf_op jit(solution)/shard_map/dot_general | solution.py:34
  295.6 16.7 %expert_backward.1 = (bf16[1152,2816]{1,0:T(8,128)(2,1)}, f32[1152,512]{1,0:T(8,128)S(1)}, bf16[1152,512]{1,0:T(8,128)(2,1)S(1)}) custom-call(s32[1]{0:T(128)} %bitcast.13.side_ref, bf16[1152,512]{1,0:T(8,128)(2,1)S(1)} %get-tuple-element.61.near_ref, bf16[1152,512]{1,0:T(8,128)(2,1)S(1)} %copy-done.3, f32[1152,1408]{1,0:T(8,128)} %get-tuple-element.63.slope_ref, ...), custom_call_target="tpu_custom_call" | custom-call | flops 9965666304 | bytes 28114944 | tf_op jit(solution)/shard_map/expert_backward/pallas_call | solution.py:384
  321.0 19.4 %collective-permute-done.12 = bf16[1152,512]{1,0:T(8,128)(2,1)S(1)} collective-permute-done((bf16[1152,512]{1,0:T(8,128)(2,1)S(1)}, bf16[1152,512]{1,0:T(8,128)(2,1)S(1)}, u32[]{:S(2)}, u32[]{:S(2)}) %collective-permute-start.12) | collective-permute-done | bytes 1179680 | tf_op jit(solution)/shard_map/ppermute | solution.py:500
  343.3 15.6 %all-to-all-done.3 = bf16[16,64,1408]{2,1,0:T(8,128)(2,1)} async-done(((bf16[16,64,1408]{2,1,0:T(8,128)(2,1)}), bf16[16,64,1408]{2,1,0:T(8,128)(2,1)}, u32[]{:S(2)}, u32[]{:S(2)}) %all-to-all-start.3) | async-done | bytes 2883616 | tf_op jit(solution)/shard_map/all_to_all | solution.py:524
  364.0 12.6 %convolution_convert_fusion = bf16[1024,2816]{1,0:T(8,128)(2,1)} fusion(bf16[1152,2816]{1,0:T(8,128)(2,1)} %get-tuple-element.68, bf16[1152,512]{1,0:T(8,128)(2,1)S(1)} %collective-permute-done.10.far_ref, bf16[1152,512]{1,0:T(8,128)(2,1)S(1)} %get-tuple-element.112.near_ref, pred[]{:T(512)S(6)} %eq.79), kind=kOutput, calls=%fused_computation.2 | convolution fusion | flops 6657277952 | bytes 14614529 | tf_op jit(solution)/shard_map/dot_general | solution.py:34
  385.1 6.8 %all-to-all-done.4 = bf16[16,72,512]{2,1,0:T(8,128)(2,1)} async-done(((bf16[16,72,512]{2,1,0:T(8,128)(2,1)}), bf16[16,72,512]{2,1,0:T(8,128)(2,1)}, u32[]{:S(2)}, u32[]{:S(2)}) %all-to-all-start.4) | async-done | bytes 1179680 | tf_op jit(solution)/shard_map/all_to_all | solution.py:524
  400.5 6.8 %collective-permute-done.14 = bf16[256,512]{1,0:T(8,128)(2,1)S(1)} collective-permute-done((bf16[256,512]{1,0:T(8,128)(2,1)S(1)}, bf16[256,512]{1,0:T(8,128)(2,1)S(1)}, u32[]{:S(2)}, u32[]{:S(2)}) %collective-permute-start.14) | collective-permute-done | bytes 262176 | tf_op jit(solution)/shard_map/ppermute | solution.py:500
  415.0 6.8 %collective-permute-done.15 = bf16[256,1024]{1,0:T(8,128)(2,1)} collective-permute-done((bf16[256,1024]{1,0:T(8,128)(2,1)S(1)}, bf16[256,1024]{1,0:T(8,128)(2,1)}, u32[]{:S(2)}, u32[]{:S(2)}) %collective-permute-start.15) | collective-permute-done | bytes 524320 | tf_op jit(solution)/shard_map/ppermute | solution.py:500
  427.5 13.3 %attend_backward.1 = (bf16[512,1536]{1,0:T(8,128)(2,1)}, f32[4,2,1024]{2,1,0:T(2,128)}) custom-call(s32[1]{0:T(128)} %dynamic_slice.75.length_ref, bf16[512,1536]{1,0:T(8,128)(2,1)} %convolution_convert_fusion.4.joined_ref, bf16[512,512]{1,0:T(8,128)(2,1)} %convolution_convert_fusion.7.grad_ref, f32[4,2,512]{2,1,0:T(2,128)} %get-tuple-element.79.total_ref, ...), custom_call_target="tpu_custom_call" | custom-call | flops 5368709120 | bytes 3670016 | tf_op jit(solution)/shard_map/attend_backward/pallas_call | solution.py:202
  459.4 12.6 %collective-permute-done.19 = bf16[256,1024]{1,0:T(8,128)(2,1)S(1)} collective-permute-done((bf16[256,1024]{1,0:T(8,128)(2,1)S(1)}, bf16[256,1024]{1,0:T(8,128)(2,1)S(1)}, u32[]{:S(2)}, u32[]{:S(2)}) %collective-permute-start.19) | collective-permute-done | bytes 524320 | tf_op jit(solution)/shard_map/ppermute | solution.py:500
  481.3 51.6 %collective-permute-done.20 = bf16[264,2048]{1,0:T(8,128)(2,1)} collective-permute-done((bf16[264,2048]{1,0:T(8,128)(2,1)}, bf16[264,2048]{1,0:T(8,128)(2,1)}, u32[]{:S(2)}, u32[]{:S(2)}) %collective-permute-start.20) | collective-permute-done | bytes 1081376 | tf_op jit(solution)/shard_map/ppermute | solution.py:503
  540.6 23.8 %all-to-all-done.5 = bf16[16,64,3392]{2,1,0:T(8,128)(2,1)} async-done(((bf16[16,64,3392]{2,1,0:T(8,128)(2,1)}), bf16[16,64,3392]{2,1,0:T(8,128)(2,1)}, u32[]{:S(2)}, u32[]{:S(2)}) %all-to-all-start.5) | async-done | bytes 6946848 | tf_op jit(solution)/shard_map/all_to_all | solution.py:524
  569.5 8.6 %slice_convert_fusion = (f32[16,64,1408]{2,1,0:T(8,128)}, f32[16,64,1408]{2,1,0:T(8,128)}) fusion(bf16[16,64,3392]{2,1,0:T(8,128)(2,1)} %all-to-all-done.5), kind=kLoop, calls=%fused_computation.13 | loop fusion | flops 2883584 | bytes 17301504 | tf_op jit(solution)/shard_map/convert_element_type | solution.py:555
  (249 shorter events, 164.3 us)
Async XLA Ops:
  1.7 11.8 %collective-permute-start.2 = (bf16[264,512]{1,0:T(8,128)(2,1)S(1)}, bf16[264,512]{1,0:T(8,128)(2,1)S(1)}, u32[]{:S(2)}, u32[]{:S(2)}) collective-permute-start(bf16[264,512]{1,0:T(8,128)(2,1)S(1)} %get-tuple-element.123), channel_id=1, source_target_pairs={{0,8},{2,10},{4,12},{6,14},{8,0},{10,2},{12,4},{14,6},{16,24},{18,... | collective-permute-start | bytes 811016 | tf_op jit(solution)/shard_map/ppermute | solution.py:503
  3.3 18.9 %collective-permute-start.3 = (bf16[264,512]{1,0:T(8,128)(2,1)S(1)}, bf16[264,512]{1,0:T(8,128)(2,1)S(1)}, u32[]{:S(2)}, u32[]{:S(2)}) collective-permute-start(bf16[264,512]{1,0:T(8,128)(2,1)S(1)} %get-tuple-element.123), channel_id=1, source_target_pairs={{0,16},{2,18},{4,20},{6,22},{8,24},{10,26},{12,28},{14,30},{16,0},... | collective-permute-start | bytes 811016 | tf_op jit(solution)/shard_map/ppermute | solution.py:503
  3.7 24.9 %collective-permute-start.4 = (bf16[264,512]{1,0:T(8,128)(2,1)S(1)}, bf16[264,512]{1,0:T(8,128)(2,1)S(1)}, u32[]{:S(2)}, u32[]{:S(2)}) collective-permute-start(bf16[264,512]{1,0:T(8,128)(2,1)S(1)} %get-tuple-element.123), channel_id=1, source_target_pairs={{0,24},{2,26},{4,28},{6,30},{8,16},{10,18},{12,20},{14,22},{16,8},... | collective-permute-start | bytes 811016 | tf_op jit(solution)/shard_map/ppermute | solution.py:503
  28.6 131.6 %all-to-all-start = ((bf16[16,64,2816]{2,1,0:T(8,128)(2,1)}), bf16[16,64,2816]{2,1,0:T(8,128)(2,1)}, u32[]{:S(2)}, u32[]{:S(2)}) async-start(bf16[16,64,2816]{2,1,0:T(8,128)(2,1)} %pad_maximum_fusion.1), calls=%async_computation | async-start | bytes 11534336 | tf_op jit(solution)/shard_map/all_to_all | solution.py:524
  34.6 61.7 %collective-permute-start.6 = (bf16[4,264,512]{2,1,0:T(8,128)(2,1)S(1)}, bf16[4,264,512]{2,1,0:T(8,128)(2,1)}, u32[]{:S(2)}, u32[]{:S(2)}) collective-permute-start(bf16[4,264,512]{2,1,0:T(8,128)(2,1)S(1)} %pad_maximum_fusion.5.refs_0_), channel_id=1, source_target_pairs={{0,4},{2,6},{4,0},{6,2},{8,12},{10,14},{12,8},{14,10},{16,20},{18,... | collective-permute-start | bytes 3244040 | tf_op jit(solution)/shard_map/ppermute | solution.py:503
  37.8 88.1 %collective-permute-start = (bf16[256,512]{1,0:T(8,128)(2,1)}, bf16[256,512]{1,0:T(8,128)(2,1)}, u32[]{:S(2)}, u32[]{:S(2)}) collective-permute-start(bf16[256,512]{1,0:T(8,128)(2,1)} %get-tuple-element.121), channel_id=1, source_target_pairs={{0,1},{1,0},{2,3},{3,2},{4,5},{5,4},{6,7},{7,6},{8,9},{9,8},{10,11... | collective-permute-start | bytes 786440 | tf_op jit(solution)/shard_map/ppermute | solution.py:500
  39.3 58.7 %collective-permute-start.1 = (bf16[256,1024]{1,0:T(8,128)(2,1)S(1)}, bf16[256,1024]{1,0:T(8,128)(2,1)S(1)}, u32[]{:S(2)}, u32[]{:S(2)}) collective-permute-start(bf16[256,1024]{1,0:T(8,128)(2,1)S(1)} %copy-done.10), channel_id=1, source_target_pairs={{0,1},{1,0},{2,3},{3,2},{4,5},{5,4},{6,7},{7,6},{8,9},{9,8},{10,11... | collective-permute-start | bytes 1572872 | tf_op jit(solution)/shard_map/ppermute | solution.py:500
  42.0 56.5 %collective-permute-start.5 = (bf16[4,264,512]{2,1,0:T(8,128)(2,1)S(1)}, bf16[4,264,512]{2,1,0:T(8,128)(2,1)}, u32[]{:S(2)}, u32[]{:S(2)}) collective-permute-start(bf16[4,264,512]{2,1,0:T(8,128)(2,1)S(1)} %pad_maximum_fusion.5.refs_0_), channel_id=1, source_target_pairs={{0,2},{2,0},{4,6},{6,4},{8,10},{10,8},{12,14},{14,12},{16,18},{18,... | collective-permute-start | bytes 3244040 | tf_op jit(solution)/shard_map/ppermute | solution.py:503
  124.0 14.1 %collective-permute-start.8 = (bf16[256,1024]{1,0:T(8,128)(2,1)S(1)}, bf16[256,1024]{1,0:T(8,128)(2,1)}, u32[]{:S(2)}, u32[]{:S(2)}) collective-permute-start(bf16[256,1024]{1,0:T(8,128)(2,1)S(1)} %dynamic-slice_convert_fusion.2), channel_id=1, source_target_pairs={{0,1},{1,0},{2,3},{3,2},{4,5},{5,4},{6,7},{7,6},{8,9},{9,8},{10,11... | collective-permute-start | bytes 1572872 | tf_op jit(solution)/shard_map/ppermute | solution.py:500
  218.6 69.9 %all-to-all-start.2 = ((bf16[16,64,1408]{2,1,0:T(8,128)(2,1)}), bf16[16,64,1408]{2,1,0:T(8,128)(2,1)}, u32[]{:S(2)}, u32[]{:S(2)}) async-start(bf16[16,64,1408]{2,1,0:T(8,128)(2,1)} %param.25), calls=%async_computation.2 | async-start | bytes 5767168 | tf_op jit(solution)/shard_map/all_to_all | solution.py:524
  225.9 28.1 %collective-permute-start.10 = (bf16[1152,512]{1,0:T(8,128)(2,1)S(1)}, bf16[1152,512]{1,0:T(8,128)(2,1)S(1)}, u32[]{:S(2)}, u32[]{:S(2)}) collective-permute-start(bf16[1152,512]{1,0:T(8,128)(2,1)S(1)} %get-tuple-element.112.near_ref), channel_id=1, source_target_pairs={{0,1},{1,0},{2,3},{3,2},{4,5},{5,4},{6,7},{7,6},{8,9},{9,8},{10,11... | collective-permute-start | bytes 3538952 | tf_op jit(solution)/shard_map/ppermute | solution.py:500
  253.9 27.2 %collective-permute-start.11 = (bf16[1152,512]{1,0:T(8,128)(2,1)S(1)}, bf16[1152,512]{1,0:T(8,128)(2,1)S(1)}, u32[]{:S(2)}, u32[]{:S(2)}) collective-permute-start(bf16[1152,512]{1,0:T(8,128)(2,1)S(1)} %get-tuple-element.61.near_ref), channel_id=1, source_target_pairs={{0,1},{1,0},{2,3},{3,2},{4,5},{5,4},{6,7},{7,6},{8,9},{9,8},{10,11... | collective-permute-start | bytes 3538952 | tf_op jit(solution)/shard_map/ppermute | solution.py:500
  288.5 70.4 %all-to-all-start.3 = ((bf16[16,64,1408]{2,1,0:T(8,128)(2,1)}), bf16[16,64,1408]{2,1,0:T(8,128)(2,1)}, u32[]{:S(2)}, u32[]{:S(2)}) async-start(bf16[16,64,1408]{2,1,0:T(8,128)(2,1)} %bitcast.91), calls=%async_computation.3 | async-start | bytes 5767168 | tf_op jit(solution)/shard_map/all_to_all | solution.py:524
  312.3 28.1 %collective-permute-start.12 = (bf16[1152,512]{1,0:T(8,128)(2,1)S(1)}, bf16[1152,512]{1,0:T(8,128)(2,1)S(1)}, u32[]{:S(2)}, u32[]{:S(2)}) collective-permute-start(bf16[1152,512]{1,0:T(8,128)(2,1)S(1)} %get-tuple-element.71), channel_id=1, source_target_pairs={{0,1},{1,0},{2,3},{3,2},{4,5},{5,4},{6,7},{7,6},{8,9},{9,8},{10,11... | collective-permute-start | bytes 3538952 | tf_op jit(solution)/shard_map/ppermute | solution.py:500
  340.4 36.2 %collective-permute-start.13 = (bf16[1152,512]{1,0:T(8,128)(2,1)}, bf16[1152,512]{1,0:T(8,128)(2,1)S(1)}, u32[]{:S(2)}, u32[]{:S(2)}) collective-permute-start(bf16[1152,512]{1,0:T(8,128)(2,1)} %dynamic-slice_convert_fusion), channel_id=1, source_target_pairs={{0,1},{1,0},{2,3},{3,2},{4,5},{5,4},{6,7},{7,6},{8,9},{9,8},{10,11... | collective-permute-start | bytes 3538952 | tf_op jit(solution)/shard_map/ppermute | solution.py:500
  358.9 33.0 %all-to-all-start.4 = ((bf16[16,72,512]{2,1,0:T(8,128)(2,1)}), bf16[16,72,512]{2,1,0:T(8,128)(2,1)}, u32[]{:S(2)}, u32[]{:S(2)}) async-start(bf16[16,72,512]{2,1,0:T(8,128)(2,1)} %bitcast.20), calls=%async_computation.4 | async-start | bytes 2359296 | tf_op jit(solution)/shard_map/all_to_all | solution.py:524
  391.9 172.5 %all-to-all-start.5 = ((bf16[16,64,3392]{2,1,0:T(8,128)(2,1)}), bf16[16,64,3392]{2,1,0:T(8,128)(2,1)}, u32[]{:S(2)}, u32[]{:S(2)}) async-start(bf16[16,64,3392]{2,1,0:T(8,128)(2,1)} %pad_maximum_fusion), calls=%async_computation.5 | async-start | bytes 14155776 | tf_op jit(solution)/shard_map/all_to_all | solution.py:524
  408.4 13.4 %collective-permute-start.15 = (bf16[256,1024]{1,0:T(8,128)(2,1)S(1)}, bf16[256,1024]{1,0:T(8,128)(2,1)}, u32[]{:S(2)}, u32[]{:S(2)}) collective-permute-start(bf16[256,1024]{1,0:T(8,128)(2,1)S(1)} %get-tuple-element.105), channel_id=1, source_target_pairs={{0,1},{1,0},{2,3},{3,2},{4,5},{5,4},{6,7},{7,6},{8,9},{9,8},{10,11... | collective-permute-start | bytes 1572872 | tf_op jit(solution)/shard_map/ppermute | solution.py:500
  446.6 28.4 %collective-permute-start.16 = (bf16[8,64,2048]{2,1,0:T(8,128)(2,1)}, bf16[8,64,2048]{2,1,0:T(8,128)(2,1)}, u32[]{:S(2)}, u32[]{:S(2)}) collective-permute-start(bf16[8,64,2048]{2,1,0:T(8,128)(2,1)} %dynamic-slice_bitcast_fusion), channel_id=1, source_target_pairs={{0,2},{2,0},{4,6},{6,4},{8,10},{10,8},{12,14},{14,12},{16,18},{18,... | collective-permute-start | bytes 6291464 | tf_op jit(solution)/shard_map/ppermute | solution.py:503
  457.8 14.3 %collective-permute-start.19 = (bf16[256,1024]{1,0:T(8,128)(2,1)S(1)}, bf16[256,1024]{1,0:T(8,128)(2,1)S(1)}, u32[]{:S(2)}, u32[]{:S(2)}) collective-permute-start(bf16[256,1024]{1,0:T(8,128)(2,1)S(1)} %dynamic-slice_convert_fusion.1), channel_id=1, source_target_pairs={{0,1},{1,0},{2,3},{3,2},{4,5},{5,4},{6,7},{7,6},{8,9},{9,8},{10,11... | collective-permute-start | bytes 1572872 | tf_op jit(solution)/shard_map/ppermute | solution.py:500
  479.8 53.1 %collective-permute-start.20 = (bf16[264,2048]{1,0:T(8,128)(2,1)}, bf16[264,2048]{1,0:T(8,128)(2,1)}, u32[]{:S(2)}, u32[]{:S(2)}) collective-permute-start(bf16[264,2048]{1,0:T(8,128)(2,1)} %pad_maximum_fusion.6), channel_id=1, source_target_pairs={{0,4},{2,6},{4,0},{6,2},{8,12},{10,14},{12,8},{14,10},{16,20},{18,... | collective-permute-start | bytes 3244040 | tf_op jit(solution)/shard_map/ppermute | solution.py:503
  537.1 42.1 %collective-permute-start.22 = (bf16[72,2048]{1,0:T(8,128)(2,1)}, bf16[72,2048]{1,0:T(8,128)(2,1)S(1)}, u32[]{:S(2)}, u32[]{:S(2)}) collective-permute-start(bf16[72,2048]{1,0:T(8,128)(2,1)} %get-tuple-element.126), channel_id=1, source_target_pairs={{0,8},{2,10},{4,12},{6,14},{8,0},{10,2},{12,4},{14,6},{16,24},{18,... | collective-permute-start | bytes 884744 | tf_op jit(solution)/shard_map/ppermute | solution.py:503
  537.1 42.1 %collective-permute-start.23 = (bf16[72,2048]{1,0:T(8,128)(2,1)}, bf16[72,2048]{1,0:T(8,128)(2,1)S(1)}, u32[]{:S(2)}, u32[]{:S(2)}) collective-permute-start(bf16[72,2048]{1,0:T(8,128)(2,1)} %get-tuple-element.125), channel_id=1, source_target_pairs={{0,16},{2,18},{4,20},{6,22},{8,24},{10,26},{12,28},{14,30},{16,0},... | collective-permute-start | bytes 884744 | tf_op jit(solution)/shard_map/ppermute | solution.py:503
  537.1 42.2 %collective-permute-start.24 = (bf16[72,2048]{1,0:T(8,128)(2,1)S(1)}, bf16[72,2048]{1,0:T(8,128)(2,1)}, u32[]{:S(2)}, u32[]{:S(2)}) collective-permute-start(bf16[72,2048]{1,0:T(8,128)(2,1)S(1)} %get-tuple-element.124), channel_id=1, source_target_pairs={{0,24},{2,26},{4,28},{6,30},{8,16},{10,18},{12,20},{14,22},{16,8},... | collective-permute-start | bytes 884744 | tf_op jit(solution)/shard_map/ppermute | solution.py:503
  (55 other events, 587.6 us)

commit v8 on v7

--- a/solution.py
+++ b/solution.py
@@ -420,27 +420,35 @@
 
 
 def finish_kernel(place_ref, stay_ref, *refs):
-    arrivals, small_ref, qkv_ref, out_ref, gain_ref, bias_ref = refs[:3], *refs[3:]
+    arrivals = refs[:3]
+    small_ref, qkv_ref, out_ref, gain_ref, bias_ref, total_ref = refs[3:]
     kinds, rows, cols = qkv_ref.shape
+    row_size = stay_ref.shape[1]
     small_rows = small_ref.shape[0]
     total = stay_ref[...].astype(jnp.float32)
     small = small_ref[...]
     for arrival in arrivals:
-        total = total + arrival[:rows].astype(jnp.float32)
-        extra = arrival[rows : rows + 2 * small_rows].astype(jnp.float32)
-        small = small + extra[:small_rows] + extra[small_rows:]
+        total = total + arrival[:, :row_size].astype(jnp.float32)
+        extra = arrival[:, row_size:].astype(jnp.float32)
+        small = small + extra[:small_rows] + extra[small_rows : 2 * small_rows]
     for kind in range(kinds):
         for pair in range(cols // LANES):
             first = (kinds * pair + kind) * LANES
             qkv_ref[kind, :, pair * LANES : (pair + 1) * LANES] = total[:, first : first + LANES]
     out_ref[...] = total[:, kinds * cols :]
-    width = small.shape[1] // 2
-    gains = jnp.concatenate([small[:1, :width], small[:1, width:]], axis=0)
-    shift = lax.rem(width - place_ref[0] * rows, width)
-    gain_ref[...] = pltpu.roll(gains, shift, 1)[:, :rows]
+    total_ref[...] = small
+    norm_rows = row_size // LANES // 2
+    first = place_ref[0] * rows
+    for norm in range(2):
+        row = total_ref[pl.ds(norm * norm_rows + first // LANES, 1), :]
+        shift = lax.rem(LANES - lax.rem(first, LANES), LANES)
+        gain_ref[norm : norm + 1, :] = pltpu.roll(row, shift, 1)[:, :rows]
     heads, buckets = bias_ref.shape
     for head in range(heads):
-        bias_ref[head : head + 1, :] = small[1:2, head * buckets : (head + 1) * buckets]
+        row, lane = divmod(head * buckets, LANES)
+        bias_ref[head : head + 1, :] = small[
+            2 * norm_rows + row : 2 * norm_rows + row + 1, lane : lane + buckets
+        ]
 
 
 def finish(place, stay, arrivals, small, cols, bias_shape):
@@ -456,6 +464,7 @@
             jax.ShapeDtypeStruct((2, rows), jnp.float32),
             jax.ShapeDtypeStruct(bias_shape, jnp.float32),
         ],
+        scratch_shapes=[pltpu.VMEM(small.shape, jnp.float32)],
         name="finish",
     )(place, stay, *arrivals, small)
 
@@ -770,10 +779,17 @@
                 came = came[: away.shape[0] * shard_rows].reshape(away.shape)
             blocks = (stay.astype(jnp.float32) + came.astype(jnp.float32)).astype(jnp.bfloat16)
         outer = dp_index // 4
+        high = lax.reduce_precision(small, 8, 7)
+        beside = jnp.concatenate([high, small - high], axis=0).astype(jnp.bfloat16)
+        beside = beside.reshape(-1, LANES)
+        beside = jnp.pad(beside, ((0, shard_rows - beside.shape[0]), (0, 0)))
         leaving = [
-            with_small(lax.dynamic_index_in_dim(blocks, outer ^ k, 0, keepdims=False))
+            jnp.concatenate(
+                [lax.dynamic_index_in_dim(blocks, outer ^ k, 0, keepdims=False), beside], axis=1
+            )
             for k in range(1, 4)
         ]
+        small = small.reshape(-1, LANES)
         stay = lax.dynamic_index_in_dim(blocks, outer, 0, keepdims=False)
         arrived_back = chain(arrived_back, leaving)[0]
         came = [partner(piece, 4 * k) for k, piece in zip(range(1, 4), leaving, strict=True)]

time: 592 us -> 591 us (level)
  no operation moved by 1% of the time
where the time goes in v8:
time: 591 us; the launch traced here: 581 us
  waiting for transfers between devices  282 us (48%)
  Pallas kernels  61.5 us (10%)
  blocking collectives  58.4 us (10%)
  starting transfers between devices  55.4 us (9%)
  matrix products  51.5 us (9%)
  other arithmetic  45.2 us (8%)
  local copies, waits for them, and re-layouts  25 us (4%)
    ppermute x12, waiting for transfers between devices, partner(): return lax.ppermute(block, 'dp', [(i, i ^ offset) for i in range(dp_count)])  124 us
    ppermute x13, waiting for transfers between devices, swap(): return lax.ppermute(block, 'tensor', [(0, 1), (1, 0)])  102 us
    all_to_all x1, blocking collectives, exchange(): return lax.all_to_all(block, 'dp', split_axis=0, concat_axis=0, tiled=True)  58.4 us
    all_to_all x5, waiting for transfers between devices, exchange(): return lax.all_to_all(block, 'dp', split_axis=0, concat_axis=0, tiled=True)  55.6 us
    dot_general x6, matrix products, dot_tn(): lax.dot_general(left, right, (((0,), (0,)), ((), ())), preferred_element_...  28.3 us
    all_to_all x5, starting transfers between devices, exchange(): return lax.all_to_all(block, 'dp', split_axis=0, concat_axis=0, tiled=True)  26.2 us
    ppermute x13, starting transfers between devices, swap(): return lax.ppermute(block, 'tensor', [(0, 1), (1, 0)])  18.9 us
    pallas_call x1, Pallas kernels, expert_backward(): pl.pallas_call(expert_backward_kernel, grid_spec=pltpu.PrefetchScalarGrid...  16.7 us
  transfers between devices with their start and end apart: 30, of which 20 were waited for; matrix products, arithmetic and copies ran while one was open for 19% of the time, Pallas kernels for 10%

profile of v8, /device:TPU:16, one launch (start us, length us, event | category | flops | bytes accessed | tf_op | source)
XLA Modules:
  0.0 581.0 jit_solution(1852697208287464403)
XLA Ops:
  13.5 8.7 %collective-permute-done.3 = bf16[264,512]{1,0:T(8,128)(2,1)S(1)} collective-permute-done((bf16[264,512]{1,0:T(8,128)(2,1)S(1)}, bf16[264,512]{1,0:T(8,128)(2,1)S(1)}, u32[]{:S(2)}, u32[]{:S(2)}) %collective-permute-start.3) | collective-permute-done | bytes 270368 | tf_op jit(solution)/shard_map/ppermute | solution.py:512
  22.2 6.4 %collective-permute-done.4 = bf16[264,512]{1,0:T(8,128)(2,1)S(1)} collective-permute-done((bf16[264,512]{1,0:T(8,128)(2,1)S(1)}, bf16[264,512]{1,0:T(8,128)(2,1)S(1)}, u32[]{:S(2)}, u32[]{:S(2)}) %collective-permute-start.4) | collective-permute-done | bytes 270368 | tf_op jit(solution)/shard_map/ppermute | solution.py:512
  42.0 54.3 %collective-permute-done.6.refs_2_ = bf16[4,264,512]{2,1,0:T(8,128)(2,1)} collective-permute-done((bf16[4,264,512]{2,1,0:T(8,128)(2,1)S(1)}, bf16[4,264,512]{2,1,0:T(8,128)(2,1)}, u32[]{:S(2)}, u32[]{:S(2)}) %collective-permute-start.6) | collective-permute-done | bytes 1081376 | tf_op jit(solution)/shard_map/ppermute | solution.py:512
  110.7 10.9 %attend_forward.1 = (bf16[512,512]{1,0:T(8,128)(2,1)}, f32[4,2,512]{2,1,0:T(2,128)}) custom-call(s32[1]{0:T(128)} %dynamic_slice.75.length_ref, bf16[512,1536]{1,0:T(8,128)(2,1)} %convolution_convert_fusion.4.joined_ref, f32[4,2,1024]{2,1,0:T(2,128)} %reshape.184.bias_ref), custom_call_target="tpu_custom_call" | custom-call | flops 2147483648 | bytes 2097152 | tf_op jit(solution)/shard_map/attend_forward/pallas_call | solution.py:104
  128.8 9.2 %collective-permute-done.8 = bf16[256,1024]{1,0:T(8,128)(2,1)} collective-permute-done((bf16[256,1024]{1,0:T(8,128)(2,1)S(1)}, bf16[256,1024]{1,0:T(8,128)(2,1)}, u32[]{:S(2)}, u32[]{:S(2)}) %collective-permute-start.8) | collective-permute-done | bytes 524320 | tf_op jit(solution)/shard_map/ppermute | solution.py:509
  142.9 6.0 %collective-permute-done.9 = bf16[256,512]{1,0:T(8,128)(2,1)S(1)} collective-permute-done((bf16[256,512]{1,0:T(8,128)(2,1)S(1)}, bf16[256,512]{1,0:T(8,128)(2,1)S(1)}, u32[]{:S(2)}, u32[]{:S(2)}) %collective-permute-start.9) | collective-permute-done | bytes 262176 | tf_op jit(solution)/shard_map/ppermute | solution.py:509
  150.6 9.6 %all-to-all-done = bf16[16,64,2816]{2,1,0:T(8,128)(2,1)} async-done(((bf16[16,64,2816]{2,1,0:T(8,128)(2,1)}), bf16[16,64,2816]{2,1,0:T(8,128)(2,1)}, u32[]{:S(2)}, u32[]{:S(2)}) %all-to-all-start) | async-done | bytes 5767200 | tf_op jit(solution)/shard_map/all_to_all | solution.py:533
  160.1 58.4 %all_to_all.30 = bf16[16,72,1024]{2,1,0:T(8,128)(2,1)} all-to-all(bf16[16,72,1024]{2,1,0:T(8,128)(2,1)S(1)} %bitcast.83), channel_id=1, replica_groups=mesh['dp'=16,'tensor'=2] {'dp'}, dimensions={0} | all-to-all | bytes 4718592 | tf_op jit(solution)/shard_map/all_to_all | solution.py:533
  227.4 26.5 %collective-permute-done.10.far_ref = bf16[1152,512]{1,0:T(8,128)(2,1)S(1)} collective-permute-done((bf16[1152,512]{1,0:T(8,128)(2,1)S(1)}, bf16[1152,512]{1,0:T(8,128)(2,1)S(1)}, u32[]{:S(2)}, u32[]{:S(2)}) %collective-permute-start.10) | collective-permute-done | bytes 1179680 | tf_op jit(solution)/shard_map/ppermute | solution.py:509
  255.4 12.9 %expert_forward.1 = (bf16[1152,1408]{1,0:T(8,128)(2,1)S(1)}, f32[1152,1408]{1,0:T(8,128)}, f32[1152,1408]{1,0:T(8,128)}) custom-call(s32[1]{0:T(128)} %bitcast.13.side_ref, bf16[1152,512]{1,0:T(8,128)(2,1)S(1)} %get-tuple-element.112.near_ref, bf16[1152,512]{1,0:T(8,128)(2,1)S(1)} %collective-permute-done.10.far_ref, ...), custom_call_target="tpu_custom_call" | custom-call | flops 6643777536 | bytes 21987328 | tf_op jit(solution)/shard_map/expert_forward/pallas_call | solution.py:312
  268.3 12.8 %collective-permute-done.11.far_ref = bf16[1152,512]{1,0:T(8,128)(2,1)S(1)} collective-permute-done((bf16[1152,512]{1,0:T(8,128)(2,1)S(1)}, bf16[1152,512]{1,0:T(8,128)(2,1)S(1)}, u32[]{:S(2)}, u32[]{:S(2)}) %collective-permute-start.11) | collective-permute-done | bytes 1179680 | tf_op jit(solution)/shard_map/ppermute | solution.py:509
  281.1 6.0 %convolution_convert_fusion.2 = bf16[1024,1408]{1,0:T(8,128)(2,1)} fusion(bf16[1152,1408]{1,0:T(8,128)(2,1)S(1)} %get-tuple-element.70, bf16[1152,512]{1,0:T(8,128)(2,1)S(1)} %collective-permute-done.11.far_ref, bf16[1152,512]{1,0:T(8,128)(2,1)S(1)} %get-tuple-element.61.near_ref, pred[]{:T(512)S(6)} %eq.79), kind=kOutput, calls=%fused_computation.9 | convolution fusion | flops 3333947392 | bytes 8486913 | tf_op jit(solution)/shard_map/dot_general | solution.py:34
  295.5 16.7 %expert_backward.1 = (bf16[1152,2816]{1,0:T(8,128)(2,1)}, f32[1152,512]{1,0:T(8,128)S(1)}, bf16[1152,512]{1,0:T(8,128)(2,1)S(1)}) custom-call(s32[1]{0:T(128)} %bitcast.13.side_ref, bf16[1152,512]{1,0:T(8,128)(2,1)S(1)} %get-tuple-element.61.near_ref, bf16[1152,512]{1,0:T(8,128)(2,1)S(1)} %copy-done.3, f32[1152,1408]{1,0:T(8,128)} %get-tuple-element.63.slope_ref, ...), custom_call_target="tpu_custom_call" | custom-call | flops 9965666304 | bytes 28114944 | tf_op jit(solution)/shard_map/expert_backward/pallas_call | solution.py:384
  321.0 19.4 %collective-permute-done.12 = bf16[1152,512]{1,0:T(8,128)(2,1)S(1)} collective-permute-done((bf16[1152,512]{1,0:T(8,128)(2,1)S(1)}, bf16[1152,512]{1,0:T(8,128)(2,1)S(1)}, u32[]{:S(2)}, u32[]{:S(2)}) %collective-permute-start.12) | collective-permute-done | bytes 1179680 | tf_op jit(solution)/shard_map/ppermute | solution.py:509
  343.3 15.6 %all-to-all-done.3 = bf16[16,64,1408]{2,1,0:T(8,128)(2,1)} async-done(((bf16[16,64,1408]{2,1,0:T(8,128)(2,1)}), bf16[16,64,1408]{2,1,0:T(8,128)(2,1)}, u32[]{:S(2)}, u32[]{:S(2)}) %all-to-all-start.3) | async-done | bytes 2883616 | tf_op jit(solution)/shard_map/all_to_all | solution.py:533
  363.9 12.6 %convolution_convert_fusion = bf16[1024,2816]{1,0:T(8,128)(2,1)} fusion(bf16[1152,2816]{1,0:T(8,128)(2,1)} %get-tuple-element.68, bf16[1152,512]{1,0:T(8,128)(2,1)S(1)} %collective-permute-done.10.far_ref, bf16[1152,512]{1,0:T(8,128)(2,1)S(1)} %get-tuple-element.112.near_ref, pred[]{:T(512)S(6)} %eq.79), kind=kOutput, calls=%fused_computation.2 | convolution fusion | flops 6657277952 | bytes 14614529 | tf_op jit(solution)/shard_map/dot_general | solution.py:34
  385.1 6.8 %all-to-all-done.4 = bf16[16,72,512]{2,1,0:T(8,128)(2,1)} async-done(((bf16[16,72,512]{2,1,0:T(8,128)(2,1)}), bf16[16,72,512]{2,1,0:T(8,128)(2,1)}, u32[]{:S(2)}, u32[]{:S(2)}) %all-to-all-start.4) | async-done | bytes 1179680 | tf_op jit(solution)/shard_map/all_to_all | solution.py:533
  400.5 6.8 %collective-permute-done.14 = bf16[256,512]{1,0:T(8,128)(2,1)S(1)} collective-permute-done((bf16[256,512]{1,0:T(8,128)(2,1)S(1)}, bf16[256,512]{1,0:T(8,128)(2,1)S(1)}, u32[]{:S(2)}, u32[]{:S(2)}) %collective-permute-start.14) | collective-permute-done | bytes 262176 | tf_op jit(solution)/shard_map/ppermute | solution.py:509
  414.9 6.8 %collective-permute-done.15 = bf16[256,1024]{1,0:T(8,128)(2,1)} collective-permute-done((bf16[256,1024]{1,0:T(8,128)(2,1)S(1)}, bf16[256,1024]{1,0:T(8,128)(2,1)}, u32[]{:S(2)}, u32[]{:S(2)}) %collective-permute-start.15) | collective-permute-done | bytes 524320 | tf_op jit(solution)/shard_map/ppermute | solution.py:509
  427.5 13.2 %attend_backward.1 = (bf16[512,1536]{1,0:T(8,128)(2,1)}, f32[4,2,1024]{2,1,0:T(2,128)}) custom-call(s32[1]{0:T(128)} %dynamic_slice.75.length_ref, bf16[512,1536]{1,0:T(8,128)(2,1)} %convolution_convert_fusion.4.joined_ref, bf16[512,512]{1,0:T(8,128)(2,1)} %convolution_convert_fusion.7.grad_ref, f32[4,2,512]{2,1,0:T(2,128)} %get-tuple-element.79.total_ref, ...), custom_call_target="tpu_custom_call" | custom-call | flops 5368709120 | bytes 3670016 | tf_op jit(solution)/shard_map/attend_backward/pallas_call | solution.py:202
  459.3 12.6 %collective-permute-done.19 = bf16[256,1024]{1,0:T(8,128)(2,1)S(1)} collective-permute-done((bf16[256,1024]{1,0:T(8,128)(2,1)S(1)}, bf16[256,1024]{1,0:T(8,128)(2,1)S(1)}, u32[]{:S(2)}, u32[]{:S(2)}) %collective-permute-start.19) | collective-permute-done | bytes 524320 | tf_op jit(solution)/shard_map/ppermute | solution.py:509
  481.1 51.6 %collective-permute-done.20 = bf16[264,2048]{1,0:T(8,128)(2,1)} collective-permute-done((bf16[264,2048]{1,0:T(8,128)(2,1)}, bf16[264,2048]{1,0:T(8,128)(2,1)}, u32[]{:S(2)}, u32[]{:S(2)}) %collective-permute-start.20) | collective-permute-done | bytes 1081376 | tf_op jit(solution)/shard_map/ppermute | solution.py:512
  540.3 23.3 %all-to-all-done.5 = bf16[16,64,3392]{2,1,0:T(8,128)(2,1)} async-done(((bf16[16,64,3392]{2,1,0:T(8,128)(2,1)}), bf16[16,64,3392]{2,1,0:T(8,128)(2,1)}, u32[]{:S(2)}, u32[]{:S(2)}) %all-to-all-start.5) | async-done | bytes 6946848 | tf_op jit(solution)/shard_map/all_to_all | solution.py:533
  568.8 8.6 %slice_convert_fusion = (f32[16,64,1408]{2,1,0:T(8,128)}, f32[16,64,1408]{2,1,0:T(8,128)}) fusion(bf16[16,64,3392]{2,1,0:T(8,128)(2,1)} %all-to-all-done.5), kind=kLoop, calls=%fused_computation.13 | loop fusion | flops 2883584 | bytes 17301504 | tf_op jit(solution)/shard_map/convert_element_type | solution.py:564
  (245 shorter events, 163.2 us)
Async XLA Ops:
  1.7 11.8 %collective-permute-start.2 = (bf16[264,512]{1,0:T(8,128)(2,1)S(1)}, bf16[264,512]{1,0:T(8,128)(2,1)S(1)}, u32[]{:S(2)}, u32[]{:S(2)}) collective-permute-start(bf16[264,512]{1,0:T(8,128)(2,1)S(1)} %get-tuple-element.123), channel_id=1, source_target_pairs={{0,8},{2,10},{4,12},{6,14},{8,0},{10,2},{12,4},{14,6},{16,24},{18,... | collective-permute-start | bytes 811016 | tf_op jit(solution)/shard_map/ppermute | solution.py:512
  3.3 18.9 %collective-permute-start.3 = (bf16[264,512]{1,0:T(8,128)(2,1)S(1)}, bf16[264,512]{1,0:T(8,128)(2,1)S(1)}, u32[]{:S(2)}, u32[]{:S(2)}) collective-permute-start(bf16[264,512]{1,0:T(8,128)(2,1)S(1)} %get-tuple-element.123), channel_id=1, source_target_pairs={{0,16},{2,18},{4,20},{6,22},{8,24},{10,26},{12,28},{14,30},{16,0},... | collective-permute-start | bytes 811016 | tf_op jit(solution)/shard_map/ppermute | solution.py:512
  3.7 24.9 %collective-permute-start.4 = (bf16[264,512]{1,0:T(8,128)(2,1)S(1)}, bf16[264,512]{1,0:T(8,128)(2,1)S(1)}, u32[]{:S(2)}, u32[]{:S(2)}) collective-permute-start(bf16[264,512]{1,0:T(8,128)(2,1)S(1)} %get-tuple-element.123), channel_id=1, source_target_pairs={{0,24},{2,26},{4,28},{6,30},{8,16},{10,18},{12,20},{14,22},{16,8},... | collective-permute-start | bytes 811016 | tf_op jit(solution)/shard_map/ppermute | solution.py:512
  28.6 131.6 %all-to-all-start = ((bf16[16,64,2816]{2,1,0:T(8,128)(2,1)}), bf16[16,64,2816]{2,1,0:T(8,128)(2,1)}, u32[]{:S(2)}, u32[]{:S(2)}) async-start(bf16[16,64,2816]{2,1,0:T(8,128)(2,1)} %pad_maximum_fusion.1), calls=%async_computation | async-start | bytes 11534336 | tf_op jit(solution)/shard_map/all_to_all | solution.py:533
  34.5 61.8 %collective-permute-start.6 = (bf16[4,264,512]{2,1,0:T(8,128)(2,1)S(1)}, bf16[4,264,512]{2,1,0:T(8,128)(2,1)}, u32[]{:S(2)}, u32[]{:S(2)}) collective-permute-start(bf16[4,264,512]{2,1,0:T(8,128)(2,1)S(1)} %pad_maximum_fusion.5.refs_0_), channel_id=1, source_target_pairs={{0,4},{2,6},{4,0},{6,2},{8,12},{10,14},{12,8},{14,10},{16,20},{18,... | collective-permute-start | bytes 3244040 | tf_op jit(solution)/shard_map/ppermute | solution.py:512
  37.7 88.2 %collective-permute-start = (bf16[256,512]{1,0:T(8,128)(2,1)}, bf16[256,512]{1,0:T(8,128)(2,1)}, u32[]{:S(2)}, u32[]{:S(2)}) collective-permute-start(bf16[256,512]{1,0:T(8,128)(2,1)} %get-tuple-element.121), channel_id=1, source_target_pairs={{0,1},{1,0},{2,3},{3,2},{4,5},{5,4},{6,7},{7,6},{8,9},{9,8},{10,11... | collective-permute-start | bytes 786440 | tf_op jit(solution)/shard_map/ppermute | solution.py:509
  39.2 58.9 %collective-permute-start.1 = (bf16[256,1024]{1,0:T(8,128)(2,1)S(1)}, bf16[256,1024]{1,0:T(8,128)(2,1)S(1)}, u32[]{:S(2)}, u32[]{:S(2)}) collective-permute-start(bf16[256,1024]{1,0:T(8,128)(2,1)S(1)} %copy-done.10), channel_id=1, source_target_pairs={{0,1},{1,0},{2,3},{3,2},{4,5},{5,4},{6,7},{7,6},{8,9},{9,8},{10,11... | collective-permute-start | bytes 1572872 | tf_op jit(solution)/shard_map/ppermute | solution.py:509
  41.9 56.6 %collective-permute-start.5 = (bf16[4,264,512]{2,1,0:T(8,128)(2,1)S(1)}, bf16[4,264,512]{2,1,0:T(8,128)(2,1)}, u32[]{:S(2)}, u32[]{:S(2)}) collective-permute-start(bf16[4,264,512]{2,1,0:T(8,128)(2,1)S(1)} %pad_maximum_fusion.5.refs_0_), channel_id=1, source_target_pairs={{0,2},{2,0},{4,6},{6,4},{8,10},{10,8},{12,14},{14,12},{16,18},{18,... | collective-permute-start | bytes 3244040 | tf_op jit(solution)/shard_map/ppermute | solution.py:512
  123.9 14.1 %collective-permute-start.8 = (bf16[256,1024]{1,0:T(8,128)(2,1)S(1)}, bf16[256,1024]{1,0:T(8,128)(2,1)}, u32[]{:S(2)}, u32[]{:S(2)}) collective-permute-start(bf16[256,1024]{1,0:T(8,128)(2,1)S(1)} %dynamic-slice_convert_fusion.2), channel_id=1, source_target_pairs={{0,1},{1,0},{2,3},{3,2},{4,5},{5,4},{6,7},{7,6},{8,9},{9,8},{10,11... | collective-permute-start | bytes 1572872 | tf_op jit(solution)/shard_map/ppermute | solution.py:509
  218.6 69.9 %all-to-all-start.2 = ((bf16[16,64,1408]{2,1,0:T(8,128)(2,1)}), bf16[16,64,1408]{2,1,0:T(8,128)(2,1)}, u32[]{:S(2)}, u32[]{:S(2)}) async-start(bf16[16,64,1408]{2,1,0:T(8,128)(2,1)} %param.25), calls=%async_computation.2 | async-start | bytes 5767168 | tf_op jit(solution)/shard_map/all_to_all | solution.py:533
  225.8 28.1 %collective-permute-start.10 = (bf16[1152,512]{1,0:T(8,128)(2,1)S(1)}, bf16[1152,512]{1,0:T(8,128)(2,1)S(1)}, u32[]{:S(2)}, u32[]{:S(2)}) collective-permute-start(bf16[1152,512]{1,0:T(8,128)(2,1)S(1)} %get-tuple-element.112.near_ref), channel_id=1, source_target_pairs={{0,1},{1,0},{2,3},{3,2},{4,5},{5,4},{6,7},{7,6},{8,9},{9,8},{10,11... | collective-permute-start | bytes 3538952 | tf_op jit(solution)/shard_map/ppermute | solution.py:509
  253.9 27.2 %collective-permute-start.11 = (bf16[1152,512]{1,0:T(8,128)(2,1)S(1)}, bf16[1152,512]{1,0:T(8,128)(2,1)S(1)}, u32[]{:S(2)}, u32[]{:S(2)}) collective-permute-start(bf16[1152,512]{1,0:T(8,128)(2,1)S(1)} %get-tuple-element.61.near_ref), channel_id=1, source_target_pairs={{0,1},{1,0},{2,3},{3,2},{4,5},{5,4},{6,7},{7,6},{8,9},{9,8},{10,11... | collective-permute-start | bytes 3538952 | tf_op jit(solution)/shard_map/ppermute | solution.py:509
  288.5 70.4 %all-to-all-start.3 = ((bf16[16,64,1408]{2,1,0:T(8,128)(2,1)}), bf16[16,64,1408]{2,1,0:T(8,128)(2,1)}, u32[]{:S(2)}, u32[]{:S(2)}) async-start(bf16[16,64,1408]{2,1,0:T(8,128)(2,1)} %bitcast.91), calls=%async_computation.3 | async-start | bytes 5767168 | tf_op jit(solution)/shard_map/all_to_all | solution.py:533
  312.3 28.1 %collective-permute-start.12 = (bf16[1152,512]{1,0:T(8,128)(2,1)S(1)}, bf16[1152,512]{1,0:T(8,128)(2,1)S(1)}, u32[]{:S(2)}, u32[]{:S(2)}) collective-permute-start(bf16[1152,512]{1,0:T(8,128)(2,1)S(1)} %get-tuple-element.71), channel_id=1, source_target_pairs={{0,1},{1,0},{2,3},{3,2},{4,5},{5,4},{6,7},{7,6},{8,9},{9,8},{10,11... | collective-permute-start | bytes 3538952 | tf_op jit(solution)/shard_map/ppermute | solution.py:509
  340.3 36.2 %collective-permute-start.13 = (bf16[1152,512]{1,0:T(8,128)(2,1)}, bf16[1152,512]{1,0:T(8,128)(2,1)S(1)}, u32[]{:S(2)}, u32[]{:S(2)}) collective-permute-start(bf16[1152,512]{1,0:T(8,128)(2,1)} %dynamic-slice_convert_fusion), channel_id=1, source_target_pairs={{0,1},{1,0},{2,3},{3,2},{4,5},{5,4},{6,7},{7,6},{8,9},{9,8},{10,11... | collective-permute-start | bytes 3538952 | tf_op jit(solution)/shard_map/ppermute | solution.py:509
  358.9 33.0 %all-to-all-start.4 = ((bf16[16,72,512]{2,1,0:T(8,128)(2,1)}), bf16[16,72,512]{2,1,0:T(8,128)(2,1)}, u32[]{:S(2)}, u32[]{:S(2)}) async-start(bf16[16,72,512]{2,1,0:T(8,128)(2,1)} %bitcast.20), calls=%async_computation.4 | async-start | bytes 2359296 | tf_op jit(solution)/shard_map/all_to_all | solution.py:533
  391.8 171.8 %all-to-all-start.5 = ((bf16[16,64,3392]{2,1,0:T(8,128)(2,1)}), bf16[16,64,3392]{2,1,0:T(8,128)(2,1)}, u32[]{:S(2)}, u32[]{:S(2)}) async-start(bf16[16,64,3392]{2,1,0:T(8,128)(2,1)} %pad_maximum_fusion), calls=%async_computation.5 | async-start | bytes 14155776 | tf_op jit(solution)/shard_map/all_to_all | solution.py:533
  408.3 13.4 %collective-permute-start.15 = (bf16[256,1024]{1,0:T(8,128)(2,1)S(1)}, bf16[256,1024]{1,0:T(8,128)(2,1)}, u32[]{:S(2)}, u32[]{:S(2)}) collective-permute-start(bf16[256,1024]{1,0:T(8,128)(2,1)S(1)} %get-tuple-element.105), channel_id=1, source_target_pairs={{0,1},{1,0},{2,3},{3,2},{4,5},{5,4},{6,7},{7,6},{8,9},{9,8},{10,11... | collective-permute-start | bytes 1572872 | tf_op jit(solution)/shard_map/ppermute | solution.py:509
  446.5 28.4 %collective-permute-start.16 = (bf16[8,64,2048]{2,1,0:T(8,128)(2,1)}, bf16[8,64,2048]{2,1,0:T(8,128)(2,1)}, u32[]{:S(2)}, u32[]{:S(2)}) collective-permute-start(bf16[8,64,2048]{2,1,0:T(8,128)(2,1)} %dynamic-slice_bitcast_fusion), channel_id=1, source_target_pairs={{0,2},{2,0},{4,6},{6,4},{8,10},{10,8},{12,14},{14,12},{16,18},{18,... | collective-permute-start | bytes 6291464 | tf_op jit(solution)/shard_map/ppermute | solution.py:512
  457.7 14.3 %collective-permute-start.19 = (bf16[256,1024]{1,0:T(8,128)(2,1)S(1)}, bf16[256,1024]{1,0:T(8,128)(2,1)S(1)}, u32[]{:S(2)}, u32[]{:S(2)}) collective-permute-start(bf16[256,1024]{1,0:T(8,128)(2,1)S(1)} %dynamic-slice_convert_fusion.1), channel_id=1, source_target_pairs={{0,1},{1,0},{2,3},{3,2},{4,5},{5,4},{6,7},{7,6},{8,9},{9,8},{10,11... | collective-permute-start | bytes 1572872 | tf_op jit(solution)/shard_map/ppermute | solution.py:509
  479.7 53.0 %collective-permute-start.20 = (bf16[264,2048]{1,0:T(8,128)(2,1)}, bf16[264,2048]{1,0:T(8,128)(2,1)}, u32[]{:S(2)}, u32[]{:S(2)}) collective-permute-start(bf16[264,2048]{1,0:T(8,128)(2,1)} %pad_maximum_fusion.6), channel_id=1, source_target_pairs={{0,4},{2,6},{4,0},{6,2},{8,12},{10,14},{12,8},{14,10},{16,20},{18,... | collective-permute-start | bytes 3244040 | tf_op jit(solution)/shard_map/ppermute | solution.py:512
  536.8 41.7 %collective-permute-start.22 = (bf16[64,2176]{1,0:T(8,128)(2,1)S(1)}, bf16[64,2176]{1,0:T(8,128)(2,1)}, u32[]{:S(2)}, u32[]{:S(2)}) collective-permute-start(bf16[64,2176]{1,0:T(8,128)(2,1)S(1)} %get-tuple-element.126), channel_id=1, source_target_pairs={{0,8},{2,10},{4,12},{6,14},{8,0},{10,2},{12,4},{14,6},{16,24},{18,... | collective-permute-start | bytes 835592 | tf_op jit(solution)/shard_map/ppermute | solution.py:512
  536.8 41.6 %collective-permute-start.23 = (bf16[64,2176]{1,0:T(8,128)(2,1)S(1)}, bf16[64,2176]{1,0:T(8,128)(2,1)}, u32[]{:S(2)}, u32[]{:S(2)}) collective-permute-start(bf16[64,2176]{1,0:T(8,128)(2,1)S(1)} %get-tuple-element.125), channel_id=1, source_target_pairs={{0,16},{2,18},{4,20},{6,22},{8,24},{10,26},{12,28},{14,30},{16,0},... | collective-permute-start | bytes 835592 | tf_op jit(solution)/shard_map/ppermute | solution.py:512
  536.9 41.5 %collective-permute-start.24 = (bf16[64,2176]{1,0:T(8,128)(2,1)S(1)}, bf16[64,2176]{1,0:T(8,128)(2,1)}, u32[]{:S(2)}, u32[]{:S(2)}) collective-permute-start(bf16[64,2176]{1,0:T(8,128)(2,1)S(1)} %get-tuple-element.124), channel_id=1, source_target_pairs={{0,24},{2,26},{4,28},{6,30},{8,16},{10,18},{12,20},{14,22},{16,8},... | collective-permute-start | bytes 835592 | tf_op jit(solution)/shard_map/ppermute | solution.py:512
  (52 other events, 583.3 us)
